TPU v7x, 128 devices: a whole 4x4x4 slice. The times are simulated.
128 devices in a mesh: tm: 32 (over y, x, core), head: 4 (over z).
Axes of the slice: x: 4, y: 4, z: 4, core: 2. Of those that a mesh axis runs over, the one named last changes fastest.
Arguments:
- queries: bfloat16 [16384, 1024], P('tm', 'head'), may hold values from -5.5 to 5.5
- key_states: bfloat16 [16384, 1024], P('tm', 'head'), may hold values from -5.5 to 5.5
- value_states: bfloat16 [16384, 1024], P('tm', 'head'), may hold values from -6 to 6
- out_weight: bfloat16 [1024, 1024], P('head'), may hold values from -6 to 6
- upstream: bfloat16 [16384, 1024], P('tm'), may hold values from -6 to 6
- windows: int32 [16], P('head'), may hold values from 64 to 256, as said below
- offsets: int32 [16], P('head'), may hold values from 0 to 31
Outputs:
- mixed: bfloat16 [16384, 1024], P('tm')
- grad_queries: bfloat16 [16384, 1024], P('tm', 'head')
- grad_keys: bfloat16 [16384, 1024], P('tm', 'head')
- grad_values: bfloat16 [16384, 1024], P('tm', 'head')
Inputs may be any that keep to these rules, and one draw needn't show every extreme that they name: `windows`: each head's window reaches at most 256 positions to each side, and some head's window is exactly 256.
All inputs are finite; a program needn't handle non-finite values.
Results may differ from a plain program's by a relative error of at most 0.017.
Values may be sent and summed in bfloat16 or wider, within the bound.
No kernel may reach another device: no remote copies, remote signals or barrier semaphores. Data moves between devices by JAX's collectives and lax.ppermute only.
A program may use at most 128 MiB of HBM per device.

v0:
```python
import jax
import jax.numpy as jnp
from jax import lax
from jax.experimental import pallas as pl
from jax.experimental.pallas import tpu as pltpu
from jax.sharding import PartitionSpec as P


F32 = jnp.float32
BF16 = jnp.bfloat16
NEG = -1e30
NT = (((1,), (1,)), ((), ()))
SMEM = pl.BlockSpec(memory_space=pltpu.SMEM)


def sds(shape, dtype):
    return jax.ShapeDtypeStruct(shape, dtype)


def dot(a, b):
    return jnp.dot(a, b, preferred_element_type=F32)


def dot_nt(a, b):
    return lax.dot_general(a, b, NT, preferred_element_type=F32)


def call(body, ins, outs, scratch=(), flops=0, nbytes=0, specs=None, out_specs=None, vmem=24):
    full = lambda x: pl.BlockSpec(x.shape, (lambda *_: (0,) * len(x.shape)))
    specs = specs or [None] * len(ins)
    in_specs = [full(x) if s is None else s for x, s in zip(ins, specs)]
    out_specs = out_specs or [full(o) for o in outs]
    return pl.pallas_call(
        body,
        out_shape=outs,
        grid=(1,),
        in_specs=in_specs,
        out_specs=out_specs,
        scratch_shapes=list(scratch),
        cost_estimate=pl.CostEstimate(flops=int(flops), bytes_accessed=int(nbytes), transcendentals=0),
        compiler_params=pltpu.CompilerParams(vmem_limit_bytes=vmem << 20),
    )(*ins)


def iota(shape, axis):
    return lax.broadcasted_iota(jnp.int32, shape, axis)


def place(n, offset):
    u = jnp.where(n >= 128, 2 * (n - 128) + 1, 4 * (n - 64) + 2)
    u = jnp.where(n >= 64, u, 8 * (n - 32) + 4)
    u = jnp.where(n >= 32, u, 16 * (n - 16) + 8)
    u = jnp.where(n >= 16, u, 32 * (n - 8) + 16)
    u = jnp.where(n >= 8, u, 32 * n)
    return (u + offset) & 255


def depth(n):
    d = jnp.where(n < 64, 2, 1)
    d = jnp.where(n < 32, 3, d)
    d = jnp.where(n < 16, 4, d)
    return jnp.where(n < 8, 5, d)


def to_depth(offset):
    s = (256, 256)
    return (iota(s, 1) == place(iota(s, 0), offset)).astype(F32).astype(BF16)


def from_depth(offset):
    s = (256, 256)
    return (iota(s, 0) == place(iota(s, 1), offset)).astype(F32).astype(BF16)


def lane_first(rows, width=128):
    return (iota((rows, width), 1) % 128) < 64


def zero_pad(x, which):
    z = jnp.zeros_like(x)
    return jnp.concatenate([x, z] if which == 0 else [z, x], axis=0)


def transposed(x):
    return x.astype(F32).T.astype(BF16)


def prep_kv(off, par, k, v, kvp, c1, n1, x1):
    keep = lane_first(256, 256)
    for pair in range(2):
        lanes = slice(pair * 128, pair * 128 + 128)
        first, second = to_depth(off[2 * pair]), to_depth(off[2 * pair + 1])
        for b in range(2):
            rows = slice(b * 256, b * 256 + 256)
            kv = jnp.concatenate([k[rows, lanes], v[rows, lanes]], axis=1)
            kvp[rows, pair * 256 : pair * 256 + 256] = jnp.where(
                keep, dot(first, kv), dot(second, kv)
            ).astype(BF16)
    x1[0:64] = kvp[0:64]
    x1[64:128] = kvp[256:320]

    @pl.when(par[0] == 0)
    def _():
        c1[0:256] = kvp[256:512]
        c1[256:384] = kvp[0:128]
        n1[...] = kvp[0:256]

    @pl.when(par[0] == 1)
    def _():
        c1[0:256] = kvp[0:256]
        c1[256:384] = kvp[256:384]
        n1[...] = kvp[256:512]


def prep_qg(off, q, up, w, qt, gt):
    g = dot_nt(w[...], up[...]).astype(BF16)
    qs = (q[...].astype(F32) * 0.125).T.astype(BF16)
    for h in range(4):
        perm = from_depth(off[h])
        hs = slice(64 * h, 64 * h + 64)
        for b in range(2):
            bs = slice(256 * b, 256 * b + 256)
            x = jnp.concatenate([qs[hs, bs], g[hs, bs]], axis=0)
            r = dot(x, perm).astype(BF16)
            qt[hs, bs] = r[0:64]
            gt[hs, bs] = r[64:128]


def pack_rows(pieces):
    return jnp.concatenate([p.astype(F32) for p in pieces], axis=0).astype(BF16)


def asm_x2(kvp, x1, out):
    out[...] = pack_rows([kvp[0:32], kvp[256:288], x1[0:32], x1[64:96]])


def asm_y1(kvp, x1, x2, out):
    out[...] = pack_rows(
        [kvp[0:16], kvp[256:272], x1[0:16], x1[64:80]] + [x2[32 * j : 32 * j + 16] for j in range(4)]
    )


def asm_y2(kvp, x1, x2, y1, out):
    heads = [kvp[0:16], kvp[256:272], x1[0:16], x1[64:80]]
    heads += [x2[32 * j : 32 * j + 16] for j in range(4)]
    heads += [y1[16 * j : 16 * j + 16] for j in range(8)]
    out[...] = jnp.concatenate([h.astype(F32)[0:8] for h in heads], axis=0).astype(BF16)


def fill_ext(par, kv, c1, n1, kx, vx):
    kx[256:768] = kv[:, 0:128]
    vx[256:768] = kv[:, 128:256]

    @pl.when(par[0] == 0)
    def _():
        kx[0:256] = n1[:, 0:128]
        vx[0:256] = n1[:, 128:256]
        kx[768:1024] = c1[0:256, 0:128]
        vx[768:1024] = c1[0:256, 128:256]

    @pl.when(par[0] == 1)
    def _():
        kx[0:256] = c1[0:256, 0:128]
        vx[0:256] = c1[0:256, 128:256]
        kx[768:1024] = n1[:, 0:128]
        vx[768:1024] = n1[:, 128:256]


def near_chunks(kx, c1, lo):
    return [kx[256:384], kx[512:640], c1[0:128, lo : lo + 128], c1[256:384, lo : lo + 128]]


def near_count():
    s = (128, 128)
    return jnp.minimum(depth(iota(s, 0)), depth(iota(s, 1))).astype(F32)


def fwd_near(pair, off, win, par, tm, qt, kv, c1, n1, pw, p1, acc_out, stat, kx, vx, vt, v1t, k1, dist, sw, s1):
    fill_ext(par, kv, c1, n1, kx, vx)
    vt[...] = transposed(vx[...])
    k1[...] = jnp.concatenate(near_chunks(kx, c1, 0), axis=0)
    v1t[...] = transposed(jnp.concatenate(near_chunks(vx, c1, 128), axis=0))
    count = near_count()
    for a in range(2):
        h = 2 * pair + a
        s = (256, 256)
        dist[...] = place(iota(s, 0), off[h]) - place(iota(s, 1), off[h])
        reach = win[h]
        lo = jnp.where(tm[0] == 0, 1000, 256 - reach)
        hi = jnp.where(tm[0] == 31, -1000, reach - 256)
        for b in range(2):
            qz = zero_pad(qt[64 * a : 64 * a + 64, 256 * b : 256 * b + 256], a)
            top = None
            for c in range(3):
                sc = dot(kx[256 * (b + c) : 256 * (b + c) + 256], qz)
                d = dist[...]
                if c == 0:
                    ok = d >= (lo if b == 0 else 256 - reach)
                elif c == 1:
                    ok = jnp.abs(d) <= reach
                else:
                    ok = d <= (hi if b == 1 else reach - 256)
                sc = jnp.where(ok, sc, NEG)
                sw[256 * c : 256 * c + 256] = sc
                part = jnp.max(sc, axis=0, keepdims=True)
                top = part if top is None else jnp.maximum(top, part)
            sc = dot(k1[...], qz[:, 0:128])
            s1[...] = sc
            near_top = jnp.maximum(top[:, 0:128], jnp.max(sc, axis=0, keepdims=True))
            top = jnp.concatenate([near_top, top[:, 128:256]], axis=1)
            total = jnp.zeros((1, 256), F32)
            for c in range(3):
                e = jnp.exp(sw[256 * c : 256 * c + 256] - top)
                total += jnp.sum(e, axis=0, keepdims=True)
                pw[a, b, 256 * c : 256 * c + 256, :] = e.astype(BF16)
            vh = slice(64 * a, 64 * a + 64)
            acc = dot(vt[vh, 256 * b : 256 * b + 768], pw[a, b])
            near_sum = jnp.zeros((1, 128), F32)
            bs = slice(128 * b, 128 * b + 128)
            for c in range(4):
                e = count * jnp.exp(s1[128 * c : 128 * c + 128] - near_top)
                near_sum += jnp.sum(e, axis=0, keepdims=True)
                p1[a, 128 * c : 128 * c + 128, bs] = e.astype(BF16)
            near_acc = dot(v1t[vh, :], p1[a, :, bs])
            acc_out[vh, 256 * b : 256 * b + 128] = acc[:, 0:128] + near_acc
            acc_out[vh, 256 * b + 128 : 256 * b + 256] = acc[:, 128:256]
            stat[a : a + 1, 256 * b : 256 * b + 256] = top
            stat[2 + a : 3 + a, 256 * b : 256 * b + 128] = total[:, 0:128] + near_sum
            stat[2 + a : 3 + a, 256 * b + 128 : 256 * b + 256] = total[:, 128:256]


def far_count():
    s = (1024, 128)
    j, i = iota(s, 0), iota(s, 1)
    level = 2 + j // 256
    chunk = jnp.where(level == 2, 64, jnp.where(level == 3, 32, jnp.where(level == 4, 16, 8)))
    both = jnp.minimum(depth(j & (chunk - 1)), depth(i & 63))
    return jnp.maximum(both - level + 1, 0).astype(F32)


def far_lanes(x):
    return jnp.concatenate([x[:, 0:64], x[:, 256:320]], axis=1)


def wide(x, b, filler):
    rows = x.shape[0]
    return jnp.concatenate([x[:, 64 * b : 64 * b + 64], jnp.full((rows, 192), filler, F32)], axis=1)


def fwd_far(off, qt, gt, acc0, acc1, st0, st1, *rest):
    bufs, (pf, attn, stat2, kf, vft, mult, at) = rest[:8], rest[8:]
    mult[...] = far_count()
    for pair in range(2):
        acc_in, stat = (acc0, st0) if pair == 0 else (acc1, st1)
        lo, hi = slice(256 * pair, 256 * pair + 128), slice(256 * pair + 128, 256 * pair + 256)
        for j, buf in enumerate(bufs):
            kf[128 * j : 128 * j + 128] = buf[:, lo]
        vft[...] = transposed(jnp.concatenate([buf[:, hi] for buf in bufs], axis=0))
        for a in range(2):
            vh = slice(64 * a, 64 * a + 64)
            h = 2 * pair + a
            hs = slice(64 * h, 64 * h + 64)
            qz = zero_pad(far_lanes(qt[hs, :]), a)
            cnt = mult[...]
            sc = jnp.where(cnt > 0, dot(kf[...], qz), NEG)
            ftop = jnp.max(sc, axis=0, keepdims=True)
            e = cnt * jnp.exp(sc - ftop)
            fsum = jnp.sum(e, axis=0, keepdims=True)
            pf[h] = e.astype(BF16)
            facc = dot(vft[vh, :], pf[h])
            for b in range(2):
                bs = slice(256 * b, 256 * b + 256)
                ntop, nsum = stat[a : a + 1, bs], stat[2 + a : 3 + a, bs]
                ftopw = wide(ftop, b, NEG)
                top = jnp.maximum(ntop, ftopw)
                wn, wf = jnp.exp(ntop - top), jnp.exp(ftopw - top)
                norm = nsum * wn + wide(fsum, b, 0.0) * wf
                acc = acc_in[vh, bs] * wn + wide(facc, b, 0.0) * wf
                o = (acc / norm).astype(BF16)
                at[vh, bs] = o
                stat2[h : h + 1, bs] = wn / norm
                stat2[4 + h : 5 + h, bs] = wf / norm
                stat2[8 + h : 9 + h, bs] = jnp.sum(
                    gt[hs, bs].astype(F32) * o.astype(F32), axis=0, keepdims=True
                )
        unperm_pair(off, pair, at, attn, slice(128 * pair, 128 * pair + 128))


def unperm_pair(off, pair, src, out, lanes):
    keep = lane_first(256)
    first, second = from_depth(off[2 * pair]), from_depth(off[2 * pair + 1])
    for b in range(2):
        x = src[:, 256 * b : 256 * b + 256]
        out[256 * b : 256 * b + 256, lanes] = jnp.where(keep, dot_nt(first, x), dot_nt(second, x)).astype(BF16)


def bwd_far(qt, gt, stat2, pf, *rest):
    bufs, (ret, own_far, dq, kx, vx) = rest[:8], rest[8:]
    for pair in range(2):
        lo, hi = slice(256 * pair, 256 * pair + 128), slice(256 * pair + 128, 256 * pair + 256)
        for j, buf in enumerate(bufs):
            kx[128 * j : 128 * j + 128] = buf[:, lo]
            vx[128 * j : 128 * j + 128] = buf[:, hi]
        kt = transposed(kx[...])
        grads, scaled_q, scaled_g = [], [], []
        for a in range(2):
            h = 2 * pair + a
            hs, vh = slice(64 * h, 64 * h + 64), slice(64 * a, 64 * a + 64)
            cf = far_lanes(stat2[4 + h : 5 + h, :])
            delta = far_lanes(stat2[8 + h : 9 + h, :])
            q, g = far_lanes(qt[hs, :]), far_lanes(gt[hs, :])
            dp = dot(vx[...], zero_pad(g, a))
            ds = (pf[h].astype(F32) * (dp - delta)).astype(BF16)
            grads.append(ds)
            scaled_q.append(zero_pad((q.astype(F32) * cf).astype(BF16), a))
            scaled_g.append(zero_pad((g.astype(F32) * cf).astype(BF16), a))
            dq[hs, :] = dot(kt[vh, :], ds) * cf
        dk = dot_nt(jnp.concatenate(grads, axis=1), jnp.concatenate(scaled_q, axis=1))
        dv = dot_nt(jnp.concatenate([pf[2 * pair], pf[2 * pair + 1]], axis=1), jnp.concatenate(scaled_g, axis=1))
        for j in range(4):
            mine, theirs = slice(256 * j, 256 * j + 128), slice(256 * j + 128, 256 * j + 256)
            rows = slice(128 * j, 128 * j + 128)
            own_far[rows, lo] = dk[mine]
            own_far[rows, hi] = dv[mine]
            ret[rows, lo] = dk[theirs].astype(BF16)
            ret[rows, hi] = dv[theirs].astype(BF16)


def bwd_near_keys(qt, gt, stat2, kv, c1, p10, p11, ret, own_near, dq):
    for pair in range(2):
        p1 = p10 if pair == 0 else p11
        lo, hi = slice(256 * pair, 256 * pair + 128), slice(256 * pair + 128, 256 * pair + 256)
        k1 = jnp.concatenate([kv[0:128, lo], kv[256:384, lo], c1[0:128, lo], c1[256:384, lo]], axis=0)
        v1 = jnp.concatenate([kv[0:128, hi], kv[256:384, hi], c1[0:128, hi], c1[256:384, hi]], axis=0)
        k1t = transposed(k1)
        grads, scaled_q, scaled_g, probs = [], [], [], []
        for a in range(2):
            h = 2 * pair + a
            hs, vh = slice(64 * h, 64 * h + 64), slice(64 * a, 64 * a + 64)
            for b in range(2):
                bs = slice(256 * b, 256 * b + 128)
                cn, delta = stat2[h : h + 1, bs], stat2[8 + h : 9 + h, bs]
                g = gt[hs, bs]
                p = p1[a, :, 128 * b : 128 * b + 128]
                ds = (p.astype(F32) * (dot(v1, zero_pad(g, a)) - delta)).astype(BF16)
                grads.append(ds)
                probs.append(p)
                scaled_q.append(zero_pad((qt[hs, bs].astype(F32) * cn).astype(BF16), a))
                scaled_g.append(zero_pad((g.astype(F32) * cn).astype(BF16), a))
                dq[hs, 128 * b : 128 * b + 128] = dot(k1t[vh, :], ds) * cn
        dk = dot_nt(jnp.concatenate(grads, axis=1), jnp.concatenate(scaled_q, axis=1))
        dv = dot_nt(jnp.concatenate(probs, axis=1), jnp.concatenate(scaled_g, axis=1))
        own_near[:, lo] = dk[0:256]
        own_near[:, hi] = dv[0:256]
        ret[:, lo] = dk[256:512].astype(BF16)
        ret[:, hi] = dv[256:512].astype(BF16)


def bwd_near(pair, off, par, qt, gt, stat2, kv, c1, n1, pw, dqf, dqn, own_near, *rest):
    if pair == 0:
        own, halo_c, halo_n, gq, kx, vx, kt, dk, dv, dqt = rest
        lanes = slice(0, 256)
    else:
        hc0, hn0, gq0, own, halo_c, halo_n, gq, kx, vx, kt, dk, dv, dqt = rest
        halo_c[:, 0:256] = hc0[...]
        halo_n[:, 0:256] = hn0[...]
        gq[:, 0:128] = gq0[...]
        lanes = slice(256, 512)
    fill_ext(par, kv, c1, n1, kx, vx)
    kt[...] = transposed(kx[...])
    dk[...] = jnp.zeros((1024, 128), F32)
    dv[...] = jnp.zeros((1024, 128), F32)
    for (dst, part) in ((dk, slice(0, 128)), (dv, slice(128, 256))):
        dst[256:384] = own_near[0:128, part]
        dst[512:640] = own_near[128:256, part]
    for b in range(2):
        bs = slice(256 * b, 256 * b + 256)
        ext = slice(256 * b, 256 * b + 768)
        for a in range(2):
            h = 2 * pair + a
            vh = slice(64 * a, 64 * a + 64)
            cn, delta = stat2[h : h + 1, bs], stat2[8 + h : 9 + h, bs]
            g = gt[vh, bs]
            dp = dot(vx[ext], zero_pad(g, a))
            p = pw[a, b]
            ds = (p.astype(F32) * (dp - delta)).astype(BF16)
            qs = zero_pad((qt[vh, bs].astype(F32) * cn).astype(BF16), a)
            gs = zero_pad((g.astype(F32) * cn).astype(BF16), a)
            dk[ext] += dot_nt(ds, qs)
            dv[ext] += dot_nt(p, gs)
            near = jnp.concatenate([dqn[vh, 128 * b : 128 * b + 128], jnp.zeros((64, 128), F32)], axis=1)
            total = dot(kt[vh, ext], ds) * cn + near + wide(dqf[vh, :], b, 0.0)
            dqt[vh, bs] = (total * 0.125).astype(BF16)
    own[:, 0:128] = dk[256:768]
    own[:, 128:256] = dv[256:768]
    low = jnp.concatenate([dk[0:256], dv[0:256]], axis=1).astype(BF16)
    high = jnp.concatenate([dk[768:1024], dv[768:1024]], axis=1).astype(BF16)

    @pl.when(par[0] == 0)
    def _():
        halo_n[:, lanes] = low
        halo_c[:, lanes] = high

    @pl.when(par[0] == 1)
    def _():
        halo_c[:, lanes] = low
        halo_n[:, lanes] = high

    unperm_pair(off, pair, dqt, gq, slice(128 * pair, 128 * pair + 128))


def ret_y2(own_far, ret, rest, send):
    total = own_far[...] + ret[...].astype(F32)
    rest[...] = total[0:384]
    send[...] = total[384:512].astype(BF16)


def ret_y1(rest, got, left, send):
    y2 = got[...].astype(F32)
    left[...] = rest[0:256]
    for j in range(2):
        left[64 * j : 64 * j + 8] += y2[16 + 8 * j : 24 + 8 * j]
    for j in range(4):
        left[128 + 32 * j : 136 + 32 * j] += y2[32 + 8 * j : 40 + 8 * j]
    zero = jnp.zeros((8, 512), F32)
    extra = []
    for j in range(8):
        extra += [y2[64 + 8 * j : 72 + 8 * j], zero]
    send[...] = (rest[256:384] + jnp.concatenate(extra, axis=0)).astype(BF16)


def ret_x2(rest, got, left, send):
    y1 = got[...].astype(F32)
    left[...] = rest[0:128]
    for j in range(2):
        left[64 * j : 64 * j + 16] += y1[32 + 16 * j : 48 + 16 * j]
    zero = jnp.zeros((16, 512), F32)
    extra = []
    for j in range(4):
        extra += [y1[64 + 16 * j : 80 + 16 * j], zero]
    send[...] = (rest[128:256] + jnp.concatenate(extra, axis=0)).astype(BF16)


def ret_x1(rest, got, send):
    x2 = got[...].astype(F32)
    zero = jnp.zeros((32, 512), F32)
    extra = [x2[64:96], zero, x2[96:128], zero]
    send[...] = (rest[...] + jnp.concatenate(extra, axis=0)).astype(BF16)


def finish(off, par, own0, own1, ret, hc, hn, y2, y1, x2, x1, gk, gv, acc):
    acc[:, 0:256] = own0[...]
    acc[:, 256:512] = own1[...]
    for b in range(2):
        at = 256 * b
        acc[at : at + 64] += x1[64 * b : 64 * b + 64].astype(F32)
        acc[at : at + 32] += x2[32 * b : 32 * b + 32].astype(F32)
        acc[at : at + 16] += y1[16 * b : 16 * b + 16].astype(F32)
        acc[at : at + 8] += y2[0:16].astype(F32)[8 * b : 8 * b + 8]

    @pl.when(par[0] == 0)
    def _():
        acc[256:512] += hc[...].astype(F32)
        acc[0:256] += hn[...].astype(F32)
        acc[256:384] += ret[0:128].astype(F32)
        acc[0:128] += ret[128:256].astype(F32)

    @pl.when(par[0] == 1)
    def _():
        acc[0:256] += hc[...].astype(F32)
        acc[256:512] += hn[...].astype(F32)
        acc[0:128] += ret[0:128].astype(F32)
        acc[256:384] += ret[128:256].astype(F32)

    keep = lane_first(256, 256)
    for pair in range(2):
        first, second = from_depth(off[2 * pair]), from_depth(off[2 * pair + 1])
        lanes = slice(128 * pair, 128 * pair + 128)
        for b in range(2):
            rows = slice(256 * b, 256 * b + 256)
            x = acc[rows, 256 * pair : 256 * pair + 256].astype(BF16)
            r = jnp.where(keep, dot(first, x), dot(second, x)).astype(BF16)
            gk[rows, lanes] = r[:, 0:128]
            gv[rows, lanes] = r[:, 128:256]


def project(a0, a1, a2, a3, w0, w1, w2, w3, out):
    a = jnp.concatenate([a0[...], a1[...], a2[...], a3[...]], axis=1)
    w = jnp.concatenate([w0[...], w1[...], w2[...], w3[...]], axis=0)
    out[...] = dot(a, w).astype(BF16)


def swap(x, axis, mask):
    return lax.ppermute(x, axis, [(i, i ^ mask) for i in range(lax.axis_size(axis))])


def side(x):
    pairs = [(i, (i + 1) % 32 if i % 2 else (i - 1) % 32) for i in range(32)]
    return lax.ppermute(x, "tm", pairs)


def bind(f, *args):
    def body(*refs):
        f(*args, *refs)

    return body


def layer(q, k, v, w, up, win, off):
    tm = lax.axis_index("tm").astype(jnp.int32).reshape(1)
    par = tm % 2
    VM = pltpu.VMEM
    kvp, c1s, n1s, x1s = call(
        prep_kv, (off, par, k, v),
        [sds((512, 512), BF16), sds((384, 512), BF16), sds((256, 512), BF16), sds((128, 512), BF16)],
        specs=[SMEM, SMEM, None, None], flops=3e8, nbytes=3e6,
    )
    x1 = swap(x1s, "tm", 2)
    c1 = swap(c1s, "tm", 1)
    n1 = side(n1s)
    wa, wb = swap(w, "head", 1), swap(w, "head", 3)
    wc = swap(wa, "head", 3)
    qt, gt = call(
        prep_qg, (off, q, up, w), [sds((256, 512), BF16), sds((256, 512), BF16)],
        specs=[SMEM, None, None, None], flops=6e8, nbytes=3e6,
    )
    x2 = swap(call(asm_x2, (kvp, x1), [sds((128, 512), BF16)])[0], "tm", 6)

    pair_lanes = lambda rows, pair: pl.BlockSpec((rows, 256), lambda *_: (0, pair))
    pair_rows = lambda cols, pair: pl.BlockSpec((128, cols), lambda *_: (pair, 0))
    near = []
    for pair in range(2):
        near.append(
            call(
                bind(fwd_near, pair), (off, win, par, tm, qt, kvp, c1, n1),
                [sds((2, 2, 768, 256), BF16), sds((2, 512, 256), BF16), sds((128, 512), F32), sds((8, 512), F32)],
                specs=[SMEM] * 4 + [pair_rows(512, pair)] + [pair_lanes(r, pair) for r in (512, 384, 256)],
                scratch=[
                    VM((1024, 128), BF16), VM((1024, 128), BF16), VM((128, 1024), BF16), VM((128, 512), BF16),
                    VM((512, 128), BF16), VM((256, 256), jnp.int32), VM((768, 256), F32), VM((512, 128), F32),
                ],
                flops=3e9, nbytes=4e6,
            )
        )
    y1 = swap(call(asm_y1, (kvp, x1, x2), [sds((128, 512), BF16)])[0], "tm", 8)
    y2 = swap(call(asm_y2, (kvp, x1, x2, y1), [sds((128, 512), BF16)])[0], "tm", 24)
    bufs = []
    for mine in (x1, x2, y1, y2):
        bufs += [mine, swap(mine, "tm", 1)]

    pf, attn, stat2 = call(
        fwd_far, (off, qt, gt, near[0][2], near[1][2], near[0][3], near[1][3], *bufs),
        [sds((4, 1024, 128), BF16), sds((512, 256), BF16), sds((16, 512), F32)],
        specs=[SMEM] + [None] * 14,
        scratch=[VM((1024, 128), BF16), VM((128, 1024), BF16), VM((1024, 128), F32), VM((128, 512), BF16)],
        flops=3e9, nbytes=4e6,
    )
    a1, a2 = swap(attn, "head", 1), swap(attn, "head", 3)
    a3 = swap(a1, "head", 3)

    ret_s, own_far, dqf = call(
        bwd_far, (qt, gt, stat2, pf, *bufs),
        [sds((512, 512), BF16), sds((512, 512), F32), sds((256, 128), F32)],
        scratch=[VM((1024, 128), BF16), VM((1024, 128), BF16)], flops=4e9, nbytes=5e6,
    )
    ret = swap(ret_s, "tm", 1)
    near_s, own_near, dqn = call(
        bwd_near_keys, (qt, gt, stat2, kvp, c1, near[0][1], near[1][1]),
        [sds((256, 512), BF16), sds((256, 512), F32), sds((256, 256), F32)],
        flops=4e9, nbytes=5e6,
    )
    near_r = swap(near_s, "tm", 1)
    back = []
    for pair in range(2):
        more = [] if pair == 0 else [back[0][1], back[0][2], back[0][3]]
        wide_out = 256 if pair == 0 else 512
        back.append(
            call(
                bind(bwd_near, pair),
                (off, par, qt, gt, stat2, kvp, c1, n1, near[pair][0], dqf, dqn, own_near, *more),
                [sds((512, 256), F32), sds((256, wide_out), BF16), sds((256, wide_out), BF16), sds((512, wide_out // 2), BF16)],
                specs=[SMEM] * 2 + [pair_rows(512, pair), pair_rows(512, pair), None]
                + [pair_lanes(r, pair) for r in (512, 384, 256)]
                + [None, pair_rows(128, pair), pair_rows(256, pair), pair_lanes(256, pair)] + [None] * len(more),
                scratch=[
                    VM((1024, 128), BF16), VM((1024, 128), BF16), VM((128, 1024), BF16),
                    VM((1024, 128), F32), VM((1024, 128), F32), VM((128, 512), BF16),
                ],
                flops=4e9, nbytes=4e6,
            )
        )
    rest, y2s = call(ret_y2, (own_far, ret), [sds((384, 512), F32), sds((128, 512), BF16)])
    y2r = swap(y2s, "tm", 24)
    rest, y1s = call(ret_y1, (rest, y2r), [sds((256, 512), F32), sds((128, 512), BF16)])
    y1r = swap(y1s, "tm", 8)
    rest, x2s = call(ret_x2, (rest, y1r), [sds((128, 512), F32), sds((128, 512), BF16)])
    x2r = swap(x2s, "tm", 6)
    (x1s,) = call(ret_x1, (rest, x2r), [sds((128, 512), BF16)])
    x1r = swap(x1s, "tm", 2)
    hc = swap(back[1][1], "tm", 1)
    hn = side(back[1][2])
    gk, gv = call(
        finish, (off, par, back[0][0], back[1][0], near_r, hc, hn, y2r, y1r, x2r, x1r),
        [sds((512, 256), BF16), sds((512, 256), BF16)],
        specs=[SMEM] * 2 + [None] * 9, scratch=[VM((512, 512), F32)], flops=3e8, nbytes=3e6,
    )
    (mixed,) = call(project, (attn, a1, a2, a3, w, wa, wb, wc), [sds((512, 1024), BF16)], flops=1e9, nbytes=4e6)
    return mixed, back[1][3], gk, gv


def solution(mesh):
    placed = (P("tm", "head"),) * 3 + (P("head", None), P("tm", None), P("head"), P("head"))
    return jax.shard_map(
        layer,
        mesh=mesh,
        in_specs=placed,
        out_specs=(P("tm", None), P("tm", "head"), P("tm", "head"), P("tm", "head")),
        check_vma=False,
    )
```

profile of v0, /device:TPU:1, one launch (start us, length us, event | category | flops | bytes accessed | tf_op | source)
XLA Modules:
  0.0 83.4 jit_solution(836008917216722426)
XLA Ops:
  0.7 0.0 copy-start.1
  0.7 0.7 copy-done.1
  1.4 0.9 %copy-done.4 = bf16[512,256]{1,0:T(8,128)(2,1)S(1)} copy-done((bf16[512,256]{1,0:T(8,128)(2,1)S(1)}, bf16[512,256]{1,0:T(8,128)(2,1)}, u32[]{:S(2)}) %copy-start.4) | copy-done | bytes 262168
  2.3 0.9 %copy-done.5 = bf16[512,256]{1,0:T(8,128)(2,1)S(1)} copy-done((bf16[512,256]{1,0:T(8,128)(2,1)S(1)}, bf16[512,256]{1,0:T(8,128)(2,1)}, u32[]{:S(2)}) %copy-start.5) | copy-done | bytes 262168
  3.3 1.1 %shard_map.103 = (bf16[512,512]{1,0:T(8,128)(2,1)S(1)}, bf16[384,512]{1,0:T(8,128)(2,1)S(1)}, bf16[256,512]{1,0:T(8,128)(2,1)S(1)}, bf16[128,512]{1,0:T(8,128)(2,1)S(1)}) custom-call(s32[4]{0:T(128)S(1)} %copy-done.1, s32[1]{0:T(128)S(6)} %select_n.7.par.refs_2_.refs_1_, bf16[512,256]{1,0:T(8,128)(2,1)S(1)} %copy-done.4, bf16[512,256]{1,0:T(8,128)(2,1)S(1)} %copy-done.5), custom_call_target="tpu_custom_call" | custom-call | flops 300000000 | bytes 3000000 | tf_op jit(solution)/shard_map/pallas_call | solution.py:33
  4.4 2.1 %collective-permute-start.2 = (bf16[128,512]{1,0:T(8,128)(2,1)S(1)}, bf16[128,512]{1,0:T(8,128)(2,1)S(1)}, u32[]{:S(2)}, u32[]{:S(2)}) collective-permute-start(bf16[128,512]{1,0:T(8,128)(2,1)S(1)} %get-tuple-element.52), channel_id=1, source_target_pairs={{0,8},{4,12},{8,0},{12,4},{16,24},{20,28},{24,16},{28,20},{32,40},... | collective-permute-start | bytes 393224 | tf_op jit(solution)/shard_map/ppermute | solution.py:494
  6.5 0.9 %collective-permute-start = (bf16[384,512]{1,0:T(8,128)(2,1)S(1)}, bf16[384,512]{1,0:T(8,128)(2,1)S(1)}, u32[]{:S(2)}, u32[]{:S(2)}) collective-permute-start(bf16[384,512]{1,0:T(8,128)(2,1)S(1)} %get-tuple-element.46), channel_id=1, source_target_pairs={{0,4},{4,0},{8,12},{12,8},{16,20},{20,16},{24,28},{28,24},{32,36},... | collective-permute-start | bytes 1179656 | tf_op jit(solution)/shard_map/ppermute | solution.py:494
  7.4 1.8 %collective-permute-done.2.x1.rest_0_ = bf16[128,512]{1,0:T(8,128)(2,1)S(1)} collective-permute-done((bf16[128,512]{1,0:T(8,128)(2,1)S(1)}, bf16[128,512]{1,0:T(8,128)(2,1)S(1)}, u32[]{:S(2)}, u32[]{:S(2)}) %collective-permute-start.2) | collective-permute-done | bytes 131104 | tf_op jit(solution)/shard_map/ppermute | solution.py:494
  9.3 2.9 %collective-permute-start.4 = (bf16[128,512]{1,0:T(8,128)(2,1)S(1)}, bf16[128,512]{1,0:T(8,128)(2,1)S(1)}, u32[]{:S(2)}, u32[]{:S(2)}) collective-permute-start(bf16[128,512]{1,0:T(8,128)(2,1)S(1)} %shard_map.106), channel_id=1, source_target_pairs={{0,24},{4,28},{8,16},{12,20},{16,8},{20,12},{24,0},{28,4},{32,56},... | collective-permute-start | bytes 393224 | tf_op jit(solution)/shard_map/ppermute | solution.py:494
  12.2 1.6 %collective-permute-start.1 = (bf16[256,512]{1,0:T(8,128)(2,1)S(1)}, bf16[256,512]{1,0:T(8,128)(2,1)S(1)}, u32[]{:S(2)}, u32[]{:S(2)}) collective-permute-start(bf16[256,512]{1,0:T(8,128)(2,1)S(1)} %get-tuple-element.47), channel_id=1, source_target_pairs={{0,124},{4,8},{8,4},{12,16},{16,12},{20,24},{24,20},{28,32},{32,28... | collective-permute-start | bytes 786440 | tf_op jit(solution)/shard_map/ppermute | solution.py:499
  13.8 0.7 collective-permute-done.4.x2.rest_2_
  14.6 1.6 %collective-permute-start.6 = (bf16[128,512]{1,0:T(8,128)(2,1)S(1)}, bf16[128,512]{1,0:T(8,128)(2,1)S(1)}, u32[]{:S(2)}, u32[]{:S(2)}) collective-permute-start(bf16[128,512]{1,0:T(8,128)(2,1)S(1)} %shard_map.107), channel_id=1, source_target_pairs={{0,32},{4,36},{8,40},{12,44},{16,48},{20,52},{24,56},{28,60},{32,0... | collective-permute-start | bytes 393224 | tf_op jit(solution)/shard_map/ppermute | solution.py:494
  16.2 1.6 %collective-permute-start.13 = (bf16[256,1024]{1,0:T(8,128)(2,1)S(1)}, bf16[256,1024]{1,0:T(8,128)(2,1)S(1)}, u32[]{:S(2)}, u32[]{:S(2)}) collective-permute-start(bf16[256,1024]{1,0:T(8,128)(2,1)S(1)} %copy-done), channel_id=1, source_target_pairs={{0,1},{1,0},{2,3},{3,2},{4,5},{5,4},{6,7},{7,6},{8,9},{9,8},{10,11... | collective-permute-start | bytes 1572872 | tf_op jit(solution)/shard_map/ppermute | solution.py:494
  17.8 1.2 %shard_map.102 = (bf16[256,512]{1,0:T(8,128)(2,1)S(1)}, bf16[256,512]{1,0:T(8,128)(2,1)S(1)}) custom-call(s32[4]{0:T(128)S(1)} %copy-done.1, bf16[512,256]{1,0:T(8,128)(2,1)S(1)} %copy-done.6, bf16[512,1024]{1,0:T(8,128)(2,1)S(1)} %copy-done.3, bf16[256,1024]{1,0:T(8,128)(2,1)S(1)} %copy-done), custom_call_target="tpu_custom_call" | custom-call | flops 600000000 | bytes 3000000 | tf_op jit(solution)/shard_map/pallas_call | solution.py:33
  19.0 3.3 %collective-permute-start.3 = (bf16[128,512]{1,0:T(8,128)(2,1)S(1)}, bf16[128,512]{1,0:T(8,128)(2,1)S(1)}, u32[]{:S(2)}, u32[]{:S(2)}) collective-permute-start(bf16[128,512]{1,0:T(8,128)(2,1)S(1)} %collective-permute-done.2.x1.rest_0_), channel_id=1, source_target_pairs={{0,4},{4,0},{8,12},{12,8},{16,20},{20,16},{24,28},{28,24},{32,36},... | collective-permute-start | bytes 393224 | tf_op jit(solution)/shard_map/ppermute | solution.py:494
  22.3 0.3 collective-permute-start.5
  22.7 3.7 %collective-permute-start.8 = (bf16[128,512]{1,0:T(8,128)(2,1)S(1)}, bf16[128,512]{1,0:T(8,128)(2,1)S(1)}, u32[]{:S(2)}, u32[]{:S(2)}) collective-permute-start(bf16[128,512]{1,0:T(8,128)(2,1)S(1)} %shard_map.108), channel_id=1, source_target_pairs={{0,96},{4,100},{8,104},{12,108},{16,112},{20,116},{24,120},{28,124... | collective-permute-start | bytes 393224 | tf_op jit(solution)/shard_map/ppermute | solution.py:494
  26.4 0.3 collective-permute-start.7
  26.7 3.1 %shard_map.105 = (bf16[2,2,768,256]{3,2,1,0:T(8,128)(2,1)S(1)}, bf16[2,512,256]{2,1,0:T(8,128)(2,1)S(1)}, f32[128,512]{1,0:T(8,128)S(1)}, f32[8,512]{1,0:T(8,128)S(1)}) custom-call(s32[4]{0:T(128)S(1)} %copy-done.1, s32[4]{0:T(128)S(1)} %copy-done.7, s32[1]{0:T(128)S(6)} %select_n.7.par.refs_2_.refs_1_, s32[1]{0:T(128)} %bitcast.refs_3_, ...), custom_call_target="tpu_custom_call" | custom-call | flops 3000000000 | bytes 4000000 | tf_op jit(solution)/shard_map/pallas_call | solution.py:33
  29.8 0.5 collective-permute-done.8.rest_6_
  30.3 0.6 collective-permute-start.9
  30.9 3.3 %shard_map.104 = (bf16[2,2,768,256]{3,2,1,0:T(8,128)(2,1)S(1)}, bf16[2,512,256]{2,1,0:T(8,128)(2,1)S(1)}, f32[128,512]{1,0:T(8,128)S(1)}, f32[8,512]{1,0:T(8,128)S(1)}) custom-call(s32[4]{0:T(128)S(1)} %copy-done.1, s32[4]{0:T(128)S(1)} %copy-done.7, s32[1]{0:T(128)S(6)} %select_n.7.par.refs_2_.refs_1_, s32[1]{0:T(128)} %bitcast.refs_3_, ...), custom_call_target="tpu_custom_call" | custom-call | flops 3000000000 | bytes 4000000 | tf_op jit(solution)/shard_map/pallas_call | solution.py:33
  34.2 3.2 %shard_map.109 = (bf16[4,1024,128]{2,1,0:T(8,128)(2,1)S(1)}, bf16[512,256]{1,0:T(8,128)(2,1)S(1)}, f32[16,512]{1,0:T(8,128)S(1)}) custom-call(s32[4]{0:T(128)S(1)} %copy-done.1, bf16[256,512]{1,0:T(8,128)(2,1)S(1)} %get-tuple-element.43.refs_4_.qt.refs_2_, bf16[256,512]{1,0:T(8,128)(2,1)S(1)} %get-tuple-element.44.gt.refs_3_, ...), custom_call_target="tpu_custom_call" | custom-call | flops 3000000000 | bytes 4000000 | tf_op jit(solution)/shard_map/pallas_call | solution.py:33
  37.4 1.8 %shard_map.111 = (bf16[512,512]{1,0:T(8,128)(2,1)S(1)}, f32[512,512]{1,0:T(8,128)S(1)}, f32[256,128]{1,0:T(8,128)S(1)}) custom-call(bf16[256,512]{1,0:T(8,128)(2,1)S(1)} %get-tuple-element.43.refs_4_.qt.refs_2_, bf16[256,512]{1,0:T(8,128)(2,1)S(1)} %get-tuple-element.44.gt.refs_3_, f32[16,512]{1,0:T(8,128)S(1)} %get-tuple-element.54.stat2.refs_4_, ...), custom_call_target="tpu_custom_call" | custom-call | flops 4000000000 | bytes 5000000 | tf_op jit(solution)/shard_map/pallas_call | solution.py:33
  39.3 0.1 collective-permute-start.19
  39.3 3.9 %collective-permute-start.14 = (bf16[256,1024]{1,0:T(8,128)(2,1)S(1)}, bf16[256,1024]{1,0:T(8,128)(2,1)S(1)}, u32[]{:S(2)}, u32[]{:S(2)}) collective-permute-start(bf16[256,1024]{1,0:T(8,128)(2,1)S(1)} %copy-done), channel_id=1, source_target_pairs={{0,3},{1,2},{2,1},{3,0},{4,7},{5,6},{6,5},{7,4},{8,11},{9,10},{10,... | collective-permute-start | bytes 1572872 | tf_op jit(solution)/shard_map/ppermute | solution.py:494
  43.2 0.1 collective-permute-start.15
  43.3 2.6 %collective-permute-start.11 = (bf16[512,256]{1,0:T(8,128)(2,1)S(1)}, bf16[512,256]{1,0:T(8,128)(2,1)S(1)}, u32[]{:S(2)}, u32[]{:S(2)}) collective-permute-start(bf16[512,256]{1,0:T(8,128)(2,1)S(1)} %get-tuple-element.53.a0), channel_id=1, source_target_pairs={{0,3},{1,2},{2,1},{3,0},{4,7},{5,6},{6,5},{7,4},{8,11},{9,10},{10,... | collective-permute-start | bytes 786440 | tf_op jit(solution)/shard_map/ppermute | solution.py:494
  45.9 0.1 shard_map.115
  46.0 2.7 %collective-permute-start.20 = (bf16[128,512]{1,0:T(8,128)(2,1)S(1)}, bf16[128,512]{1,0:T(8,128)(2,1)S(1)}, u32[]{:S(2)}, u32[]{:S(2)}) collective-permute-start(bf16[128,512]{1,0:T(8,128)(2,1)S(1)} %get-tuple-element.74), channel_id=1, source_target_pairs={{0,96},{4,100},{8,104},{12,108},{16,112},{20,116},{24,120},{28,124... | collective-permute-start | bytes 393224 | tf_op jit(solution)/shard_map/ppermute | solution.py:494
  48.7 2.3 %shard_map.112 = (bf16[256,512]{1,0:T(8,128)(2,1)S(1)}, f32[256,512]{1,0:T(8,128)S(1)}, f32[256,256]{1,0:T(8,128)S(1)}) custom-call(bf16[256,512]{1,0:T(8,128)(2,1)S(1)} %get-tuple-element.43.refs_4_.qt.refs_2_, bf16[256,512]{1,0:T(8,128)(2,1)S(1)} %get-tuple-element.44.gt.refs_3_, f32[16,512]{1,0:T(8,128)S(1)} %get-tuple-element.54.stat2.refs_4_, ...), custom_call_target="tpu_custom_call" | custom-call | flops 4000000000 | bytes 5000000 | tf_op jit(solution)/shard_map/pallas_call | solution.py:33
  51.1 0.3 collective-permute-done.20.got.y2
  51.4 0.1 shard_map.116
  51.4 0.1 collective-permute-start.21
  51.5 2.7 %shard_map.113 = (f32[512,256]{1,0:T(8,128)S(1)}, bf16[256,256]{1,0:T(8,128)(2,1)S(1)}, bf16[256,256]{1,0:T(8,128)(2,1)S(1)}, bf16[512,128]{1,0:T(8,128)(2,1)S(1)}) custom-call(s32[4]{0:T(128)S(1)} %copy-done.2, s32[1]{0:T(128)S(6)} %select_n.7.par.refs_2_.refs_1_, bf16[256,512]{1,0:T(8,128)(2,1)S(1)} %get-tuple-element.43.refs_4_.qt.refs_2_, ...), custom_call_target="tpu_custom_call" | custom-call | flops 4000000000 | bytes 4000000 | tf_op jit(solution)/shard_map/pallas_call | solution.py:33
  54.3 0.4 collective-permute-start.12
  54.7 0.9 %collective-permute-done.21.got.y1 = bf16[128,512]{1,0:T(8,128)(2,1)S(1)} collective-permute-done((bf16[128,512]{1,0:T(8,128)(2,1)S(1)}, bf16[128,512]{1,0:T(8,128)(2,1)S(1)}, u32[]{:S(2)}, u32[]{:S(2)}) %collective-permute-start.21) | collective-permute-done | bytes 131104 | tf_op jit(solution)/shard_map/ppermute | solution.py:494
  55.7 2.8 %collective-permute-start.22 = (bf16[128,512]{1,0:T(8,128)(2,1)S(1)}, bf16[128,512]{1,0:T(8,128)(2,1)S(1)}, u32[]{:S(2)}, u32[]{:S(2)}) collective-permute-start(bf16[128,512]{1,0:T(8,128)(2,1)S(1)} %get-tuple-element.78), channel_id=1, source_target_pairs={{0,24},{4,28},{8,16},{12,20},{16,8},{20,12},{24,0},{28,4},{32,56},... | collective-permute-start | bytes 393224 | tf_op jit(solution)/shard_map/ppermute | solution.py:494
  58.5 3.5 %shard_map.114 = (f32[512,256]{1,0:T(8,128)S(1)}, bf16[256,512]{1,0:T(8,128)(2,1)S(1)}, bf16[256,512]{1,0:T(8,128)(2,1)S(1)}, bf16[512,256]{1,0:T(8,128)(2,1)}) custom-call(s32[4]{0:T(128)S(1)} %copy-done.2, s32[1]{0:T(128)S(6)} %select_n.7.par.refs_2_.refs_1_, bf16[256,512]{1,0:T(8,128)(2,1)S(1)} %get-tuple-element.43.refs_4_.qt.refs_2_, ...), custom_call_target="tpu_custom_call" | custom-call | flops 4000000000 | bytes 4000000 | tf_op jit(solution)/shard_map/pallas_call | solution.py:33
  62.0 3.2 %collective-permute-start.17 = (bf16[256,512]{1,0:T(8,128)(2,1)S(1)}, bf16[256,512]{1,0:T(8,128)(2,1)S(1)}, u32[]{:S(2)}, u32[]{:S(2)}) collective-permute-start(bf16[256,512]{1,0:T(8,128)(2,1)S(1)} %get-tuple-element.70), channel_id=1, source_target_pairs={{0,4},{4,0},{8,12},{12,8},{16,20},{20,16},{24,28},{28,24},{32,36},... | collective-permute-start | bytes 786440 | tf_op jit(solution)/shard_map/ppermute | solution.py:494
  65.2 6.7 %collective-permute-done.11.a2 = bf16[512,256]{1,0:T(8,128)(2,1)S(1)} collective-permute-done((bf16[512,256]{1,0:T(8,128)(2,1)S(1)}, bf16[512,256]{1,0:T(8,128)(2,1)S(1)}, u32[]{:S(2)}, u32[]{:S(2)}) %collective-permute-start.11) | collective-permute-done | bytes 262176 | tf_op jit(solution)/shard_map/ppermute | solution.py:494
  71.9 0.8 collective-permute-start.18
  72.7 3.4 %collective-permute-start.16 = (bf16[256,512]{1,0:T(8,128)(2,1)S(1)}, bf16[256,512]{1,0:T(8,128)(2,1)S(1)}, u32[]{:S(2)}, u32[]{:S(2)}) collective-permute-start(bf16[256,512]{1,0:T(8,128)(2,1)S(1)} %get-tuple-element.69), channel_id=1, source_target_pairs={{0,4},{4,0},{8,12},{12,8},{16,20},{20,16},{24,28},{28,24},{32,36},... | collective-permute-start | bytes 786440 | tf_op jit(solution)/shard_map/ppermute | solution.py:494
  76.2 0.1 collective-permute-start.23
  76.2 1.3 %collective-permute-done.12.a3 = bf16[512,256]{1,0:T(8,128)(2,1)S(1)} collective-permute-done((bf16[512,256]{1,0:T(8,128)(2,1)S(1)}, bf16[512,256]{1,0:T(8,128)(2,1)S(1)}, u32[]{:S(2)}, u32[]{:S(2)}) %collective-permute-start.12) | collective-permute-done | bytes 262176 | tf_op jit(solution)/shard_map/ppermute | solution.py:494
  77.6 2.2 %shard_map.110 = bf16[512,1024]{1,0:T(8,128)(2,1)} custom-call(bf16[512,256]{1,0:T(8,128)(2,1)S(1)} %get-tuple-element.53.a0, bf16[512,256]{1,0:T(8,128)(2,1)S(1)} %collective-permute-done.10.a1, bf16[512,256]{1,0:T(8,128)(2,1)S(1)} %collective-permute-done.11.a2, bf16[512,256]{1,0:T(8,128)(2,1)S(1)} %collective-permute-done.12.a3, ...), custom_call_target="tpu_custom_call" | custom-call | flops 1000000000 | bytes 4000000 | tf_op jit(solution)/shard_map/pallas_call | solution.py:33
  79.8 1.5 %collective-permute-done.23.x1 = bf16[128,512]{1,0:T(8,128)(2,1)S(1)} collective-permute-done((bf16[128,512]{1,0:T(8,128)(2,1)S(1)}, bf16[128,512]{1,0:T(8,128)(2,1)S(1)}, u32[]{:S(2)}, u32[]{:S(2)}) %collective-permute-start.23) | collective-permute-done | bytes 131104 | tf_op jit(solution)/shard_map/ppermute | solution.py:494
  81.3 2.1 %shard_map.119 = (bf16[512,256]{1,0:T(8,128)(2,1)}, bf16[512,256]{1,0:T(8,128)(2,1)}) custom-call(s32[4]{0:T(128)S(1)} %copy-done.2, s32[1]{0:T(128)S(6)} %select_n.7.par.refs_2_.refs_1_, f32[512,256]{1,0:T(8,128)S(1)} %get-tuple-element.67.own0, f32[512,256]{1,0:T(8,128)S(1)} %get-tuple-element.68.own1, bf16[256,512]{1,0:T(8,128)(2,1)S(1)} %collective-permute-done.16.ret, ...), custom_call_target="tpu_custom_call" | custom-call | flops 300000000 | bytes 3000000 | tf_op jit(solution)/shard_map/pallas_call | solution.py:33
  (34 shorter events, 0.2 us)
Async XLA Ops:
  0.6 15.5 %copy-start = (bf16[256,1024]{1,0:T(8,128)(2,1)S(1)}, bf16[256,1024]{1,0:T(8,128)(2,1)}, u32[]{:S(2)}) copy-start(bf16[256,1024]{1,0:T(8,128)(2,1)} %w0.1) | copy-start | bytes 1572868
  0.7 0.7 copy-start.1
  1.4 0.9 %copy-start.4 = (bf16[512,256]{1,0:T(8,128)(2,1)S(1)}, bf16[512,256]{1,0:T(8,128)(2,1)}, u32[]{:S(2)}) copy-start(bf16[512,256]{1,0:T(8,128)(2,1)} %k.1) | copy-start | bytes 786436
  2.3 0.9 %copy-start.5 = (bf16[512,256]{1,0:T(8,128)(2,1)S(1)}, bf16[512,256]{1,0:T(8,128)(2,1)}, u32[]{:S(2)}) copy-start(bf16[512,256]{1,0:T(8,128)(2,1)} %v.1) | copy-start | bytes 786436
  3.3 14.5 %copy-start.3 = (bf16[512,1024]{1,0:T(8,128)(2,1)S(1)}, bf16[512,1024]{1,0:T(8,128)(2,1)}, u32[]{:S(2)}) copy-start(bf16[512,1024]{1,0:T(8,128)(2,1)} %up.1) | copy-start | bytes 3145732
  3.3 14.5 %copy-start.6 = (bf16[512,256]{1,0:T(8,128)(2,1)S(1)}, bf16[512,256]{1,0:T(8,128)(2,1)}, u32[]{:S(2)}) copy-start(bf16[512,256]{1,0:T(8,128)(2,1)} %q.1) | copy-start | bytes 786436
  4.4 4.9 %collective-permute-start.2 = (bf16[128,512]{1,0:T(8,128)(2,1)S(1)}, bf16[128,512]{1,0:T(8,128)(2,1)S(1)}, u32[]{:S(2)}, u32[]{:S(2)}) collective-permute-start(bf16[128,512]{1,0:T(8,128)(2,1)S(1)} %get-tuple-element.52), channel_id=1, source_target_pairs={{0,8},{4,12},{8,0},{12,4},{16,24},{20,28},{24,16},{28,20},{32,40},... | collective-permute-start | bytes 393224 | tf_op jit(solution)/shard_map/ppermute | solution.py:494
  6.5 20.0 %collective-permute-start = (bf16[384,512]{1,0:T(8,128)(2,1)S(1)}, bf16[384,512]{1,0:T(8,128)(2,1)S(1)}, u32[]{:S(2)}, u32[]{:S(2)}) collective-permute-start(bf16[384,512]{1,0:T(8,128)(2,1)S(1)} %get-tuple-element.46), channel_id=1, source_target_pairs={{0,4},{4,0},{8,12},{12,8},{16,20},{20,16},{24,28},{28,24},{32,36},... | collective-permute-start | bytes 1179656 | tf_op jit(solution)/shard_map/ppermute | solution.py:494
  9.3 5.3 %collective-permute-start.4 = (bf16[128,512]{1,0:T(8,128)(2,1)S(1)}, bf16[128,512]{1,0:T(8,128)(2,1)S(1)}, u32[]{:S(2)}, u32[]{:S(2)}) collective-permute-start(bf16[128,512]{1,0:T(8,128)(2,1)S(1)} %shard_map.106), channel_id=1, source_target_pairs={{0,24},{4,28},{8,16},{12,20},{16,8},{20,12},{24,0},{28,4},{32,56},... | collective-permute-start | bytes 393224 | tf_op jit(solution)/shard_map/ppermute | solution.py:494
  12.2 10.5 %collective-permute-start.1 = (bf16[256,512]{1,0:T(8,128)(2,1)S(1)}, bf16[256,512]{1,0:T(8,128)(2,1)S(1)}, u32[]{:S(2)}, u32[]{:S(2)}) collective-permute-start(bf16[256,512]{1,0:T(8,128)(2,1)S(1)} %get-tuple-element.47), channel_id=1, source_target_pairs={{0,124},{4,8},{8,4},{12,16},{16,12},{20,24},{24,20},{28,32},{32,28... | collective-permute-start | bytes 786440 | tf_op jit(solution)/shard_map/ppermute | solution.py:499
  14.6 12.1 %copy-start.7 = (s32[4]{0:T(128)S(1)}, s32[4]{0:T(128)}, u32[]{:S(2)}) copy-start(s32[4]{0:T(128)} %refs_1_.3) | copy-start | bytes 52
  14.6 7.7 %collective-permute-start.6 = (bf16[128,512]{1,0:T(8,128)(2,1)S(1)}, bf16[128,512]{1,0:T(8,128)(2,1)S(1)}, u32[]{:S(2)}, u32[]{:S(2)}) collective-permute-start(bf16[128,512]{1,0:T(8,128)(2,1)S(1)} %shard_map.107), channel_id=1, source_target_pairs={{0,32},{4,36},{8,40},{12,44},{16,48},{20,52},{24,56},{28,60},{32,0... | collective-permute-start | bytes 393224 | tf_op jit(solution)/shard_map/ppermute | solution.py:494
  16.2 27.0 %collective-permute-start.13 = (bf16[256,1024]{1,0:T(8,128)(2,1)S(1)}, bf16[256,1024]{1,0:T(8,128)(2,1)S(1)}, u32[]{:S(2)}, u32[]{:S(2)}) collective-permute-start(bf16[256,1024]{1,0:T(8,128)(2,1)S(1)} %copy-done), channel_id=1, source_target_pairs={{0,1},{1,0},{2,3},{3,2},{4,5},{5,4},{6,7},{7,6},{8,9},{9,8},{10,11... | collective-permute-start | bytes 1572872 | tf_op jit(solution)/shard_map/ppermute | solution.py:494
  19.0 15.1 %collective-permute-start.3 = (bf16[128,512]{1,0:T(8,128)(2,1)S(1)}, bf16[128,512]{1,0:T(8,128)(2,1)S(1)}, u32[]{:S(2)}, u32[]{:S(2)}) collective-permute-start(bf16[128,512]{1,0:T(8,128)(2,1)S(1)} %collective-permute-done.2.x1.rest_0_), channel_id=1, source_target_pairs={{0,4},{4,0},{8,12},{12,8},{16,20},{20,16},{24,28},{28,24},{32,36},... | collective-permute-start | bytes 393224 | tf_op jit(solution)/shard_map/ppermute | solution.py:494
  22.3 11.8 %collective-permute-start.5 = (bf16[128,512]{1,0:T(8,128)(2,1)S(1)}, bf16[128,512]{1,0:T(8,128)(2,1)S(1)}, u32[]{:S(2)}, u32[]{:S(2)}) collective-permute-start(bf16[128,512]{1,0:T(8,128)(2,1)S(1)} %collective-permute-done.4.x2.rest_2_), channel_id=1, source_target_pairs={{0,4},{4,0},{8,12},{12,8},{16,20},{20,16},{24,28},{28,24},{32,36},... | collective-permute-start | bytes 393224 | tf_op jit(solution)/shard_map/ppermute | solution.py:494
  22.7 7.6 %collective-permute-start.8 = (bf16[128,512]{1,0:T(8,128)(2,1)S(1)}, bf16[128,512]{1,0:T(8,128)(2,1)S(1)}, u32[]{:S(2)}, u32[]{:S(2)}) collective-permute-start(bf16[128,512]{1,0:T(8,128)(2,1)S(1)} %shard_map.108), channel_id=1, source_target_pairs={{0,96},{4,100},{8,104},{12,108},{16,112},{20,116},{24,120},{28,124... | collective-permute-start | bytes 393224 | tf_op jit(solution)/shard_map/ppermute | solution.py:494
  26.4 7.8 %collective-permute-start.7 = (bf16[128,512]{1,0:T(8,128)(2,1)S(1)}, bf16[128,512]{1,0:T(8,128)(2,1)S(1)}, u32[]{:S(2)}, u32[]{:S(2)}) collective-permute-start(bf16[128,512]{1,0:T(8,128)(2,1)S(1)} %collective-permute-done.6.y1.rest_4_), channel_id=1, source_target_pairs={{0,4},{4,0},{8,12},{12,8},{16,20},{20,16},{24,28},{28,24},{32,36},... | collective-permute-start | bytes 393224 | tf_op jit(solution)/shard_map/ppermute | solution.py:494
  30.3 3.9 %collective-permute-start.9 = (bf16[128,512]{1,0:T(8,128)(2,1)S(1)}, bf16[128,512]{1,0:T(8,128)(2,1)S(1)}, u32[]{:S(2)}, u32[]{:S(2)}) collective-permute-start(bf16[128,512]{1,0:T(8,128)(2,1)S(1)} %collective-permute-done.8.rest_6_), channel_id=1, source_target_pairs={{0,4},{4,0},{8,12},{12,8},{16,20},{20,16},{24,28},{28,24},{32,36},... | collective-permute-start | bytes 393224 | tf_op jit(solution)/shard_map/ppermute | solution.py:494
  39.3 6.6 %collective-permute-start.19 = (bf16[512,512]{1,0:T(8,128)(2,1)S(1)}, bf16[512,512]{1,0:T(8,128)(2,1)S(1)}, u32[]{:S(2)}, u32[]{:S(2)}) collective-permute-start(bf16[512,512]{1,0:T(8,128)(2,1)S(1)} %get-tuple-element.73), channel_id=1, source_target_pairs={{0,4},{4,0},{8,12},{12,8},{16,20},{20,16},{24,28},{28,24},{32,36},... | collective-permute-start | bytes 1572872 | tf_op jit(solution)/shard_map/ppermute | solution.py:494
  39.3 22.6 %collective-permute-start.14 = (bf16[256,1024]{1,0:T(8,128)(2,1)S(1)}, bf16[256,1024]{1,0:T(8,128)(2,1)S(1)}, u32[]{:S(2)}, u32[]{:S(2)}) collective-permute-start(bf16[256,1024]{1,0:T(8,128)(2,1)S(1)} %copy-done), channel_id=1, source_target_pairs={{0,3},{1,2},{2,1},{3,0},{4,7},{5,6},{6,5},{7,4},{8,11},{9,10},{10,... | collective-permute-start | bytes 1572872 | tf_op jit(solution)/shard_map/ppermute | solution.py:494
  43.2 32.9 %collective-permute-start.15 = (bf16[256,1024]{1,0:T(8,128)(2,1)S(1)}, bf16[256,1024]{1,0:T(8,128)(2,1)S(1)}, u32[]{:S(2)}, u32[]{:S(2)}) collective-permute-start(bf16[256,1024]{1,0:T(8,128)(2,1)S(1)} %collective-permute-done.13.w1), channel_id=1, source_target_pairs={{0,3},{1,2},{2,1},{3,0},{4,7},{5,6},{6,5},{7,4},{8,11},{9,10},{10,... | collective-permute-start | bytes 1572872 | tf_op jit(solution)/shard_map/ppermute | solution.py:494
  43.3 11.0 %collective-permute-start.10 = (bf16[512,256]{1,0:T(8,128)(2,1)S(1)}, bf16[512,256]{1,0:T(8,128)(2,1)S(1)}, u32[]{:S(2)}, u32[]{:S(2)}) collective-permute-start(bf16[512,256]{1,0:T(8,128)(2,1)S(1)} %get-tuple-element.53.a0), channel_id=1, source_target_pairs={{0,1},{1,0},{2,3},{3,2},{4,5},{5,4},{6,7},{7,6},{8,9},{9,8},{10,11... | collective-permute-start | bytes 786440 | tf_op jit(solution)/shard_map/ppermute | solution.py:494
  43.3 28.6 %collective-permute-start.11 = (bf16[512,256]{1,0:T(8,128)(2,1)S(1)}, bf16[512,256]{1,0:T(8,128)(2,1)S(1)}, u32[]{:S(2)}, u32[]{:S(2)}) collective-permute-start(bf16[512,256]{1,0:T(8,128)(2,1)S(1)} %get-tuple-element.53.a0), channel_id=1, source_target_pairs={{0,3},{1,2},{2,1},{3,0},{4,7},{5,6},{6,5},{7,4},{8,11},{9,10},{10,... | collective-permute-start | bytes 786440 | tf_op jit(solution)/shard_map/ppermute | solution.py:494
  46.0 5.4 %collective-permute-start.20 = (bf16[128,512]{1,0:T(8,128)(2,1)S(1)}, bf16[128,512]{1,0:T(8,128)(2,1)S(1)}, u32[]{:S(2)}, u32[]{:S(2)}) collective-permute-start(bf16[128,512]{1,0:T(8,128)(2,1)S(1)} %get-tuple-element.74), channel_id=1, source_target_pairs={{0,96},{4,100},{8,104},{12,108},{16,112},{20,116},{24,120},{28,124... | collective-permute-start | bytes 393224 | tf_op jit(solution)/shard_map/ppermute | solution.py:494
  48.7 2.8 %copy-start.2 = (s32[4]{0:T(128)S(1)}, s32[4]{0:T(128)}, u32[]{:S(2)}) copy-start(s32[4]{0:T(128)} %off.7) | copy-start | bytes 52
  51.4 4.2 %collective-permute-start.21 = (bf16[128,512]{1,0:T(8,128)(2,1)S(1)}, bf16[128,512]{1,0:T(8,128)(2,1)S(1)}, u32[]{:S(2)}, u32[]{:S(2)}) collective-permute-start(bf16[128,512]{1,0:T(8,128)(2,1)S(1)} %get-tuple-element.76), channel_id=1, source_target_pairs={{0,32},{4,36},{8,40},{12,44},{16,48},{20,52},{24,56},{28,60},{32,0... | collective-permute-start | bytes 393224 | tf_op jit(solution)/shard_map/ppermute | solution.py:494
  54.3 23.3 %collective-permute-start.12 = (bf16[512,256]{1,0:T(8,128)(2,1)S(1)}, bf16[512,256]{1,0:T(8,128)(2,1)S(1)}, u32[]{:S(2)}, u32[]{:S(2)}) collective-permute-start(bf16[512,256]{1,0:T(8,128)(2,1)S(1)} %collective-permute-done.10.a1), channel_id=1, source_target_pairs={{0,3},{1,2},{2,1},{3,0},{4,7},{5,6},{6,5},{7,4},{8,11},{9,10},{10,... | collective-permute-start | bytes 786440 | tf_op jit(solution)/shard_map/ppermute | solution.py:494
  55.7 17.1 %collective-permute-start.22 = (bf16[128,512]{1,0:T(8,128)(2,1)S(1)}, bf16[128,512]{1,0:T(8,128)(2,1)S(1)}, u32[]{:S(2)}, u32[]{:S(2)}) collective-permute-start(bf16[128,512]{1,0:T(8,128)(2,1)S(1)} %get-tuple-element.78), channel_id=1, source_target_pairs={{0,24},{4,28},{8,16},{12,20},{16,8},{20,12},{24,0},{28,4},{32,56},... | collective-permute-start | bytes 393224 | tf_op jit(solution)/shard_map/ppermute | solution.py:494
  62.0 17.8 %collective-permute-start.17 = (bf16[256,512]{1,0:T(8,128)(2,1)S(1)}, bf16[256,512]{1,0:T(8,128)(2,1)S(1)}, u32[]{:S(2)}, u32[]{:S(2)}) collective-permute-start(bf16[256,512]{1,0:T(8,128)(2,1)S(1)} %get-tuple-element.70), channel_id=1, source_target_pairs={{0,4},{4,0},{8,12},{12,8},{16,20},{20,16},{24,28},{28,24},{32,36},... | collective-permute-start | bytes 786440 | tf_op jit(solution)/shard_map/ppermute | solution.py:494
  71.9 7.8 %collective-permute-start.18 = (bf16[256,512]{1,0:T(8,128)(2,1)S(1)}, bf16[256,512]{1,0:T(8,128)(2,1)S(1)}, u32[]{:S(2)}, u32[]{:S(2)}) collective-permute-start(bf16[256,512]{1,0:T(8,128)(2,1)S(1)} %get-tuple-element.71), channel_id=1, source_target_pairs={{0,124},{4,8},{8,4},{12,16},{16,12},{20,24},{24,20},{28,32},{32,28... | collective-permute-start | bytes 786440 | tf_op jit(solution)/shard_map/ppermute | solution.py:499
  72.7 7.0 %collective-permute-start.16 = (bf16[256,512]{1,0:T(8,128)(2,1)S(1)}, bf16[256,512]{1,0:T(8,128)(2,1)S(1)}, u32[]{:S(2)}, u32[]{:S(2)}) collective-permute-start(bf16[256,512]{1,0:T(8,128)(2,1)S(1)} %get-tuple-element.69), channel_id=1, source_target_pairs={{0,4},{4,0},{8,12},{12,8},{16,20},{20,16},{24,28},{28,24},{32,36},... | collective-permute-start | bytes 786440 | tf_op jit(solution)/shard_map/ppermute | solution.py:494
  76.2 5.1 %collective-permute-start.23 = (bf16[128,512]{1,0:T(8,128)(2,1)S(1)}, bf16[128,512]{1,0:T(8,128)(2,1)S(1)}, u32[]{:S(2)}, u32[]{:S(2)}) collective-permute-start(bf16[128,512]{1,0:T(8,128)(2,1)S(1)} %shard_map.118), channel_id=1, source_target_pairs={{0,8},{4,12},{8,0},{12,4},{16,24},{20,28},{24,16},{28,20},{32,40},... | collective-permute-start | bytes 393224 | tf_op jit(solution)/shard_map/ppermute | solution.py:494
where the time goes:
time: 83.5 us; the launch traced here: 83.4 us
  starting transfers between devices  39.3 us (47%)
  Pallas kernels  26.8 us (32%)
  waiting for transfers between devices  13.8 us (17%)
  local copies, waits for them, and re-layouts  2.63 us (3%)
  between operations  0.87 us (1%)
    ppermute x22, starting transfers between devices, swap(): lax.ppermute(x, axis, [(i, i ^ mask) for i in range(lax.axis_size(axis))])  36.8 us
    pallas_call x18, Pallas kernels, call(): pl.pallas_call(body, out_shape=outs, grid=(1,), in_specs=in_specs, out_sp...  26.8 us
    ppermute x22, waiting for transfers between devices, swap(): lax.ppermute(x, axis, [(i, i ^ mask) for i in range(lax.axis_size(axis))])  13.8 us
    unnamed x16, local copies, waits for them, and re-layouts  2.63 us
    ppermute x2, starting transfers between devices, side(): return lax.ppermute(x, 'tm', pairs)  2.43 us
  transfers between devices with their start and end apart: 24, of which 8 were waited for; matrix products, arithmetic and copies ran while one was open for 0% of the time, Pallas kernels for 28%

commit v1 on v0

v1 whole, which is shorter than its diff:
```python
import jax
import jax.numpy as jnp
from jax import lax
from jax.experimental import pallas as pl
from jax.experimental.pallas import tpu as pltpu
from jax.sharding import PartitionSpec as P


F32 = jnp.float32
BF16 = jnp.bfloat16
NEG = -1e30
NT = (((1,), (1,)), ((), ()))
SMEM = pl.BlockSpec(memory_space=pltpu.SMEM)


def sds(shape, dtype):
    return jax.ShapeDtypeStruct(shape, dtype)


def dot(a, b):
    return jnp.dot(a, b, preferred_element_type=F32)


def dot_nt(a, b):
    return lax.dot_general(a, b, NT, preferred_element_type=F32)


def call(body, ins, outs, scratch=(), flops=0, nbytes=0, specs=None, out_specs=None, vmem=24):
    full = lambda x: pl.BlockSpec(x.shape, (lambda *_: (0,) * len(x.shape)))
    specs = specs or [None] * len(ins)
    in_specs = [full(x) if s is None else s for x, s in zip(ins, specs)]
    out_specs = out_specs or [full(o) for o in outs]
    return pl.pallas_call(
        body,
        out_shape=outs,
        grid=(1,),
        in_specs=in_specs,
        out_specs=out_specs,
        scratch_shapes=list(scratch),
        cost_estimate=pl.CostEstimate(flops=int(flops), bytes_accessed=int(nbytes), transcendentals=0),
        compiler_params=pltpu.CompilerParams(vmem_limit_bytes=vmem << 20),
    )(*ins)


def iota(shape, axis):
    return lax.broadcasted_iota(jnp.int32, shape, axis)


def place_row(offset):
    n = iota((1, 256), 1)
    u = jnp.where(n >= 128, 2 * (n - 128) + 1, 4 * (n - 64) + 2)
    u = jnp.where(n >= 64, u, 8 * (n - 32) + 4)
    u = jnp.where(n >= 32, u, 16 * (n - 16) + 8)
    u = jnp.where(n >= 16, u, 32 * (n - 8) + 16)
    u = jnp.where(n >= 8, u, 32 * n)
    return (u + offset) & 255


def rank_row(offset):
    u = (iota((1, 256), 1) - offset) & 255
    n = jnp.where((u & 16) != 0, 8 + (u >> 5), u >> 5)
    n = jnp.where((u & 8) != 0, 16 + (u >> 4), n)
    n = jnp.where((u & 4) != 0, 32 + (u >> 3), n)
    n = jnp.where((u & 2) != 0, 64 + (u >> 2), n)
    return jnp.where((u & 1) != 0, 128 + (u >> 1), n)


def depth(n):
    d = jnp.where(n < 64, 2, 1)
    d = jnp.where(n < 32, 3, d)
    d = jnp.where(n < 16, 4, d)
    return jnp.where(n < 8, 5, d)


def to_depth(offset):
    return (iota((256, 256), 0) == rank_row(offset)).astype(F32).astype(BF16)


def from_depth(offset):
    return (iota((256, 256), 0) == place_row(offset)).astype(F32).astype(BF16)


def lane_first(rows, width=128):
    return (iota((rows, width), 1) % 128) < 64


def zero_pad(x, which):
    z = jnp.zeros_like(x)
    return jnp.concatenate([x, z] if which == 0 else [z, x], axis=0)


def transposed(x):
    return x.astype(F32).T.astype(BF16)


def parity(tm):
    return tm[0] & 1


def block_rows(tm, which):
    block = (1 - parity(tm)) if which == 0 else parity(tm)
    return pl.ds(pl.multiple_of(256 * block, 256), 256)


def prep_kv(off, tm, k, v, q, up, w, kvp, c1, n1, x1, qv, upv, wv, kb, vb, sem):
    copies = []
    for src, dst in ((k, kb), (v, vb), (q, qv), (up, upv)):
        for which in range(2):
            copies.append(
                pltpu.make_async_copy(
                    src.at[block_rows(tm, which)], dst.at[pl.ds(256 * which, 256)], sem.at[len(copies)]
                )
            )
    copies.append(pltpu.make_async_copy(w, wv, sem.at[8]))
    for c in copies:
        c.start()
    perms = [to_depth(off[h]) for h in range(4)]
    for c in copies[:4]:
        c.wait()
    keep = lane_first(256, 256)
    for pair in range(2):
        lanes = slice(pair * 128, pair * 128 + 128)
        for b in range(2):
            rows = slice(b * 256, b * 256 + 256)
            kv = jnp.concatenate([kb[rows, lanes], vb[rows, lanes]], axis=1)
            kvp[rows, pair * 256 : pair * 256 + 256] = jnp.where(
                keep, dot(perms[2 * pair], kv), dot(perms[2 * pair + 1], kv)
            ).astype(BF16)
    x1[0:64] = kvp[0:64]
    x1[64:128] = kvp[256:320]
    c1[...] = kvp[0:384]
    n1[...] = kvp[256:512]
    for c in copies[4:]:
        c.wait()


def prep_qg(off, q, up, w, qt, gt):
    g = dot_nt(w[...], up[...]).astype(BF16)
    qs = (q[...].astype(F32) * 0.125).T.astype(BF16)
    for h in range(4):
        perm = from_depth(off[h])
        hs = slice(64 * h, 64 * h + 64)
        for b in range(2):
            bs = slice(256 * b, 256 * b + 256)
            x = jnp.concatenate([qs[hs, bs], g[hs, bs]], axis=0)
            r = dot(x, perm).astype(BF16)
            qt[b, hs] = r[0:64]
            gt[b, hs] = r[64:128]


def pack_rows(pieces):
    return jnp.concatenate([p.astype(F32) for p in pieces], axis=0).astype(BF16)


def asm_x2(kvp, x1, out):
    out[...] = pack_rows([kvp[0:32], kvp[256:288], x1[0:32], x1[64:96]])


def asm_y1(kvp, x1, x2, out):
    out[...] = pack_rows(
        [kvp[0:16], kvp[256:272], x1[0:16], x1[64:80]] + [x2[32 * j : 32 * j + 16] for j in range(4)]
    )


def asm_y2(kvp, x1, x2, y1, out):
    heads = [kvp[0:16], kvp[256:272], x1[0:16], x1[64:80]]
    heads += [x2[32 * j : 32 * j + 16] for j in range(4)]
    heads += [y1[16 * j : 16 * j + 16] for j in range(8)]
    out[...] = jnp.concatenate([h.astype(F32)[0:8] for h in heads], axis=0).astype(BF16)


def near_count():
    s = (128, 128)
    return jnp.minimum(depth(iota(s, 0)), depth(iota(s, 1))).astype(F32)


def near_keys(kv, c1, lanes):
    return jnp.concatenate([kv[0:128, lanes], kv[256:384, lanes], c1[0:128, lanes], c1[256:384, lanes]], axis=0)


def pair_slices(pair):
    return slice(256 * pair, 256 * pair + 128), slice(256 * pair + 128, 256 * pair + 256)


def side_chunks(which, kv, halo, lanes):
    own, other = slice(256 * which, 256 * which + 256), slice(256 - 256 * which, 512 - 256 * which)
    return [halo[0:256, lanes], kv[own, lanes], kv[other, lanes]]


def fwd_near(which, off, win, tm, qt, kv, c1, *rest):
    if which == 0:
        halo = c1
        pw, p1, acc_out, stat, vt, v1t, k1, dist, sw, s1 = rest
    else:
        halo, pw, p1, acc_out, stat, vt, v1t, k1, dist, sw, s1 = rest
    count = near_count()
    sign = (1 - 2 * parity(tm)) * (1 if which == 0 else -1)
    for h in range(4):
        a, pair = h % 2, h // 2
        lo, hi = pair_slices(pair)
        if a == 0:
            vt[...] = transposed(jnp.concatenate(side_chunks(which, kv, halo, hi), axis=0))
            k1[...] = near_keys(kv, c1, lo)
            v1t[...] = transposed(near_keys(kv, c1, hi))
        row = place_row(off[h]).astype(F32) * sign.astype(F32)
        col = jnp.broadcast_to(row, (128, 256)).T
        dist[...] = jnp.concatenate([col, col], axis=1) - row
        reach = win[h].astype(F32)
        if which == 0:
            outer = reach - 256.0
        else:
            outer = jnp.where((tm[0] == 0) | (tm[0] == 31), -1000.0, reach - 256.0)
        qz = zero_pad(qt[which, 64 * h : 64 * h + 64, :], a)
        top = None
        for c, keys in enumerate(side_chunks(which, kv, halo, lo)):
            sc = dot(keys, qz)
            d = dist[...]
            ok = (d <= outer, jnp.abs(d) <= reach, d >= 256.0 - reach)[c]
            sc = jnp.where(ok, sc, NEG)
            sw[256 * c : 256 * c + 256] = sc
            part = jnp.max(sc, axis=0, keepdims=True)
            top = part if top is None else jnp.maximum(top, part)
        sc = dot(k1[...], qz[:, 0:128])
        s1[...] = sc
        near_top = jnp.maximum(top[:, 0:128], jnp.max(sc, axis=0, keepdims=True))
        top = jnp.concatenate([near_top, top[:, 128:256]], axis=1)
        total = jnp.zeros((1, 256), F32)
        for c in range(3):
            e = jnp.exp(sw[256 * c : 256 * c + 256] - top)
            total += jnp.sum(e, axis=0, keepdims=True)
            pw[h, 256 * c : 256 * c + 256, :] = e.astype(BF16)
        vh, hs = slice(64 * a, 64 * a + 64), slice(64 * h, 64 * h + 64)
        acc = dot(vt[vh, :], pw[h])
        near_sum = jnp.zeros((1, 128), F32)
        for c in range(4):
            e = count * jnp.exp(s1[128 * c : 128 * c + 128] - near_top)
            near_sum += jnp.sum(e, axis=0, keepdims=True)
            p1[h, 128 * c : 128 * c + 128, :] = e.astype(BF16)
        near_acc = dot(v1t[vh, :], p1[h])
        acc_out[hs, 0:128] = acc[:, 0:128] + near_acc
        acc_out[hs, 128:256] = acc[:, 128:256]
        stat[h : h + 1, :] = top
        stat[4 + h : 5 + h, 0:128] = total[:, 0:128] + near_sum
        stat[4 + h : 5 + h, 128:256] = total[:, 128:256]


def far_count(level):
    s = (256 >> level, 128)
    both = jnp.minimum(depth(iota(s, 0)), depth(iota(s, 1) & 63))
    return jnp.maximum(both - level + 1, 0).astype(F32)


def far_lanes(x):
    return jnp.concatenate([x[:, 0:64], x[:, 256:320]], axis=1)


def far_cols(x, hs):
    return jnp.concatenate([x[0, hs, 0:64], x[1, hs, 0:64]], axis=1)


def wide(x, b, filler):
    rows = x.shape[0]
    return jnp.concatenate([x[:, 64 * b : 64 * b + 64], jnp.full((rows, 192), filler, F32)], axis=1)


def unperm_pair(off, pair, src):
    first, second = from_depth(off[2 * pair]), from_depth(off[2 * pair + 1])
    return jnp.where(lane_first(256), dot_nt(first, src), dot_nt(second, src)).astype(BF16)


def fwd_far(off, qt, gt, acc0, acc1, st0, st1, *rest):
    bufs, (pf, attn, stat2, kf, vft, mult, at) = rest[:8], rest[8:]
    for level in range(2, 6):
        n = 256 >> level
        piece = far_count(level)
        for j in range(256 // n):
            mult[256 * (level - 2) + n * j : 256 * (level - 2) + n * j + n] = piece
    for pair in range(2):
        lo, hi = pair_slices(pair)
        for j, buf in enumerate(bufs):
            kf[128 * j : 128 * j + 128] = buf[:, lo]
        vft[...] = transposed(jnp.concatenate([buf[:, hi] for buf in bufs], axis=0))
        for a in range(2):
            vh = slice(64 * a, 64 * a + 64)
            h = 2 * pair + a
            hs = slice(64 * h, 64 * h + 64)
            qz = zero_pad(far_cols(qt, hs), a)
            cnt = mult[...]
            sc = jnp.where(cnt > 0, dot(kf[...], qz), NEG)
            ftop = jnp.max(sc, axis=0, keepdims=True)
            e = cnt * jnp.exp(sc - ftop)
            fsum = jnp.sum(e, axis=0, keepdims=True)
            pf[h] = e.astype(BF16)
            facc = dot(vft[vh, :], pf[h])
            for b in range(2):
                bs = slice(256 * b, 256 * b + 256)
                acc_in, stat = (acc0, st0) if b == 0 else (acc1, st1)
                ntop, nsum = stat[h : h + 1, :], stat[4 + h : 5 + h, :]
                ftopw = wide(ftop, b, NEG)
                top = jnp.maximum(ntop, ftopw)
                wn, wf = jnp.exp(ntop - top), jnp.exp(ftopw - top)
                norm = nsum * wn + wide(fsum, b, 0.0) * wf
                acc = acc_in[hs, :] * wn + wide(facc, b, 0.0) * wf
                o = (acc / norm).astype(BF16)
                at[vh, bs] = o
                stat2[h : h + 1, bs] = wn / norm
                stat2[4 + h : 5 + h, bs] = wf / norm
                stat2[8 + h : 9 + h, bs] = jnp.sum(
                    gt[b, hs].astype(F32) * o.astype(F32), axis=0, keepdims=True
                )
        for b in range(2):
            bs = slice(256 * b, 256 * b + 256)
            attn[bs, 128 * pair : 128 * pair + 128] = unperm_pair(off, pair, at[:, bs])


def bwd_far(qt, gt, stat2, pf, *rest):
    bufs, (ret, own_far, dq, kx, vx) = rest[:8], rest[8:]
    for pair in range(2):
        lo, hi = pair_slices(pair)
        for j, buf in enumerate(bufs):
            kx[128 * j : 128 * j + 128] = buf[:, lo]
            vx[128 * j : 128 * j + 128] = buf[:, hi]
        kt = transposed(kx[...])
        grads, scaled_q, scaled_g = [], [], []
        for a in range(2):
            h = 2 * pair + a
            hs, vh = slice(64 * h, 64 * h + 64), slice(64 * a, 64 * a + 64)
            cf = far_lanes(stat2[4 + h : 5 + h, :])
            delta = far_lanes(stat2[8 + h : 9 + h, :])
            q, g = far_cols(qt, hs), far_cols(gt, hs)
            dp = dot(vx[...], zero_pad(g, a))
            ds = (pf[h].astype(F32) * (dp - delta)).astype(BF16)
            grads.append(ds)
            scaled_q.append(zero_pad((q.astype(F32) * cf).astype(BF16), a))
            scaled_g.append(zero_pad((g.astype(F32) * cf).astype(BF16), a))
            dq[hs, :] = dot(kt[vh, :], ds) * cf
        dk = dot_nt(jnp.concatenate(grads, axis=1), jnp.concatenate(scaled_q, axis=1))
        dv = dot_nt(jnp.concatenate([pf[2 * pair], pf[2 * pair + 1]], axis=1), jnp.concatenate(scaled_g, axis=1))
        for j in range(4):
            mine, theirs = slice(256 * j, 256 * j + 128), slice(256 * j + 128, 256 * j + 256)
            rows = slice(128 * j, 128 * j + 128)
            own_far[rows, lo] = dk[mine]
            own_far[rows, hi] = dv[mine]
            ret[rows, lo] = dk[theirs].astype(BF16)
            ret[rows, hi] = dv[theirs].astype(BF16)


def bwd_keys(qt, gt, stat2, kv, c1, p10, p11, ret, own_near, dq):
    for pair in range(2):
        lo, hi = pair_slices(pair)
        k1t = transposed(near_keys(kv, c1, lo))
        v1 = near_keys(kv, c1, hi)
        grads, scaled_q, scaled_g, probs = [], [], [], []
        for a in range(2):
            h = 2 * pair + a
            hs, vh = slice(64 * h, 64 * h + 64), slice(64 * a, 64 * a + 64)
            for b in range(2):
                bs = slice(256 * b, 256 * b + 128)
                cn, delta = stat2[h : h + 1, bs], stat2[8 + h : 9 + h, bs]
                g = gt[b, hs, 0:128]
                p = (p10 if b == 0 else p11)[h]
                ds = (p.astype(F32) * (dot(v1, zero_pad(g, a)) - delta)).astype(BF16)
                grads.append(ds)
                probs.append(p)
                scaled_q.append(zero_pad((qt[b, hs, 0:128].astype(F32) * cn).astype(BF16), a))
                scaled_g.append(zero_pad((g.astype(F32) * cn).astype(BF16), a))
                dq[hs, 128 * b : 128 * b + 128] = dot(k1t[vh, :], ds) * cn
        dk = dot_nt(jnp.concatenate(grads, axis=1), jnp.concatenate(scaled_q, axis=1))
        dv = dot_nt(jnp.concatenate(probs, axis=1), jnp.concatenate(scaled_g, axis=1))
        own_near[:, lo] = dk[0:256]
        own_near[:, hi] = dv[0:256]
        ret[:, lo] = dk[256:512].astype(BF16)
        ret[:, hi] = dv[256:512].astype(BF16)


def bwd_near(which, off, tm, qt, gt, stat2, kv, halo, pw, dqf, dqn, *rest):
    if which == 1:
        own, halo_out, gq, dqt = rest
    else:
        own_in, own_near, gq_in, own, halo_out, gq, dqt = rest
        gq[block_rows(tm, 1), :] = gq_in[...]
    bs = slice(256 * which, 256 * which + 256)
    ob = slice(256 - 256 * which, 512 - 256 * which)
    for pair in range(2):
        lo, hi = pair_slices(pair)
        vx = jnp.concatenate(side_chunks(which, kv, halo, hi), axis=0)
        kt = transposed(jnp.concatenate(side_chunks(which, kv, halo, lo), axis=0))
        grads, scaled_q, scaled_g = [], [], []
        for a in range(2):
            h = 2 * pair + a
            hs, vh = slice(64 * h, 64 * h + 64), slice(64 * a, 64 * a + 64)
            cn, delta = stat2[h : h + 1, bs], stat2[8 + h : 9 + h, bs]
            g = gt[which, hs]
            dp = dot(vx, zero_pad(g, a))
            ds = (pw[h].astype(F32) * (dp - delta)).astype(BF16)
            grads.append(ds)
            scaled_q.append(zero_pad((qt[which, hs].astype(F32) * cn).astype(BF16), a))
            scaled_g.append(zero_pad((g.astype(F32) * cn).astype(BF16), a))
            near = jnp.concatenate(
                [dqn[hs, 128 * which : 128 * which + 128], jnp.zeros((64, 128), F32)], axis=1
            )
            total = dot(kt[vh, :], ds) * cn + near + wide(dqf[hs, :], which, 0.0)
            dqt[vh, :] = (total * 0.125).astype(BF16)
        probs = jnp.concatenate([pw[2 * pair], pw[2 * pair + 1]], axis=1)
        for lanes, left, right in ((lo, jnp.concatenate(grads, axis=1), scaled_q), (hi, probs, scaled_g)):
            d = dot_nt(left, jnp.concatenate(right, axis=1))
            halo_out[:, lanes] = d[0:256].astype(BF16)
            if which == 1:
                own[bs, lanes] = d[256:512]
                own[ob, lanes] = d[512:768]
            else:
                own[bs, lanes] = d[256:512] + own_in[bs, lanes]
                own[ob, lanes] = d[512:768] + own_in[ob, lanes]
                own[0:128, lanes] += own_near[0:128, lanes]
                own[256:384, lanes] += own_near[128:256, lanes]
        r = unperm_pair(off, pair, dqt[...])
        if which == 1:
            gq[:, 128 * pair : 128 * pair + 128] = r
        else:
            gq[block_rows(tm, 0), 128 * pair : 128 * pair + 128] = r


def ret_y2(own_far, ret, rest, send):
    total = own_far[...] + ret[...].astype(F32)
    rest[...] = total[0:384]
    send[...] = total[384:512].astype(BF16)


def ret_y1(rest, got, left, send):
    y2 = got[...].astype(F32)
    left[...] = rest[0:256]
    for j in range(2):
        left[64 * j : 64 * j + 8] += y2[16 + 8 * j : 24 + 8 * j]
    for j in range(4):
        left[128 + 32 * j : 136 + 32 * j] += y2[32 + 8 * j : 40 + 8 * j]
    zero = jnp.zeros((8, 512), F32)
    extra = []
    for j in range(8):
        extra += [y2[64 + 8 * j : 72 + 8 * j], zero]
    send[...] = (rest[256:384] + jnp.concatenate(extra, axis=0)).astype(BF16)


def ret_x2(rest, got, left, send):
    y1 = got[...].astype(F32)
    left[...] = rest[0:128]
    for j in range(2):
        left[64 * j : 64 * j + 16] += y1[32 + 16 * j : 48 + 16 * j]
    zero = jnp.zeros((16, 512), F32)
    extra = []
    for j in range(4):
        extra += [y1[64 + 16 * j : 80 + 16 * j], zero]
    send[...] = (rest[128:256] + jnp.concatenate(extra, axis=0)).astype(BF16)


def ret_x1(rest, got, send):
    x2 = got[...].astype(F32)
    zero = jnp.zeros((32, 512), F32)
    extra = [x2[64:96], zero, x2[96:128], zero]
    send[...] = (rest[...] + jnp.concatenate(extra, axis=0)).astype(BF16)


def gather_own(own, near_r, hc, hn, y2, y1, x2, acc):
    acc[...] = own[...]
    acc[0:256] += hc[...].astype(F32)
    acc[256:512] += hn[...].astype(F32)
    for b in range(2):
        at = 256 * b
        acc[at : at + 128] += near_r[128 * b : 128 * b + 128].astype(F32)
        acc[at : at + 32] += x2[32 * b : 32 * b + 32].astype(F32)
        acc[at : at + 16] += y1[16 * b : 16 * b + 16].astype(F32)
        acc[at : at + 8] += y2[0:16].astype(F32)[8 * b : 8 * b + 8]


def finish(off, tm, acc, x1, gk, gv):
    keep = lane_first(256, 256)
    for pair in range(2):
        first, second = from_depth(off[2 * pair]), from_depth(off[2 * pair + 1])
        lanes = slice(128 * pair, 128 * pair + 128)
        cols = slice(256 * pair, 256 * pair + 256)
        for b in range(2):
            at = 256 * b
            head = acc[at : at + 64, cols] + x1[64 * b : 64 * b + 64, cols].astype(F32)
            x = jnp.concatenate([head, acc[at + 64 : at + 256, cols]], axis=0).astype(BF16)
            r = jnp.where(keep, dot(first, x), dot(second, x)).astype(BF16)
            gk[block_rows(tm, b), lanes] = r[:, 0:128]
            gv[block_rows(tm, b), lanes] = r[:, 128:256]


def project(attn, w, ma, mb):
    ma[...] = dot(attn[0:256], w[...]).astype(BF16)
    mb[...] = dot(attn[256:512], w[...]).astype(BF16)


def add_first(ma, mb, ra, rb, sa, sb):
    sa[...] = (ma[...].astype(F32) + ra[...].astype(F32)).astype(BF16)
    sb[...] = (mb[...].astype(F32) + rb[...].astype(F32)).astype(BF16)


def add_second(tm, ma, mb, ra, rb, out):
    out[block_rows(tm, 0), :] = (ma[...].astype(F32) + ra[...].astype(F32)).astype(BF16)
    out[block_rows(tm, 1), :] = (mb[...].astype(F32) + rb[...].astype(F32)).astype(BF16)


def swap(x, axis, mask):
    return lax.ppermute(x, axis, [(i, i ^ mask) for i in range(lax.axis_size(axis))])


def side(x):
    pairs = [(i, (i + 1) % 32 if i % 2 else (i - 1) % 32) for i in range(32)]
    return lax.ppermute(x, "tm", pairs)


def bind(f, *args):
    def body(*refs):
        f(*args, *refs)

    return body


def layer(q, k, v, w, up, win, off):
    tm = lax.axis_index("tm").astype(jnp.int32).reshape(1)
    VM = pltpu.VMEM
    hbm = pl.BlockSpec(memory_space=pltpu.HBM)
    kvp, c1s, n1s, x1s, qv, upv, wv = call(
        prep_kv, (off, tm) + tuple(pltpu.with_memory_space_constraint(x, pltpu.HBM) for x in (k, v, q, up, w)),
        [sds((512, 512), BF16), sds((384, 512), BF16), sds((256, 512), BF16), sds((128, 512), BF16),
         sds((512, 256), BF16), sds((512, 1024), BF16), sds((256, 1024), BF16)],
        specs=[SMEM, SMEM] + [hbm] * 5,
        scratch=[VM((512, 256), BF16), VM((512, 256), BF16), pltpu.SemaphoreType.DMA((9,))],
        flops=3e8, nbytes=3e6,
    )
    x1 = swap(x1s, "tm", 2)
    c1 = swap(c1s, "tm", 1)
    n1 = side(n1s)
    qt, gt = call(
        prep_qg, (off, qv, upv, wv), [sds((2, 256, 256), BF16), sds((2, 256, 256), BF16)],
        specs=[SMEM, None, None, None], flops=6e8, nbytes=3e6,
    )
    x2 = swap(call(asm_x2, (kvp, x1), [sds((128, 512), BF16)])[0], "tm", 6)
    near = []
    for which in range(2):
        near.append(
            call(
                bind(fwd_near, which), (off, win, tm, qt, kvp, c1) + ((n1,) if which else ()),
                [sds((4, 768, 256), BF16), sds((4, 512, 128), BF16), sds((256, 256), F32), sds((8, 256), F32)],
                specs=[SMEM] * 3 + [None] * (3 + which),
                scratch=[
                    VM((128, 768), BF16), VM((128, 512), BF16), VM((512, 128), BF16), VM((256, 256), F32),
                    VM((768, 256), F32), VM((512, 128), F32),
                ],
                flops=3e9, nbytes=4e6,
            )
        )
    y1 = swap(call(asm_y1, (kvp, x1, x2), [sds((128, 512), BF16)])[0], "tm", 8)
    y2 = swap(call(asm_y2, (kvp, x1, x2, y1), [sds((128, 512), BF16)])[0], "tm", 24)
    bufs = []
    for mine in (x1, x2, y1, y2):
        bufs += [mine, swap(mine, "tm", 1)]
    pf, attn, stat2 = call(
        fwd_far, (off, qt, gt, near[0][2], near[1][2], near[0][3], near[1][3], *bufs),
        [sds((4, 1024, 128), BF16), sds((512, 256), BF16), sds((16, 512), F32)],
        specs=[SMEM] + [None] * 14,
        scratch=[VM((1024, 128), BF16), VM((128, 1024), BF16), VM((1024, 128), F32), VM((128, 512), BF16)],
        flops=3e9, nbytes=4e6,
    )
    ma, mb = call(project, (attn, wv), [sds((256, 1024), BF16)] * 2, flops=3e8, nbytes=2e6)
    sa, sb = call(
        add_first, (ma, mb, swap(ma, "head", 1), swap(mb, "head", 3)),
        [sds((256, 1024), BF16)] * 2, nbytes=3e6,
    )
    (mixed,) = call(
        add_second, (tm, sa, sb, swap(sa, "head", 3), swap(sb, "head", 1)),
        [sds((512, 1024), BF16)], specs=[SMEM] + [None] * 4, nbytes=3e6,
    )
    ret_s, own_far, dqf = call(
        bwd_far, (qt, gt, stat2, pf, *bufs),
        [sds((512, 512), BF16), sds((512, 512), F32), sds((256, 128), F32)],
        scratch=[VM((1024, 128), BF16), VM((1024, 128), BF16)], flops=4e9, nbytes=5e6,
    )
    ret = swap(ret_s, "tm", 1)
    near_s, own_near, dqn = call(
        bwd_keys, (qt, gt, stat2, kvp, c1, near[0][1], near[1][1]),
        [sds((256, 512), BF16), sds((256, 512), F32), sds((256, 256), F32)],
        flops=4e9, nbytes=5e6,
    )
    near_r = swap(near_s, "tm", 1)

    def back(which, halo, gq_rows, more):
        return call(
            bind(bwd_near, which), (off, tm, qt, gt, stat2, kvp, halo, near[which][0], dqf, dqn, *more),
            [sds((512, 512), F32), sds((256, 512), BF16), sds((gq_rows, 256), BF16)],
            specs=[SMEM] * 2 + [None] * (8 + len(more)),
            scratch=[VM((128, 256), BF16)], flops=4e9, nbytes=4e6,
        )

    own1, hn_s, gq1 = back(1, n1, 256, ())
    own, hc_s, gq = back(0, c1, 512, (own1, own_near, gq1))
    rest, y2s = call(ret_y2, (own_far, ret), [sds((384, 512), F32), sds((128, 512), BF16)])
    y2r = swap(y2s, "tm", 24)
    rest, y1s = call(ret_y1, (rest, y2r), [sds((256, 512), F32), sds((128, 512), BF16)])
    y1r = swap(y1s, "tm", 8)
    rest, x2s = call(ret_x2, (rest, y1r), [sds((128, 512), F32), sds((128, 512), BF16)])
    x2r = swap(x2s, "tm", 6)
    (x1s,) = call(ret_x1, (rest, x2r), [sds((128, 512), BF16)])
    x1r = swap(x1s, "tm", 2)
    hc, hn = swap(hc_s, "tm", 1), side(hn_s)
    (acc,) = call(gather_own, (own, near_r, hc, hn, y2r, y1r, x2r), [sds((512, 512), F32)], nbytes=3e6)
    gk, gv = call(
        finish, (off, tm, acc, x1r), [sds((512, 256), BF16), sds((512, 256), BF16)],
        specs=[SMEM] * 2 + [None] * 2, flops=3e8, nbytes=3e6,
    )
    return mixed, gq, gk, gv


def solution(mesh):
    placed = (P("tm", "head"),) * 3 + (P("head", None), P("tm", None), P("head"), P("head"))
    return jax.shard_map(
        layer,
        mesh=mesh,
        in_specs=placed,
        out_specs=(P("tm", None), P("tm", "head"), P("tm", "head"), P("tm", "head")),
        check_vma=False,
    )
```

time: 83.5 us -> 78 us (0.934)
  starting transfers between devices: 39.3 us -> 28.8 us
  waiting for transfers between devices: 13.8 us -> 19.1 us
  local copies, waits for them, and re-layouts: 2.63 us -> 0.66 us
  Pallas kernels: 26.8 us -> 27.7 us
    ppermute x22 -> x20, starting transfers between devices: 36.8 us -> 26 us  [swap(): lax.ppermute(x, axis, [(i, i ^ mask) for i in range(lax.axis_size(axis))])]
    ppermute x2, waiting for transfers between devices: 0.01 us -> 5.97 us  [side(): return lax.ppermute(x, 'tm', pairs)]
    unnamed x16 -> x6, local copies, waits for them, and re-layouts: 2.63 us -> 0.66 us
    pallas_call x18 -> x21, Pallas kernels: 26.8 us -> 27.7 us  [call(): pl.pallas_call(body, out_shape=outs, grid=(1,), in_specs=in_specs, out_sp...]
    ppermute x22 -> x20, waiting for transfers between devices: 13.8 us -> 13.1 us  [swap(): lax.ppermute(x, axis, [(i, i ^ mask) for i in range(lax.axis_size(axis))])]
  transfers between devices with their start and end apart: 24 -> 22, of which waited for: 8 -> 9; matrix products, arithmetic and copies ran while one was open for 0% -> 0% of each run, Pallas kernels for 28% -> 25%
where the time goes in v1:
time: 78 us; the launch traced here: 77.1 us
  starting transfers between devices  28.8 us (37%)
  Pallas kernels  27.7 us (36%)
  waiting for transfers between devices  19.1 us (24%)
  between operations  0.83 us (1%)
    pallas_call x21, Pallas kernels, call(): pl.pallas_call(body, out_shape=outs, grid=(1,), in_specs=in_specs, out_sp...  27.7 us
    ppermute x20, starting transfers between devices, swap(): lax.ppermute(x, axis, [(i, i ^ mask) for i in range(lax.axis_size(axis))])  26 us
    ppermute x20, waiting for transfers between devices, swap(): lax.ppermute(x, axis, [(i, i ^ mask) for i in range(lax.axis_size(axis))])  13.1 us
    ppermute x2, waiting for transfers between devices, side(): return lax.ppermute(x, 'tm', pairs)  5.97 us
    ppermute x2, starting transfers between devices, side(): return lax.ppermute(x, 'tm', pairs)  2.85 us
  transfers between devices with their start and end apart: 22, of which 9 were waited for; matrix products, arithmetic and copies ran while one was open for 0% of the time, Pallas kernels for 25%

profile of v1, /device:TPU:1, one launch (start us, length us, event | category | flops | bytes accessed | tf_op | source)
XLA Modules:
  0.0 77.1 jit_solution(838235236493709161)
XLA Ops:
  0.6 0.0 copy-start
  0.6 0.6 copy-done
  1.3 2.3 %shard_map.102 = (bf16[512,512]{1,0:T(8,128)(2,1)S(1)}, bf16[384,512]{1,0:T(8,128)(2,1)S(1)}, bf16[256,512]{1,0:T(8,128)(2,1)S(1)}, bf16[128,512]{1,0:T(8,128)(2...) custom-call(s32[4]{0:T(128)S(1)} %copy-done, ...), custom_call_target="tpu_custom_call" | custom-call | flops 300000000 | bytes 3000000 | tf_op jit(solution)/shard_map/pallas_call | solution.py:33
  3.6 2.1 %collective-permute-start.2 = (bf16[128,512]{1,0:T(8,128)(2,1)S(1)}, bf16[128,512]{1,0:T(8,128)(2,1)S(1)}, u32[]{:S(2)}, u32[]{:S(2)}) collective-permute-start(bf16[128,512]{1,0:T(8,128)(2,1)S(1)} %get-tuple-element.60), channel_id=1, source_target_pairs={{0,8},{4,12},{8,0},{12,4},{16,24},{20,28},{24,16},{28,20},{32,40},... | collective-permute-start | bytes 393224 | tf_op jit(solution)/shard_map/ppermute | solution.py:505
  5.7 1.0 %collective-permute-start = (bf16[384,512]{1,0:T(8,128)(2,1)S(1)}, bf16[384,512]{1,0:T(8,128)(2,1)S(1)}, u32[]{:S(2)}, u32[]{:S(2)}) collective-permute-start(bf16[384,512]{1,0:T(8,128)(2,1)S(1)} %get-tuple-element.54), channel_id=1, source_target_pairs={{0,4},{4,0},{8,12},{12,8},{16,20},{20,16},{24,28},{28,24},{32,36},... | collective-permute-start | bytes 1179656 | tf_op jit(solution)/shard_map/ppermute | solution.py:505
  6.7 1.8 %collective-permute-done.2.x1.rest_0_ = bf16[128,512]{1,0:T(8,128)(2,1)S(1)} collective-permute-done((bf16[128,512]{1,0:T(8,128)(2,1)S(1)}, bf16[128,512]{1,0:T(8,128)(2,1)S(1)}, u32[]{:S(2)}, u32[]{:S(2)}) %collective-permute-start.2) | collective-permute-done | bytes 131104 | tf_op jit(solution)/shard_map/ppermute | solution.py:505
  8.5 2.9 %collective-permute-start.4 = (bf16[128,512]{1,0:T(8,128)(2,1)S(1)}, bf16[128,512]{1,0:T(8,128)(2,1)S(1)}, u32[]{:S(2)}, u32[]{:S(2)}) collective-permute-start(bf16[128,512]{1,0:T(8,128)(2,1)S(1)} %shard_map.106), channel_id=1, source_target_pairs={{0,24},{4,28},{8,16},{12,20},{16,8},{20,12},{24,0},{28,4},{32,56},... | collective-permute-start | bytes 393224 | tf_op jit(solution)/shard_map/ppermute | solution.py:505
  11.5 2.4 %collective-permute-done.4.x2.rest_2_ = bf16[128,512]{1,0:T(8,128)(2,1)S(1)} collective-permute-done((bf16[128,512]{1,0:T(8,128)(2,1)S(1)}, bf16[128,512]{1,0:T(8,128)(2,1)S(1)}, u32[]{:S(2)}, u32[]{:S(2)}) %collective-permute-start.4) | collective-permute-done | bytes 131104 | tf_op jit(solution)/shard_map/ppermute | solution.py:505
  13.8 1.6 %collective-permute-start.6 = (bf16[128,512]{1,0:T(8,128)(2,1)S(1)}, bf16[128,512]{1,0:T(8,128)(2,1)S(1)}, u32[]{:S(2)}, u32[]{:S(2)}) collective-permute-start(bf16[128,512]{1,0:T(8,128)(2,1)S(1)} %shard_map.107), channel_id=1, source_target_pairs={{0,32},{4,36},{8,40},{12,44},{16,48},{20,52},{24,56},{28,60},{32,0... | collective-permute-start | bytes 393224 | tf_op jit(solution)/shard_map/ppermute | solution.py:505
  15.4 2.8 %collective-permute-start.1 = (bf16[256,512]{1,0:T(8,128)(2,1)S(1)}, bf16[256,512]{1,0:T(8,128)(2,1)S(1)}, u32[]{:S(2)}, u32[]{:S(2)}) collective-permute-start(bf16[256,512]{1,0:T(8,128)(2,1)S(1)} %get-tuple-element.56), channel_id=1, source_target_pairs={{0,124},{4,8},{8,4},{12,16},{16,12},{20,24},{24,20},{28,32},{32,28... | collective-permute-start | bytes 786440 | tf_op jit(solution)/shard_map/ppermute | solution.py:510
  18.3 1.2 %shard_map.103 = (bf16[2,256,256]{2,1,0:T(8,128)(2,1)S(1)}, bf16[2,256,256]{2,1,0:T(8,128)(2,1)S(1)}) custom-call(s32[4]{0:T(128)S(1)} %copy-done, bf16[512,256]{1,0:T(8,128)(2,1)S(1)} %get-tuple-element.48.q, bf16[512,1024]{1,0:T(8,128)(2,1)S(1)} %get-tuple-element.49.up, bf16[256,1024]{1,0:T(8,128)(2,1)S(1)} %get-tuple-element.50.w), custom_call_target="tpu_custom_call" | custom-call | flops 600000000 | bytes 3000000 | tf_op jit(solution)/shard_map/pallas_call | solution.py:33
  19.5 1.7 %collective-permute-start.3 = (bf16[128,512]{1,0:T(8,128)(2,1)S(1)}, bf16[128,512]{1,0:T(8,128)(2,1)S(1)}, u32[]{:S(2)}, u32[]{:S(2)}) collective-permute-start(bf16[128,512]{1,0:T(8,128)(2,1)S(1)} %collective-permute-done.2.x1.rest_0_), channel_id=1, source_target_pairs={{0,4},{4,0},{8,12},{12,8},{16,20},{20,16},{24,28},{28,24},{32,36},... | collective-permute-start | bytes 393224 | tf_op jit(solution)/shard_map/ppermute | solution.py:505
  21.2 0.1 collective-permute-start.5
  21.3 1.1 %collective-permute-start.8 = (bf16[128,512]{1,0:T(8,128)(2,1)S(1)}, bf16[128,512]{1,0:T(8,128)(2,1)S(1)}, u32[]{:S(2)}, u32[]{:S(2)}) collective-permute-start(bf16[128,512]{1,0:T(8,128)(2,1)S(1)} %shard_map.108), channel_id=1, source_target_pairs={{0,96},{4,100},{8,104},{12,108},{16,112},{20,116},{24,120},{28,124... | collective-permute-start | bytes 393224 | tf_op jit(solution)/shard_map/ppermute | solution.py:505
  22.4 0.0 collective-permute-done.refs_5_.c1.refs_6_
  22.4 2.5 %collective-permute-start.7 = (bf16[128,512]{1,0:T(8,128)(2,1)S(1)}, bf16[128,512]{1,0:T(8,128)(2,1)S(1)}, u32[]{:S(2)}, u32[]{:S(2)}) collective-permute-start(bf16[128,512]{1,0:T(8,128)(2,1)S(1)} %collective-permute-done.6.y1.rest_4_), channel_id=1, source_target_pairs={{0,4},{4,0},{8,12},{12,8},{16,20},{20,16},{24,28},{28,24},{32,36},... | collective-permute-start | bytes 393224 | tf_op jit(solution)/shard_map/ppermute | solution.py:505
  24.9 3.0 %shard_map.104 = (bf16[4,768,256]{2,1,0:T(8,128)(2,1)S(1)}, bf16[4,512,128]{2,1,0:T(8,128)(2,1)S(1)}, f32[256,256]{1,0:T(8,128)S(1)}, f32[8,256]{1,0:T(8,128)S(1)}) custom-call(s32[4]{0:T(128)S(1)} %copy-done, s32[4]{0:T(128)S(1)} %copy-done.2, s32[1]{0:T(128)} %bitcast.tm.refs_2_.refs_1_, bf16[2,256,256]{2,1,0:T(8,128)(2,1)S(1)} %get-tuple-element.51.refs_3_.qt.refs_2_, ...), custom_call_target="tpu_custom_call" | custom-call | flops 3000000000 | bytes 4000000 | tf_op jit(solution)/shard_map/pallas_call | solution.py:33
  27.9 1.9 %collective-permute-done.8.rest_6_ = bf16[128,512]{1,0:T(8,128)(2,1)S(1)} collective-permute-done((bf16[128,512]{1,0:T(8,128)(2,1)S(1)}, bf16[128,512]{1,0:T(8,128)(2,1)S(1)}, u32[]{:S(2)}, u32[]{:S(2)}) %collective-permute-start.8) | collective-permute-done | bytes 131104 | tf_op jit(solution)/shard_map/ppermute | solution.py:505
  29.8 0.5 collective-permute-start.9
  30.3 3.0 %shard_map.105 = (bf16[4,768,256]{2,1,0:T(8,128)(2,1)S(1)}, bf16[4,512,128]{2,1,0:T(8,128)(2,1)S(1)}, f32[256,256]{1,0:T(8,128)S(1)}, f32[8,256]{1,0:T(8,128)S(1)}) custom-call(s32[4]{0:T(128)S(1)} %copy-done, s32[4]{0:T(128)S(1)} %copy-done.2, s32[1]{0:T(128)} %bitcast.tm.refs_2_.refs_1_, bf16[2,256,256]{2,1,0:T(8,128)(2,1)S(1)} %get-tuple-element.51.refs_3_.qt.refs_2_, ...), custom_call_target="tpu_custom_call" | custom-call | flops 3000000000 | bytes 4000000 | tf_op jit(solution)/shard_map/pallas_call | solution.py:33
  33.3 0.0 collective-permute-done.5.rest_3_
  33.3 0.0 collective-permute-done.7.rest_5_
  33.4 3.1 %shard_map.109 = (bf16[4,1024,128]{2,1,0:T(8,128)(2,1)S(1)}, bf16[512,256]{1,0:T(8,128)(2,1)S(1)}, f32[16,512]{1,0:T(8,128)S(1)}) custom-call(s32[4]{0:T(128)S(1)} %copy-done, bf16[2,256,256]{2,1,0:T(8,128)(2,1)S(1)} %get-tuple-element.51.refs_3_.qt.refs_2_, bf16[2,256,256]{2,1,0:T(8,128)(2,1)S(1)} %get-tuple-element.52.gt.refs_3_, ...), custom_call_target="tpu_custom_call" | custom-call | flops 3000000000 | bytes 4000000 | tf_op jit(solution)/shard_map/pallas_call | solution.py:33
  36.5 1.8 %shard_map.113 = (bf16[512,512]{1,0:T(8,128)(2,1)S(1)}, f32[512,512]{1,0:T(8,128)S(1)}, f32[256,128]{1,0:T(8,128)S(1)}) custom-call(bf16[2,256,256]{2,1,0:T(8,128)(2,1)S(1)} %get-tuple-element.51.refs_3_.qt.refs_2_, bf16[2,256,256]{2,1,0:T(8,128)(2,1)S(1)} %get-tuple-element.52.gt.refs_3_, f32[16,512]{1,0:T(8,128)S(1)} %get-tuple-element.66.stat2.refs_4_, ...), custom_call_target="tpu_custom_call" | custom-call | flops 4000000000 | bytes 5000000 | tf_op jit(solution)/shard_map/pallas_call | solution.py:33
  38.3 0.1 collective-permute-start.17
  38.4 0.4 shard_map.110
  38.9 1.7 %collective-permute-start.10 = (bf16[256,1024]{1,0:T(8,128)(2,1)S(1)}, bf16[256,1024]{1,0:T(8,128)(2,1)S(1)}, u32[]{:S(2)}, u32[]{:S(2)}) collective-permute-start(bf16[256,1024]{1,0:T(8,128)(2,1)S(1)} %get-tuple-element.62.ma), channel_id=1, source_target_pairs={{0,1},{1,0},{2,3},{3,2},{4,5},{5,4},{6,7},{7,6},{8,9},{9,8},{10,11... | collective-permute-start | bytes 1572872 | tf_op jit(solution)/shard_map/ppermute | solution.py:505
  40.6 2.2 %collective-permute-start.11 = (bf16[256,1024]{1,0:T(8,128)(2,1)S(1)}, bf16[256,1024]{1,0:T(8,128)(2,1)S(1)}, u32[]{:S(2)}, u32[]{:S(2)}) collective-permute-start(bf16[256,1024]{1,0:T(8,128)(2,1)S(1)} %get-tuple-element.63.mb), channel_id=1, source_target_pairs={{0,3},{1,2},{2,1},{3,0},{4,7},{5,6},{6,5},{7,4},{8,11},{9,10},{10,... | collective-permute-start | bytes 1572872 | tf_op jit(solution)/shard_map/ppermute | solution.py:505
  42.8 0.1 shard_map.117
  42.9 0.5 collective-permute-start.18
  43.5 2.3 %shard_map.114 = (bf16[256,512]{1,0:T(8,128)(2,1)S(1)}, f32[256,512]{1,0:T(8,128)S(1)}, f32[256,256]{1,0:T(8,128)S(1)}) custom-call(bf16[2,256,256]{2,1,0:T(8,128)(2,1)S(1)} %get-tuple-element.51.refs_3_.qt.refs_2_, bf16[2,256,256]{2,1,0:T(8,128)(2,1)S(1)} %get-tuple-element.52.gt.refs_3_, f32[16,512]{1,0:T(8,128)S(1)} %get-tuple-element.66.stat2.refs_4_, ...), custom_call_target="tpu_custom_call" | custom-call | flops 4000000000 | bytes 5000000 | tf_op jit(solution)/shard_map/pallas_call | solution.py:33
  45.8 2.5 %collective-permute-done.18.got.y2 = bf16[128,512]{1,0:T(8,128)(2,1)S(1)} collective-permute-done((bf16[128,512]{1,0:T(8,128)(2,1)S(1)}, bf16[128,512]{1,0:T(8,128)(2,1)S(1)}, u32[]{:S(2)}, u32[]{:S(2)}) %collective-permute-start.18) | collective-permute-done | bytes 131104 | tf_op jit(solution)/shard_map/ppermute | solution.py:505
  48.3 0.1 shard_map.118
  48.4 0.1 collective-permute-start.19
  48.5 3.0 %shard_map.115 = (f32[512,512]{1,0:T(8,128)S(1)}, bf16[256,512]{1,0:T(8,128)(2,1)S(1)}, bf16[256,256]{1,0:T(8,128)(2,1)S(1)}) custom-call(s32[4]{0:T(128)S(1)} %copy-done.1, s32[1]{0:T(128)} %bitcast.tm.refs_2_.refs_1_, bf16[2,256,256]{2,1,0:T(8,128)(2,1)S(1)} %get-tuple-element.51.refs_3_.qt.refs_2_, bf16[2,256,256]{2,1,0:T(8,128)(2,1)S(1)} %get-tuple-element.52.gt.refs_3_, ...), custom_call_target="tpu_custom_call" | custom-call | flops 4000000000 | bytes 4000000 | tf_op jit(solution)/shard_map/pallas_call | solution.py:33
  51.5 0.8 collective-permute-done.10.ra
  52.3 2.2 %collective-permute-done.11.rb = bf16[256,1024]{1,0:T(8,128)(2,1)S(1)} collective-permute-done((bf16[256,1024]{1,0:T(8,128)(2,1)S(1)}, bf16[256,1024]{1,0:T(8,128)(2,1)S(1)}, u32[]{:S(2)}, u32[]{:S(2)}) %collective-permute-start.11) | collective-permute-done | bytes 524320 | tf_op jit(solution)/shard_map/ppermute | solution.py:505
  54.5 0.2 shard_map.111
  54.7 2.5 %collective-permute-start.12 = (bf16[256,1024]{1,0:T(8,128)(2,1)S(1)}, bf16[256,1024]{1,0:T(8,128)(2,1)S(1)}, u32[]{:S(2)}, u32[]{:S(2)}) collective-permute-start(bf16[256,1024]{1,0:T(8,128)(2,1)S(1)} %get-tuple-element.64.ma), channel_id=1, source_target_pairs={{0,3},{1,2},{2,1},{3,0},{4,7},{5,6},{6,5},{7,4},{8,11},{9,10},{10,... | collective-permute-start | bytes 1572872 | tf_op jit(solution)/shard_map/ppermute | solution.py:505
  57.3 3.1 %collective-permute-start.20 = (bf16[128,512]{1,0:T(8,128)(2,1)S(1)}, bf16[128,512]{1,0:T(8,128)(2,1)S(1)}, u32[]{:S(2)}, u32[]{:S(2)}) collective-permute-start(bf16[128,512]{1,0:T(8,128)(2,1)S(1)} %get-tuple-element.88), channel_id=1, source_target_pairs={{0,24},{4,28},{8,16},{12,20},{16,8},{20,12},{24,0},{28,4},{32,56},... | collective-permute-start | bytes 393224 | tf_op jit(solution)/shard_map/ppermute | solution.py:505
  60.4 3.8 %shard_map.116 = (f32[512,512]{1,0:T(8,128)S(1)}, bf16[256,512]{1,0:T(8,128)(2,1)S(1)}, bf16[512,256]{1,0:T(8,128)(2,1)}) custom-call(s32[4]{0:T(128)S(1)} %copy-done.1, s32[1]{0:T(128)} %bitcast.tm.refs_2_.refs_1_, bf16[2,256,256]{2,1,0:T(8,128)(2,1)S(1)} %get-tuple-element.51.refs_3_.qt.refs_2_, bf16[2,256,256]{2,1,0:T(8,128)(2,1)S(1)} %get-tuple-element.52.gt.refs_3_, ...), custom_call_target="tpu_custom_call" | custom-call | flops 4000000000 | bytes 4000000 | tf_op jit(solution)/shard_map/pallas_call | solution.py:33
  64.2 2.2 %collective-permute-start.15 = (bf16[256,512]{1,0:T(8,128)(2,1)S(1)}, bf16[256,512]{1,0:T(8,128)(2,1)S(1)}, u32[]{:S(2)}, u32[]{:S(2)}) collective-permute-start(bf16[256,512]{1,0:T(8,128)(2,1)S(1)} %get-tuple-element.80), channel_id=1, source_target_pairs={{0,4},{4,0},{8,12},{12,8},{16,20},{20,16},{24,28},{28,24},{32,36},... | collective-permute-start | bytes 786440 | tf_op jit(solution)/shard_map/ppermute | solution.py:505
  66.4 1.1 %collective-permute-done.15.hc = bf16[256,512]{1,0:T(8,128)(2,1)S(1)} collective-permute-done((bf16[256,512]{1,0:T(8,128)(2,1)S(1)}, bf16[256,512]{1,0:T(8,128)(2,1)S(1)}, u32[]{:S(2)}, u32[]{:S(2)}) %collective-permute-start.15) | collective-permute-done | bytes 262176 | tf_op jit(solution)/shard_map/ppermute | solution.py:505
  67.5 0.4 collective-permute-done.14.near_r
  67.9 6.0 %collective-permute-done.16.hn = bf16[256,512]{1,0:T(8,128)(2,1)S(1)} collective-permute-done((bf16[256,512]{1,0:T(8,128)(2,1)S(1)}, bf16[256,512]{1,0:T(8,128)(2,1)S(1)}, u32[]{:S(2)}, u32[]{:S(2)}) %collective-permute-start.16) | collective-permute-done | bytes 262176 | tf_op jit(solution)/shard_map/ppermute | solution.py:510
  73.9 0.2 shard_map.120.acc
  74.1 1.8 %shard_map.122 = (bf16[512,256]{1,0:T(8,128)(2,1)}, bf16[512,256]{1,0:T(8,128)(2,1)}) custom-call(s32[4]{0:T(128)S(1)} %copy-done.1, s32[1]{0:T(128)} %bitcast.tm.refs_2_.refs_1_, f32[512,512]{1,0:T(8,128)S(1)} %shard_map.120.acc, bf16[128,512]{1,0:T(8,128)(2,1)S(1)} %collective-permute-done.21.x1), custom_call_target="tpu_custom_call" | custom-call | flops 300000000 | bytes 3000000 | tf_op jit(solution)/shard_map/pallas_call | solution.py:33
  75.9 1.2 %shard_map.112 = bf16[512,1024]{1,0:T(8,128)(2,1)} custom-call(s32[1]{0:T(128)} %bitcast.tm.refs_2_.refs_1_, bf16[256,1024]{1,0:T(8,128)(2,1)S(1)} %get-tuple-element.64.ma, bf16[256,1024]{1,0:T(8,128)(2,1)S(1)} %get-tuple-element.65.mb, bf16[256,1024]{1,0:T(8,128)(2,1)S(1)} %collective-permute-done.12.ra, bf16[256,1024]{1,0:T(8,128)(2,1)S(1)} %collective-permute-done.13.rb), custom_call_target="tpu_custom_call" | custom-call | bytes 3000000 | tf_op jit(solution)/shard_map/pallas_call | solution.py:33
  (23 shorter events, 0.1 us)
Async XLA Ops:
  0.6 0.7 copy-start
  3.6 4.9 %collective-permute-start.2 = (bf16[128,512]{1,0:T(8,128)(2,1)S(1)}, bf16[128,512]{1,0:T(8,128)(2,1)S(1)}, u32[]{:S(2)}, u32[]{:S(2)}) collective-permute-start(bf16[128,512]{1,0:T(8,128)(2,1)S(1)} %get-tuple-element.60), channel_id=1, source_target_pairs={{0,8},{4,12},{8,0},{12,4},{16,24},{20,28},{24,16},{28,20},{32,40},... | collective-permute-start | bytes 393224 | tf_op jit(solution)/shard_map/ppermute | solution.py:505
  5.7 16.7 %collective-permute-start = (bf16[384,512]{1,0:T(8,128)(2,1)S(1)}, bf16[384,512]{1,0:T(8,128)(2,1)S(1)}, u32[]{:S(2)}, u32[]{:S(2)}) collective-permute-start(bf16[384,512]{1,0:T(8,128)(2,1)S(1)} %get-tuple-element.54), channel_id=1, source_target_pairs={{0,4},{4,0},{8,12},{12,8},{16,20},{20,16},{24,28},{28,24},{32,36},... | collective-permute-start | bytes 1179656 | tf_op jit(solution)/shard_map/ppermute | solution.py:505
  8.5 5.3 %collective-permute-start.4 = (bf16[128,512]{1,0:T(8,128)(2,1)S(1)}, bf16[128,512]{1,0:T(8,128)(2,1)S(1)}, u32[]{:S(2)}, u32[]{:S(2)}) collective-permute-start(bf16[128,512]{1,0:T(8,128)(2,1)S(1)} %shard_map.106), channel_id=1, source_target_pairs={{0,24},{4,28},{8,16},{12,20},{16,8},{20,12},{24,0},{28,4},{32,56},... | collective-permute-start | bytes 393224 | tf_op jit(solution)/shard_map/ppermute | solution.py:505
  13.8 7.4 %collective-permute-start.6 = (bf16[128,512]{1,0:T(8,128)(2,1)S(1)}, bf16[128,512]{1,0:T(8,128)(2,1)S(1)}, u32[]{:S(2)}, u32[]{:S(2)}) collective-permute-start(bf16[128,512]{1,0:T(8,128)(2,1)S(1)} %shard_map.107), channel_id=1, source_target_pairs={{0,32},{4,36},{8,40},{12,44},{16,48},{20,52},{24,56},{28,60},{32,0... | collective-permute-start | bytes 393224 | tf_op jit(solution)/shard_map/ppermute | solution.py:505
  15.4 14.9 %collective-permute-start.1 = (bf16[256,512]{1,0:T(8,128)(2,1)S(1)}, bf16[256,512]{1,0:T(8,128)(2,1)S(1)}, u32[]{:S(2)}, u32[]{:S(2)}) collective-permute-start(bf16[256,512]{1,0:T(8,128)(2,1)S(1)} %get-tuple-element.56), channel_id=1, source_target_pairs={{0,124},{4,8},{8,4},{12,16},{16,12},{20,24},{24,20},{28,32},{32,28... | collective-permute-start | bytes 786440 | tf_op jit(solution)/shard_map/ppermute | solution.py:510
  18.3 6.6 %copy-start.2 = (s32[4]{0:T(128)S(1)}, s32[4]{0:T(128)}, u32[]{:S(2)}) copy-start(s32[4]{0:T(128)} %refs_1_.3) | copy-start | bytes 52
  19.5 13.9 %collective-permute-start.3 = (bf16[128,512]{1,0:T(8,128)(2,1)S(1)}, bf16[128,512]{1,0:T(8,128)(2,1)S(1)}, u32[]{:S(2)}, u32[]{:S(2)}) collective-permute-start(bf16[128,512]{1,0:T(8,128)(2,1)S(1)} %collective-permute-done.2.x1.rest_0_), channel_id=1, source_target_pairs={{0,4},{4,0},{8,12},{12,8},{16,20},{20,16},{24,28},{28,24},{32,36},... | collective-permute-start | bytes 393224 | tf_op jit(solution)/shard_map/ppermute | solution.py:505
  21.2 12.1 %collective-permute-start.5 = (bf16[128,512]{1,0:T(8,128)(2,1)S(1)}, bf16[128,512]{1,0:T(8,128)(2,1)S(1)}, u32[]{:S(2)}, u32[]{:S(2)}) collective-permute-start(bf16[128,512]{1,0:T(8,128)(2,1)S(1)} %collective-permute-done.4.x2.rest_2_), channel_id=1, source_target_pairs={{0,4},{4,0},{8,12},{12,8},{16,20},{20,16},{24,28},{28,24},{32,36},... | collective-permute-start | bytes 393224 | tf_op jit(solution)/shard_map/ppermute | solution.py:505
  21.3 8.5 %collective-permute-start.8 = (bf16[128,512]{1,0:T(8,128)(2,1)S(1)}, bf16[128,512]{1,0:T(8,128)(2,1)S(1)}, u32[]{:S(2)}, u32[]{:S(2)}) collective-permute-start(bf16[128,512]{1,0:T(8,128)(2,1)S(1)} %shard_map.108), channel_id=1, source_target_pairs={{0,96},{4,100},{8,104},{12,108},{16,112},{20,116},{24,120},{28,124... | collective-permute-start | bytes 393224 | tf_op jit(solution)/shard_map/ppermute | solution.py:505
  22.4 11.0 %collective-permute-start.7 = (bf16[128,512]{1,0:T(8,128)(2,1)S(1)}, bf16[128,512]{1,0:T(8,128)(2,1)S(1)}, u32[]{:S(2)}, u32[]{:S(2)}) collective-permute-start(bf16[128,512]{1,0:T(8,128)(2,1)S(1)} %collective-permute-done.6.y1.rest_4_), channel_id=1, source_target_pairs={{0,4},{4,0},{8,12},{12,8},{16,20},{20,16},{24,28},{28,24},{32,36},... | collective-permute-start | bytes 393224 | tf_op jit(solution)/shard_map/ppermute | solution.py:505
  29.8 3.5 %collective-permute-start.9 = (bf16[128,512]{1,0:T(8,128)(2,1)S(1)}, bf16[128,512]{1,0:T(8,128)(2,1)S(1)}, u32[]{:S(2)}, u32[]{:S(2)}) collective-permute-start(bf16[128,512]{1,0:T(8,128)(2,1)S(1)} %collective-permute-done.8.rest_6_), channel_id=1, source_target_pairs={{0,4},{4,0},{8,12},{12,8},{16,20},{20,16},{24,28},{28,24},{32,36},... | collective-permute-start | bytes 393224 | tf_op jit(solution)/shard_map/ppermute | solution.py:505
  38.3 4.5 %collective-permute-start.17 = (bf16[512,512]{1,0:T(8,128)(2,1)S(1)}, bf16[512,512]{1,0:T(8,128)(2,1)S(1)}, u32[]{:S(2)}, u32[]{:S(2)}) collective-permute-start(bf16[512,512]{1,0:T(8,128)(2,1)S(1)} %get-tuple-element.83), channel_id=1, source_target_pairs={{0,4},{4,0},{8,12},{12,8},{16,20},{20,16},{24,28},{28,24},{32,36},... | collective-permute-start | bytes 1572872 | tf_op jit(solution)/shard_map/ppermute | solution.py:505
  38.9 13.4 %collective-permute-start.10 = (bf16[256,1024]{1,0:T(8,128)(2,1)S(1)}, bf16[256,1024]{1,0:T(8,128)(2,1)S(1)}, u32[]{:S(2)}, u32[]{:S(2)}) collective-permute-start(bf16[256,1024]{1,0:T(8,128)(2,1)S(1)} %get-tuple-element.62.ma), channel_id=1, source_target_pairs={{0,1},{1,0},{2,3},{3,2},{4,5},{5,4},{6,7},{7,6},{8,9},{9,8},{10,11... | collective-permute-start | bytes 1572872 | tf_op jit(solution)/shard_map/ppermute | solution.py:505
  40.6 13.9 %collective-permute-start.11 = (bf16[256,1024]{1,0:T(8,128)(2,1)S(1)}, bf16[256,1024]{1,0:T(8,128)(2,1)S(1)}, u32[]{:S(2)}, u32[]{:S(2)}) collective-permute-start(bf16[256,1024]{1,0:T(8,128)(2,1)S(1)} %get-tuple-element.63.mb), channel_id=1, source_target_pairs={{0,3},{1,2},{2,1},{3,0},{4,7},{5,6},{6,5},{7,4},{8,11},{9,10},{10,... | collective-permute-start | bytes 1572872 | tf_op jit(solution)/shard_map/ppermute | solution.py:505
  42.9 5.4 %collective-permute-start.18 = (bf16[128,512]{1,0:T(8,128)(2,1)S(1)}, bf16[128,512]{1,0:T(8,128)(2,1)S(1)}, u32[]{:S(2)}, u32[]{:S(2)}) collective-permute-start(bf16[128,512]{1,0:T(8,128)(2,1)S(1)} %get-tuple-element.84), channel_id=1, source_target_pairs={{0,96},{4,100},{8,104},{12,108},{16,112},{20,116},{24,120},{28,124... | collective-permute-start | bytes 393224 | tf_op jit(solution)/shard_map/ppermute | solution.py:505
  43.5 5.0 %copy-start.1 = (s32[4]{0:T(128)S(1)}, s32[4]{0:T(128)}, u32[]{:S(2)}) copy-start(s32[4]{0:T(128)} %off.7) | copy-start | bytes 52
  48.4 8.9 %collective-permute-start.19 = (bf16[128,512]{1,0:T(8,128)(2,1)S(1)}, bf16[128,512]{1,0:T(8,128)(2,1)S(1)}, u32[]{:S(2)}, u32[]{:S(2)}) collective-permute-start(bf16[128,512]{1,0:T(8,128)(2,1)S(1)} %get-tuple-element.86), channel_id=1, source_target_pairs={{0,32},{4,36},{8,40},{12,44},{16,48},{20,52},{24,56},{28,60},{32,0... | collective-permute-start | bytes 393224 | tf_op jit(solution)/shard_map/ppermute | solution.py:505
  54.7 21.2 %collective-permute-start.12 = (bf16[256,1024]{1,0:T(8,128)(2,1)S(1)}, bf16[256,1024]{1,0:T(8,128)(2,1)S(1)}, u32[]{:S(2)}, u32[]{:S(2)}) collective-permute-start(bf16[256,1024]{1,0:T(8,128)(2,1)S(1)} %get-tuple-element.64.ma), channel_id=1, source_target_pairs={{0,3},{1,2},{2,1},{3,0},{4,7},{5,6},{6,5},{7,4},{8,11},{9,10},{10,... | collective-permute-start | bytes 1572872 | tf_op jit(solution)/shard_map/ppermute | solution.py:505
  57.3 18.6 %collective-permute-start.13 = (bf16[256,1024]{1,0:T(8,128)(2,1)S(1)}, bf16[256,1024]{1,0:T(8,128)(2,1)S(1)}, u32[]{:S(2)}, u32[]{:S(2)}) collective-permute-start(bf16[256,1024]{1,0:T(8,128)(2,1)S(1)} %get-tuple-element.65.mb), channel_id=1, source_target_pairs={{0,1},{1,0},{2,3},{3,2},{4,5},{5,4},{6,7},{7,6},{8,9},{9,8},{10,11... | collective-permute-start | bytes 1572872 | tf_op jit(solution)/shard_map/ppermute | solution.py:505
  57.3 9.0 %collective-permute-start.20 = (bf16[128,512]{1,0:T(8,128)(2,1)S(1)}, bf16[128,512]{1,0:T(8,128)(2,1)S(1)}, u32[]{:S(2)}, u32[]{:S(2)}) collective-permute-start(bf16[128,512]{1,0:T(8,128)(2,1)S(1)} %get-tuple-element.88), channel_id=1, source_target_pairs={{0,24},{4,28},{8,16},{12,20},{16,8},{20,12},{24,0},{28,4},{32,56},... | collective-permute-start | bytes 393224 | tf_op jit(solution)/shard_map/ppermute | solution.py:505
  64.2 3.4 %collective-permute-start.15 = (bf16[256,512]{1,0:T(8,128)(2,1)S(1)}, bf16[256,512]{1,0:T(8,128)(2,1)S(1)}, u32[]{:S(2)}, u32[]{:S(2)}) collective-permute-start(bf16[256,512]{1,0:T(8,128)(2,1)S(1)} %get-tuple-element.80), channel_id=1, source_target_pairs={{0,4},{4,0},{8,12},{12,8},{16,20},{20,16},{24,28},{28,24},{32,36},... | collective-permute-start | bytes 786440 | tf_op jit(solution)/shard_map/ppermute | solution.py:505
  66.4 1.5 %collective-permute-start.14 = (bf16[256,512]{1,0:T(8,128)(2,1)S(1)}, bf16[256,512]{1,0:T(8,128)(2,1)S(1)}, u32[]{:S(2)}, u32[]{:S(2)}) collective-permute-start(bf16[256,512]{1,0:T(8,128)(2,1)S(1)} %get-tuple-element.79), channel_id=1, source_target_pairs={{0,4},{4,0},{8,12},{12,8},{16,20},{20,16},{24,28},{28,24},{32,36},... | collective-permute-start | bytes 786440 | tf_op jit(solution)/shard_map/ppermute | solution.py:505
  66.4 7.5 %collective-permute-start.16 = (bf16[256,512]{1,0:T(8,128)(2,1)S(1)}, bf16[256,512]{1,0:T(8,128)(2,1)S(1)}, u32[]{:S(2)}, u32[]{:S(2)}) collective-permute-start(bf16[256,512]{1,0:T(8,128)(2,1)S(1)} %get-tuple-element.81), channel_id=1, source_target_pairs={{0,124},{4,8},{8,4},{12,16},{16,12},{20,24},{24,20},{28,32},{32,28... | collective-permute-start | bytes 786440 | tf_op jit(solution)/shard_map/ppermute | solution.py:510
  67.5 6.6 %collective-permute-start.21 = (bf16[128,512]{1,0:T(8,128)(2,1)S(1)}, bf16[128,512]{1,0:T(8,128)(2,1)S(1)}, u32[]{:S(2)}, u32[]{:S(2)}) collective-permute-start(bf16[128,512]{1,0:T(8,128)(2,1)S(1)} %shard_map.121), channel_id=1, source_target_pairs={{0,8},{4,12},{8,0},{12,4},{16,24},{20,28},{24,16},{28,20},{32,40},... | collective-permute-start | bytes 393224 | tf_op jit(solution)/shard_map/ppermute | solution.py:505

commit v2 on v1

--- a/solution.py
+++ b/solution.py
@@ -102,7 +102,7 @@
     return pl.ds(pl.multiple_of(256 * block, 256), 256)
 
 
-def prep_kv(off, tm, k, v, q, up, w, kvp, c1, n1, x1, qv, upv, wv, kb, vb, sem):
+def prep_kv(off, tm, k, v, q, up, w, kvp, c1, n1, x1, x2, qv, upv, wv, kb, vb, sem):
     copies = []
     for src, dst in ((k, kb), (v, vb), (q, qv), (up, upv)):
         for which in range(2):
@@ -128,6 +128,8 @@
             ).astype(BF16)
     x1[0:64] = kvp[0:64]
     x1[64:128] = kvp[256:320]
+    x2[0:32] = kvp[0:32]
+    x2[32:64] = kvp[256:288]
     c1[...] = kvp[0:384]
     n1[...] = kvp[256:512]
     for c in copies[4:]:
@@ -148,25 +150,33 @@
             gt[b, hs] = r[64:128]
 
 
-def pack_rows(pieces):
-    return jnp.concatenate([p.astype(F32) for p in pieces], axis=0).astype(BF16)
-
-
-def asm_x2(kvp, x1, out):
-    out[...] = pack_rows([kvp[0:32], kvp[256:288], x1[0:32], x1[64:96]])
-
-
-def asm_y1(kvp, x1, x2, out):
-    out[...] = pack_rows(
-        [kvp[0:16], kvp[256:272], x1[0:16], x1[64:80]] + [x2[32 * j : 32 * j + 16] for j in range(4)]
-    )
-
-
-def asm_y2(kvp, x1, x2, y1, out):
-    heads = [kvp[0:16], kvp[256:272], x1[0:16], x1[64:80]]
-    heads += [x2[32 * j : 32 * j + 16] for j in range(4)]
-    heads += [y1[16 * j : 16 * j + 16] for j in range(8)]
-    out[...] = jnp.concatenate([h.astype(F32)[0:8] for h in heads], axis=0).astype(BF16)
+def asm_y(kvp, x1, x2a, x2b, y1, y2, both):
+    heads = [kvp[0:16], kvp[256:272], x1[0:16], x1[64:80], x2a[0:16], x2a[32:48], x2b[0:16], x2b[32:48]]
+    heads = [h.astype(F32) for h in heads]
+    y1[...] = jnp.concatenate(heads, axis=0).astype(BF16)
+    y2[...] = jnp.concatenate([h[0:8] for h in heads], axis=0).astype(BF16)
+    stack(x1, x2a, x2b, both)
+
+
+def stack(*refs):
+    out, at = refs[-1], 0
+    for ref in refs[:-1]:
+        out[at : at + ref.shape[0]] = ref[...]
+        at += ref.shape[0]
+
+
+def beside(left, right, out):
+    out[:, 0 : left.shape[1]] = left[...]
+    out[:, left.shape[1] :] = right[...]
+
+
+def far_rows(bufs, lanes):
+    mine_x, other_x, mine_y, other_y = bufs
+    out = []
+    for mine, other in ((mine_x, other_x), (mine_y, other_y)):
+        for half in (slice(0, 128), slice(128, 256)):
+            out += [mine[half, lanes], other[half, lanes]]
+    return jnp.concatenate(out, axis=0)
 
 
 def near_count():
@@ -269,7 +279,7 @@
 
 
 def fwd_far(off, qt, gt, acc0, acc1, st0, st1, *rest):
-    bufs, (pf, attn, stat2, kf, vft, mult, at) = rest[:8], rest[8:]
+    bufs, (pf, attn, stat2, kf, vft, mult, at) = rest[:4], rest[4:]
     for level in range(2, 6):
         n = 256 >> level
         piece = far_count(level)
@@ -277,9 +287,8 @@
             mult[256 * (level - 2) + n * j : 256 * (level - 2) + n * j + n] = piece
     for pair in range(2):
         lo, hi = pair_slices(pair)
-        for j, buf in enumerate(bufs):
-            kf[128 * j : 128 * j + 128] = buf[:, lo]
-        vft[...] = transposed(jnp.concatenate([buf[:, hi] for buf in bufs], axis=0))
+        kf[...] = far_rows(bufs, lo)
+        vft[...] = transposed(far_rows(bufs, hi))
         for a in range(2):
             vh = slice(64 * a, 64 * a + 64)
             h = 2 * pair + a
@@ -314,12 +323,11 @@
 
 
 def bwd_far(qt, gt, stat2, pf, *rest):
-    bufs, (ret, own_far, dq, kx, vx) = rest[:8], rest[8:]
+    bufs, (ret, own_far, dq, kx, vx) = rest[:4], rest[4:]
     for pair in range(2):
         lo, hi = pair_slices(pair)
-        for j, buf in enumerate(bufs):
-            kx[128 * j : 128 * j + 128] = buf[:, lo]
-            vx[128 * j : 128 * j + 128] = buf[:, hi]
+        kx[...] = far_rows(bufs, lo)
+        vx[...] = far_rows(bufs, hi)
         kt = transposed(kx[...])
         grads, scaled_q, scaled_g = [], [], []
         for a in range(2):
@@ -420,58 +428,40 @@
             gq[block_rows(tm, 0), 128 * pair : 128 * pair + 128] = r
 
 
-def ret_y2(own_far, ret, rest, send):
+def ret_y(own_far, ret, rest, y1, y2a, y2b):
     total = own_far[...] + ret[...].astype(F32)
-    rest[...] = total[0:384]
-    send[...] = total[384:512].astype(BF16)
-
-
-def ret_y1(rest, got, left, send):
-    y2 = got[...].astype(F32)
-    left[...] = rest[0:256]
-    for j in range(2):
-        left[64 * j : 64 * j + 8] += y2[16 + 8 * j : 24 + 8 * j]
-    for j in range(4):
-        left[128 + 32 * j : 136 + 32 * j] += y2[32 + 8 * j : 40 + 8 * j]
-    zero = jnp.zeros((8, 512), F32)
-    extra = []
-    for j in range(8):
-        extra += [y2[64 + 8 * j : 72 + 8 * j], zero]
-    send[...] = (rest[256:384] + jnp.concatenate(extra, axis=0)).astype(BF16)
-
-
-def ret_x2(rest, got, left, send):
-    y1 = got[...].astype(F32)
-    left[...] = rest[0:128]
-    for j in range(2):
-        left[64 * j : 64 * j + 16] += y1[32 + 16 * j : 48 + 16 * j]
-    zero = jnp.zeros((16, 512), F32)
-    extra = []
-    for j in range(4):
-        extra += [y1[64 + 16 * j : 80 + 16 * j], zero]
-    send[...] = (rest[128:256] + jnp.concatenate(extra, axis=0)).astype(BF16)
-
-
-def ret_x1(rest, got, send):
-    x2 = got[...].astype(F32)
-    zero = jnp.zeros((32, 512), F32)
-    extra = [x2[64:96], zero, x2[96:128], zero]
-    send[...] = (rest[...] + jnp.concatenate(extra, axis=0)).astype(BF16)
-
-
-def gather_own(own, near_r, hc, hn, y2, y1, x2, acc):
+    rest[...] = total[0:256]
+    y1[...] = total[256:384].astype(BF16)
+    y2a[...] = total[384:448].astype(BF16)
+    y2b[...] = total[448:512].astype(BF16)
+
+
+def ret_x(rest, y1, y2a, y2b, x1, x2a, x2b):
+    deep = y1[...].astype(F32)
+    deeper = y2a[...].astype(F32) + y2b[...].astype(F32)
+    total = []
+    for j, at in enumerate((0, 64, 128, 160, 192, 224)):
+        size = 64 if at < 128 else 32
+        top = deep[32 + 16 * j : 48 + 16 * j]
+        head = rest[at : at + 16] + top
+        total += [head[0:8] + deeper[16 + 8 * j : 24 + 8 * j], head[8:16], rest[at + 16 : at + size]]
+    x1[...] = jnp.concatenate(total[0:6], axis=0).astype(BF16)
+    x2a[...] = jnp.concatenate(total[6:12], axis=0).astype(BF16)
+    x2b[...] = jnp.concatenate(total[12:18], axis=0).astype(BF16)
+
+
+def gather_own(own, near_r, hc, hn, y1, y2a, y2b, acc):
     acc[...] = own[...]
     acc[0:256] += hc[...].astype(F32)
     acc[256:512] += hn[...].astype(F32)
     for b in range(2):
         at = 256 * b
         acc[at : at + 128] += near_r[128 * b : 128 * b + 128].astype(F32)
-        acc[at : at + 32] += x2[32 * b : 32 * b + 32].astype(F32)
         acc[at : at + 16] += y1[16 * b : 16 * b + 16].astype(F32)
-        acc[at : at + 8] += y2[0:16].astype(F32)[8 * b : 8 * b + 8]
-
-
-def finish(off, tm, acc, x1, gk, gv):
+        acc[at : at + 8] += (y2a[0:16].astype(F32) + y2b[0:16].astype(F32))[8 * b : 8 * b + 8]
+
+
+def finish(off, tm, acc, x1, x2a, x2b, gk, gv):
     keep = lane_first(256, 256)
     for pair in range(2):
         first, second = from_depth(off[2 * pair]), from_depth(off[2 * pair + 1])
@@ -480,25 +470,19 @@
         for b in range(2):
             at = 256 * b
             head = acc[at : at + 64, cols] + x1[64 * b : 64 * b + 64, cols].astype(F32)
-            x = jnp.concatenate([head, acc[at + 64 : at + 256, cols]], axis=0).astype(BF16)
+            deep = x2a[32 * b : 32 * b + 32, cols].astype(F32) + x2b[32 * b : 32 * b + 32, cols].astype(F32)
+            x = jnp.concatenate([head[0:32] + deep, head[32:64], acc[at + 64 : at + 256, cols]], axis=0).astype(BF16)
             r = jnp.where(keep, dot(first, x), dot(second, x)).astype(BF16)
             gk[block_rows(tm, b), lanes] = r[:, 0:128]
             gv[block_rows(tm, b), lanes] = r[:, 128:256]
 
 
-def project(attn, w, ma, mb):
-    ma[...] = dot(attn[0:256], w[...]).astype(BF16)
-    mb[...] = dot(attn[256:512], w[...]).astype(BF16)
-
-
-def add_first(ma, mb, ra, rb, sa, sb):
-    sa[...] = (ma[...].astype(F32) + ra[...].astype(F32)).astype(BF16)
-    sb[...] = (mb[...].astype(F32) + rb[...].astype(F32)).astype(BF16)
-
-
-def add_second(tm, ma, mb, ra, rb, out):
-    out[block_rows(tm, 0), :] = (ma[...].astype(F32) + ra[...].astype(F32)).astype(BF16)
-    out[block_rows(tm, 1), :] = (mb[...].astype(F32) + rb[...].astype(F32)).astype(BF16)
+def project(tm, a01, a23, w02, w13, out):
+    w = jnp.concatenate([w02[0:256], w13[0:256], w02[256:512], w13[256:512]], axis=0)
+    for b in range(2):
+        bs = slice(256 * b, 256 * b + 256)
+        a = jnp.concatenate([a01[bs], a23[bs]], axis=1)
+        out[block_rows(tm, b), :] = dot(a, w).astype(BF16)
 
 
 def swap(x, axis, mask):
@@ -506,7 +490,7 @@
 
 
 def side(x):
-    pairs = [(i, (i + 1) % 32 if i % 2 else (i - 1) % 32) for i in range(32)]
+    pairs = [(i, i + 1 if i % 2 else i - 1) for i in range(1, lax.axis_size("tm") - 1)]
     return lax.ppermute(x, "tm", pairs)
 
 
@@ -521,22 +505,25 @@
     tm = lax.axis_index("tm").astype(jnp.int32).reshape(1)
     VM = pltpu.VMEM
     hbm = pl.BlockSpec(memory_space=pltpu.HBM)
-    kvp, c1s, n1s, x1s, qv, upv, wv = call(
+    rows = lambda n: sds((n, 512), BF16)
+    kvp, c1s, n1s, x1s, x2s, qv, upv, wv = call(
         prep_kv, (off, tm) + tuple(pltpu.with_memory_space_constraint(x, pltpu.HBM) for x in (k, v, q, up, w)),
-        [sds((512, 512), BF16), sds((384, 512), BF16), sds((256, 512), BF16), sds((128, 512), BF16),
+        [rows(512), rows(384), rows(256), rows(128), rows(64),
          sds((512, 256), BF16), sds((512, 1024), BF16), sds((256, 1024), BF16)],
         specs=[SMEM, SMEM] + [hbm] * 5,
         scratch=[VM((512, 256), BF16), VM((512, 256), BF16), pltpu.SemaphoreType.DMA((9,))],
         flops=3e8, nbytes=3e6,
     )
-    x1 = swap(x1s, "tm", 2)
+    x1, x2a, x2b = swap(x1s, "tm", 2), swap(x2s, "tm", 4), swap(x2s, "tm", 6)
     c1 = swap(c1s, "tm", 1)
     n1 = side(n1s)
+    w1 = swap(wv, "head", 3)
+    (w02,) = call(stack, (wv, w1), [sds((512, 1024), BF16)])
+    w13 = swap(w02, "head", 1)
     qt, gt = call(
         prep_qg, (off, qv, upv, wv), [sds((2, 256, 256), BF16), sds((2, 256, 256), BF16)],
-        specs=[SMEM, None, None, None], flops=6e8, nbytes=3e6,
-    )
-    x2 = swap(call(asm_x2, (kvp, x1), [sds((128, 512), BF16)])[0], "tm", 6)
+        specs=[SMEM] + [None] * 3, flops=6e8, nbytes=3e6,
+    )
     near = []
     for which in range(2):
         near.append(
@@ -551,26 +538,23 @@
                 flops=3e9, nbytes=4e6,
             )
         )
-    y1 = swap(call(asm_y1, (kvp, x1, x2), [sds((128, 512), BF16)])[0], "tm", 8)
-    y2 = swap(call(asm_y2, (kvp, x1, x2, y1), [sds((128, 512), BF16)])[0], "tm", 24)
-    bufs = []
-    for mine in (x1, x2, y1, y2):
-        bufs += [mine, swap(mine, "tm", 1)]
+    y1s, y2s, mine_x = call(asm_y, (kvp, x1, x2a, x2b), [rows(128), rows(64), rows(256)])
+    y1, y2a, y2b = swap(y1s, "tm", 8), swap(y2s, "tm", 16), swap(y2s, "tm", 24)
+    (mine_y,) = call(stack, (y1, y2a, y2b), [rows(256)])
+    bufs = (mine_x, swap(mine_x, "tm", 1), mine_y, swap(mine_y, "tm", 1))
     pf, attn, stat2 = call(
         fwd_far, (off, qt, gt, near[0][2], near[1][2], near[0][3], near[1][3], *bufs),
         [sds((4, 1024, 128), BF16), sds((512, 256), BF16), sds((16, 512), F32)],
-        specs=[SMEM] + [None] * 14,
+        specs=[SMEM] + [None] * 10,
         scratch=[VM((1024, 128), BF16), VM((128, 1024), BF16), VM((1024, 128), F32), VM((128, 512), BF16)],
         flops=3e9, nbytes=4e6,
     )
-    ma, mb = call(project, (attn, wv), [sds((256, 1024), BF16)] * 2, flops=3e8, nbytes=2e6)
-    sa, sb = call(
-        add_first, (ma, mb, swap(ma, "head", 1), swap(mb, "head", 3)),
-        [sds((256, 1024), BF16)] * 2, nbytes=3e6,
-    )
+    a1 = swap(attn, "head", 1)
+    (a01,) = call(beside, (attn, a1), [rows(512)])
+    a23 = swap(a01, "head", 3)
     (mixed,) = call(
-        add_second, (tm, sa, sb, swap(sa, "head", 3), swap(sb, "head", 1)),
-        [sds((512, 1024), BF16)], specs=[SMEM] + [None] * 4, nbytes=3e6,
+        project, (tm, a01, a23, w02, w13), [sds((512, 1024), BF16)],
+        specs=[SMEM] + [None] * 4, flops=1e9, nbytes=4e6,
     )
     ret_s, own_far, dqf = call(
         bwd_far, (qt, gt, stat2, pf, *bufs),
@@ -595,19 +579,15 @@
 
     own1, hn_s, gq1 = back(1, n1, 256, ())
     own, hc_s, gq = back(0, c1, 512, (own1, own_near, gq1))
-    rest, y2s = call(ret_y2, (own_far, ret), [sds((384, 512), F32), sds((128, 512), BF16)])
-    y2r = swap(y2s, "tm", 24)
-    rest, y1s = call(ret_y1, (rest, y2r), [sds((256, 512), F32), sds((128, 512), BF16)])
-    y1r = swap(y1s, "tm", 8)
-    rest, x2s = call(ret_x2, (rest, y1r), [sds((128, 512), F32), sds((128, 512), BF16)])
-    x2r = swap(x2s, "tm", 6)
-    (x1s,) = call(ret_x1, (rest, x2r), [sds((128, 512), BF16)])
-    x1r = swap(x1s, "tm", 2)
+    rest, y1s, y2as, y2bs = call(ret_y, (own_far, ret), [sds((256, 512), F32), rows(128), rows(64), rows(64)])
+    yr = [swap(x, "tm", m) for x, m in ((y1s, 8), (y2as, 16), (y2bs, 24))]
+    x1s, x2as, x2bs = call(ret_x, (rest, *yr), [rows(128), rows(64), rows(64)])
+    xr = [swap(x, "tm", m) for x, m in ((x1s, 2), (x2as, 4), (x2bs, 6))]
     hc, hn = swap(hc_s, "tm", 1), side(hn_s)
-    (acc,) = call(gather_own, (own, near_r, hc, hn, y2r, y1r, x2r), [sds((512, 512), F32)], nbytes=3e6)
+    (acc,) = call(gather_own, (own, near_r, hc, hn, *yr), [sds((512, 512), F32)], nbytes=3e6)
     gk, gv = call(
-        finish, (off, tm, acc, x1r), [sds((512, 256), BF16), sds((512, 256), BF16)],
-        specs=[SMEM] * 2 + [None] * 2, flops=3e8, nbytes=3e6,
+        finish, (off, tm, acc, *xr), [sds((512, 256), BF16), sds((512, 256), BF16)],
+        specs=[SMEM] * 2 + [None] * 4, flops=3e8, nbytes=3e6,
     )
     return mixed, gq, gk, gv
 

time: 78 us -> 82.4 us (1.056)
  starting transfers between devices: 28.8 us -> 35.4 us
  waiting for transfers between devices: 19.1 us -> 17 us
    ppermute x20 -> x22, starting transfers between devices: 26 us -> 30.6 us  [swap(): lax.ppermute(x, axis, [(i, i ^ mask) for i in range(lax.axis_size(axis))])]
    ppermute x20 -> x22, waiting for transfers between devices: 13.1 us -> 10.7 us  [swap(): lax.ppermute(x, axis, [(i, i ^ mask) for i in range(lax.axis_size(axis))])]
    ppermute x2, starting transfers between devices: 2.85 us -> 4.79 us  [side(): return lax.ppermute(x, 'tm', pairs)]
    pallas_call x21 -> x18, Pallas kernels: 27.7 us -> 28.2 us  [call(): pl.pallas_call(body, out_shape=outs, grid=(1,), in_specs=in_specs, out_sp...]
  transfers between devices with their start and end apart: 22 -> 24, of which waited for: 9 -> 7; matrix products, arithmetic and copies ran while one was open for 0% -> 0% of each run, Pallas kernels for 25% -> 29%
where the time goes in v2:
time: 82.4 us; the launch traced here: 82.1 us
  starting transfers between devices  35.4 us (43%)
  Pallas kernels  28.2 us (34%)
  waiting for transfers between devices  17 us (21%)
  between operations  0.87 us (1%)
    ppermute x22, starting transfers between devices, swap(): lax.ppermute(x, axis, [(i, i ^ mask) for i in range(lax.axis_size(axis))])  30.6 us
    pallas_call x18, Pallas kernels, call(): pl.pallas_call(body, out_shape=outs, grid=(1,), in_specs=in_specs, out_sp...  28.2 us
    ppermute x22, waiting for transfers between devices, swap(): lax.ppermute(x, axis, [(i, i ^ mask) for i in range(lax.axis_size(axis))])  10.7 us
    ppermute x2, waiting for transfers between devices, side(): return lax.ppermute(x, 'tm', pairs)  6.25 us
    ppermute x2, starting transfers between devices, side(): return lax.ppermute(x, 'tm', pairs)  4.79 us
  transfers between devices with their start and end apart: 24, of which 7 were waited for; matrix products, arithmetic and copies ran while one was open for 0% of the time, Pallas kernels for 29%

profile of v2, /device:TPU:1, one launch (start us, length us, event | category | flops | bytes accessed | tf_op | source)
XLA Modules:
  0.0 82.1 jit_solution(7344408493883705643)
XLA Ops:
  0.6 0.6 copy-done
  1.3 2.3 %shard_map.102 = (bf16[512,512]{1,0:T(8,128)(2,1)S(1)}, bf16[384,512]{1,0:T(8,128)(2,1)S(1)}, bf16[256,512]{1,0:T(8,128)(2,1)S(1)}, bf16[128,512]{1,0:T(8,128)(2...) custom-call(s32[4]{0:T(128)S(1)} %copy-done, ...), custom_call_target="tpu_custom_call" | custom-call | flops 300000000 | bytes 3000000 | tf_op jit(solution)/shard_map/pallas_call | solution.py:33
  3.6 1.5 %collective-permute-start = (bf16[384,512]{1,0:T(8,128)(2,1)S(1)}, bf16[384,512]{1,0:T(8,128)(2,1)S(1)}, u32[]{:S(2)}, u32[]{:S(2)}) collective-permute-start(bf16[384,512]{1,0:T(8,128)(2,1)S(1)} %get-tuple-element.55), channel_id=1, source_target_pairs={{0,4},{4,0},{8,12},{12,8},{16,20},{20,16},{24,28},{28,24},{32,36},... | collective-permute-start | bytes 1179656 | tf_op jit(solution)/shard_map/ppermute | solution.py:489
  5.1 1.3 %collective-permute-start.2 = (bf16[128,512]{1,0:T(8,128)(2,1)S(1)}, bf16[128,512]{1,0:T(8,128)(2,1)S(1)}, u32[]{:S(2)}, u32[]{:S(2)}) collective-permute-start(bf16[128,512]{1,0:T(8,128)(2,1)S(1)} %get-tuple-element.61), channel_id=1, source_target_pairs={{0,8},{4,12},{8,0},{12,4},{16,24},{20,28},{24,16},{28,20},{32,40},... | collective-permute-start | bytes 393224 | tf_op jit(solution)/shard_map/ppermute | solution.py:489
  6.4 2.5 %collective-permute-start.3 = (bf16[64,512]{1,0:T(8,128)(2,1)S(1)}, bf16[64,512]{1,0:T(8,128)(2,1)S(1)}, u32[]{:S(2)}, u32[]{:S(2)}) collective-permute-start(bf16[64,512]{1,0:T(8,128)(2,1)S(1)} %get-tuple-element.62), channel_id=1, source_target_pairs={{0,16},{4,20},{8,24},{12,28},{16,0},{20,4},{24,8},{28,12},{32,48},... | collective-permute-start | bytes 196616 | tf_op jit(solution)/shard_map/ppermute | solution.py:489
  8.9 0.1 collective-permute-start.4
  8.9 4.8 %collective-permute-done.3.x2a = bf16[64,512]{1,0:T(8,128)(2,1)S(1)} collective-permute-done((bf16[64,512]{1,0:T(8,128)(2,1)S(1)}, bf16[64,512]{1,0:T(8,128)(2,1)S(1)}, u32[]{:S(2)}, u32[]{:S(2)}) %collective-permute-start.3) | collective-permute-done | bytes 65568 | tf_op jit(solution)/shard_map/ppermute | solution.py:489
  13.8 1.2 %collective-permute-done.4.x2b = bf16[64,512]{1,0:T(8,128)(2,1)S(1)} collective-permute-done((bf16[64,512]{1,0:T(8,128)(2,1)S(1)}, bf16[64,512]{1,0:T(8,128)(2,1)S(1)}, u32[]{:S(2)}, u32[]{:S(2)}) %collective-permute-start.4) | collective-permute-done | bytes 65568 | tf_op jit(solution)/shard_map/ppermute | solution.py:489
  14.9 0.0 collective-permute-done.2.x1
  15.0 0.0 copy-start.2
  15.0 1.4 %collective-permute-start.6 = (bf16[128,512]{1,0:T(8,128)(2,1)S(1)}, bf16[128,512]{1,0:T(8,128)(2,1)S(1)}, u32[]{:S(2)}, u32[]{:S(2)}) collective-permute-start(bf16[128,512]{1,0:T(8,128)(2,1)S(1)} %get-tuple-element.64), channel_id=1, source_target_pairs={{0,32},{4,36},{8,40},{12,44},{16,48},{20,52},{24,56},{28,60},{32,0... | collective-permute-start | bytes 393224 | tf_op jit(solution)/shard_map/ppermute | solution.py:489
  16.4 2.6 %collective-permute-start.7 = (bf16[64,512]{1,0:T(8,128)(2,1)S(1)}, bf16[64,512]{1,0:T(8,128)(2,1)S(1)}, u32[]{:S(2)}, u32[]{:S(2)}) collective-permute-start(bf16[64,512]{1,0:T(8,128)(2,1)S(1)} %get-tuple-element.65), channel_id=1, source_target_pairs={{0,64},{4,68},{8,72},{12,76},{16,80},{20,84},{24,88},{28,92},{32,9... | collective-permute-start | bytes 196616 | tf_op jit(solution)/shard_map/ppermute | solution.py:489
  19.0 0.0 collective-permute-start.8
  19.0 3.8 %collective-permute-start.12 = (bf16[256,1024]{1,0:T(8,128)(2,1)S(1)}, bf16[256,1024]{1,0:T(8,128)(2,1)S(1)}, u32[]{:S(2)}, u32[]{:S(2)}) collective-permute-start(bf16[256,1024]{1,0:T(8,128)(2,1)S(1)} %get-tuple-element.51.w.refs_0_), channel_id=1, source_target_pairs={{0,3},{1,2},{2,1},{3,0},{4,7},{5,6},{6,5},{7,4},{8,11},{9,10},{10,... | collective-permute-start | bytes 1572872 | tf_op jit(solution)/shard_map/ppermute | solution.py:489
  22.8 1.2 %shard_map.103 = (bf16[2,256,256]{2,1,0:T(8,128)(2,1)S(1)}, bf16[2,256,256]{2,1,0:T(8,128)(2,1)S(1)}) custom-call(s32[4]{0:T(128)S(1)} %copy-done.1, bf16[512,256]{1,0:T(8,128)(2,1)S(1)} %get-tuple-element.49.q, bf16[512,1024]{1,0:T(8,128)(2,1)S(1)} %get-tuple-element.50.up, bf16[256,1024]{1,0:T(8,128)(2,1)S(1)} %get-tuple-element.51.w.refs_0_), custom_call_target="tpu_custom_call" | custom-call | flops 600000000 | bytes 3000000 | tf_op jit(solution)/shard_map/pallas_call | solution.py:33
  24.0 2.9 %collective-permute-start.1 = (bf16[256,512]{1,0:T(8,128)(2,1)S(1)}, bf16[256,512]{1,0:T(8,128)(2,1)S(1)}, u32[]{:S(2)}, u32[]{:S(2)}) collective-permute-start(bf16[256,512]{1,0:T(8,128)(2,1)S(1)} %get-tuple-element.57), channel_id=1, source_target_pairs={{4,8},{8,4},{12,16},{16,12},{20,24},{24,20},{28,32},{32,28},{36,40... | collective-permute-start | bytes 786440 | tf_op jit(solution)/shard_map/ppermute | solution.py:494
  26.9 0.1 collective-permute-start.5
  27.0 0.7 collective-permute-start.9
  27.8 0.0 collective-permute-done.refs_5_.c1.refs_6_
  27.8 3.0 %shard_map.104 = (bf16[4,768,256]{2,1,0:T(8,128)(2,1)S(1)}, bf16[4,512,128]{2,1,0:T(8,128)(2,1)S(1)}, f32[256,256]{1,0:T(8,128)S(1)}, f32[8,256]{1,0:T(8,128)S(1)}) custom-call(s32[4]{0:T(128)S(1)} %copy-done.1, s32[4]{0:T(128)S(1)} %copy-done.2, s32[1]{0:T(128)} %bitcast.tm.refs_2_.refs_1_, bf16[2,256,256]{2,1,0:T(8,128)(2,1)S(1)} %get-tuple-element.52.refs_3_.qt.refs_2_, ...), custom_call_target="tpu_custom_call" | custom-call | flops 3000000000 | bytes 4000000 | tf_op jit(solution)/shard_map/pallas_call | solution.py:33
  30.8 1.2 %collective-permute-done.1.refs_6_ = bf16[256,512]{1,0:T(8,128)(2,1)S(1)} collective-permute-done((bf16[256,512]{1,0:T(8,128)(2,1)S(1)}, bf16[256,512]{1,0:T(8,128)(2,1)S(1)}, u32[]{:S(2)}, u32[]{:S(2)}) %collective-permute-start.1) | collective-permute-done | bytes 262176 | tf_op jit(solution)/shard_map/ppermute | solution.py:494
  32.0 3.0 %shard_map.105 = (bf16[4,768,256]{2,1,0:T(8,128)(2,1)S(1)}, bf16[4,512,128]{2,1,0:T(8,128)(2,1)S(1)}, f32[256,256]{1,0:T(8,128)S(1)}, f32[8,256]{1,0:T(8,128)S(1)}) custom-call(s32[4]{0:T(128)S(1)} %copy-done.1, s32[4]{0:T(128)S(1)} %copy-done.2, s32[1]{0:T(128)} %bitcast.tm.refs_2_.refs_1_, bf16[2,256,256]{2,1,0:T(8,128)(2,1)S(1)} %get-tuple-element.52.refs_3_.qt.refs_2_, ...), custom_call_target="tpu_custom_call" | custom-call | flops 3000000000 | bytes 4000000 | tf_op jit(solution)/shard_map/pallas_call | solution.py:33
  35.0 3.1 %shard_map.108 = (bf16[4,1024,128]{2,1,0:T(8,128)(2,1)S(1)}, bf16[512,256]{1,0:T(8,128)(2,1)S(1)}, f32[16,512]{1,0:T(8,128)S(1)}) custom-call(s32[4]{0:T(128)S(1)} %copy-done.1, bf16[2,256,256]{2,1,0:T(8,128)(2,1)S(1)} %get-tuple-element.52.refs_3_.qt.refs_2_, bf16[2,256,256]{2,1,0:T(8,128)(2,1)S(1)} %get-tuple-element.53.gt.refs_3_, ...), custom_call_target="tpu_custom_call" | custom-call | flops 3000000000 | bytes 4000000 | tf_op jit(solution)/shard_map/pallas_call | solution.py:33
  38.1 1.8 %shard_map.112 = (bf16[512,512]{1,0:T(8,128)(2,1)S(1)}, f32[512,512]{1,0:T(8,128)S(1)}, f32[256,128]{1,0:T(8,128)S(1)}) custom-call(bf16[2,256,256]{2,1,0:T(8,128)(2,1)S(1)} %get-tuple-element.52.refs_3_.qt.refs_2_, bf16[2,256,256]{2,1,0:T(8,128)(2,1)S(1)} %get-tuple-element.53.gt.refs_3_, f32[16,512]{1,0:T(8,128)S(1)} %get-tuple-element.67.stat2.refs_4_, ...), custom_call_target="tpu_custom_call" | custom-call | flops 4000000000 | bytes 5000000 | tf_op jit(solution)/shard_map/pallas_call | solution.py:33
  40.0 0.1 collective-permute-start.17
  40.1 0.6 collective-permute-start.10
  40.7 0.1 shard_map.110.w02
  40.7 1.3 %collective-permute-start.13 = (bf16[512,1024]{1,0:T(8,128)(2,1)S(1)}, bf16[512,1024]{1,0:T(8,128)(2,1)S(1)}, u32[]{:S(2)}, u32[]{:S(2)}) collective-permute-start(bf16[512,1024]{1,0:T(8,128)(2,1)S(1)} %shard_map.110.w02), channel_id=1, source_target_pairs={{0,1},{1,0},{2,3},{3,2},{4,5},{5,4},{6,7},{7,6},{8,9},{9,8},{10,11... | collective-permute-start | bytes 3145736 | tf_op jit(solution)/shard_map/ppermute | solution.py:489
  42.0 2.3 %shard_map.113 = (bf16[256,512]{1,0:T(8,128)(2,1)S(1)}, f32[256,512]{1,0:T(8,128)S(1)}, f32[256,256]{1,0:T(8,128)S(1)}) custom-call(bf16[2,256,256]{2,1,0:T(8,128)(2,1)S(1)} %get-tuple-element.52.refs_3_.qt.refs_2_, bf16[2,256,256]{2,1,0:T(8,128)(2,1)S(1)} %get-tuple-element.53.gt.refs_3_, f32[16,512]{1,0:T(8,128)S(1)} %get-tuple-element.67.stat2.refs_4_, ...), custom_call_target="tpu_custom_call" | custom-call | flops 4000000000 | bytes 5000000 | tf_op jit(solution)/shard_map/pallas_call | solution.py:33
  44.3 3.0 %shard_map.114 = (f32[512,512]{1,0:T(8,128)S(1)}, bf16[256,512]{1,0:T(8,128)(2,1)S(1)}, bf16[256,256]{1,0:T(8,128)(2,1)S(1)}) custom-call(s32[4]{0:T(128)S(1)} %copy-done.1, s32[1]{0:T(128)} %bitcast.tm.refs_2_.refs_1_, bf16[2,256,256]{2,1,0:T(8,128)(2,1)S(1)} %get-tuple-element.52.refs_3_.qt.refs_2_, bf16[2,256,256]{2,1,0:T(8,128)(2,1)S(1)} %get-tuple-element.53.gt.refs_3_, ...), custom_call_target="tpu_custom_call" | custom-call | flops 4000000000 | bytes 4000000 | tf_op jit(solution)/shard_map/pallas_call | solution.py:33
  47.4 0.2 collective-permute-done.10.right
  47.6 2.7 %collective-permute-start.11 = (bf16[512,512]{1,0:T(8,128)(2,1)S(1)}, bf16[512,512]{1,0:T(8,128)(2,1)S(1)}, u32[]{:S(2)}, u32[]{:S(2)}) collective-permute-start(bf16[512,512]{1,0:T(8,128)(2,1)S(1)} %shard_map.109.a01), channel_id=1, source_target_pairs={{0,3},{1,2},{2,1},{3,0},{4,7},{5,6},{6,5},{7,4},{8,11},{9,10},{10,... | collective-permute-start | bytes 1572872 | tf_op jit(solution)/shard_map/ppermute | solution.py:489
  50.4 0.1 shard_map.116
  50.5 4.1 %collective-permute-start.18 = (bf16[128,512]{1,0:T(8,128)(2,1)S(1)}, bf16[128,512]{1,0:T(8,128)(2,1)S(1)}, u32[]{:S(2)}, u32[]{:S(2)}) collective-permute-start(bf16[128,512]{1,0:T(8,128)(2,1)S(1)} %get-tuple-element.85), channel_id=1, source_target_pairs={{0,32},{4,36},{8,40},{12,44},{16,48},{20,52},{24,56},{28,60},{32,0... | collective-permute-start | bytes 393224 | tf_op jit(solution)/shard_map/ppermute | solution.py:489
  54.5 1.5 %collective-permute-start.19 = (bf16[64,512]{1,0:T(8,128)(2,1)S(1)}, bf16[64,512]{1,0:T(8,128)(2,1)S(1)}, u32[]{:S(2)}, u32[]{:S(2)}) collective-permute-start(bf16[64,512]{1,0:T(8,128)(2,1)S(1)} %get-tuple-element.86), channel_id=1, source_target_pairs={{0,64},{4,68},{8,72},{12,76},{16,80},{20,84},{24,88},{28,92},{32,9... | collective-permute-start | bytes 196616 | tf_op jit(solution)/shard_map/ppermute | solution.py:489
  56.0 0.9 %collective-permute-start.20 = (bf16[64,512]{1,0:T(8,128)(2,1)S(1)}, bf16[64,512]{1,0:T(8,128)(2,1)S(1)}, u32[]{:S(2)}, u32[]{:S(2)}) collective-permute-start(bf16[64,512]{1,0:T(8,128)(2,1)S(1)} %get-tuple-element.87), channel_id=1, source_target_pairs={{0,96},{4,100},{8,104},{12,108},{16,112},{20,116},{24,120},{28,124... | collective-permute-start | bytes 196616 | tf_op jit(solution)/shard_map/ppermute | solution.py:489
  57.0 3.7 %shard_map.115 = (f32[512,512]{1,0:T(8,128)S(1)}, bf16[256,512]{1,0:T(8,128)(2,1)S(1)}, bf16[512,256]{1,0:T(8,128)(2,1)}) custom-call(s32[4]{0:T(128)S(1)} %copy-done.1, s32[1]{0:T(128)} %bitcast.tm.refs_2_.refs_1_, bf16[2,256,256]{2,1,0:T(8,128)(2,1)S(1)} %get-tuple-element.52.refs_3_.qt.refs_2_, bf16[2,256,256]{2,1,0:T(8,128)(2,1)S(1)} %get-tuple-element.53.gt.refs_3_, ...), custom_call_target="tpu_custom_call" | custom-call | flops 4000000000 | bytes 4000000 | tf_op jit(solution)/shard_map/pallas_call | solution.py:33
  60.7 2.3 %collective-permute-start.15 = (bf16[256,512]{1,0:T(8,128)(2,1)S(1)}, bf16[256,512]{1,0:T(8,128)(2,1)S(1)}, u32[]{:S(2)}, u32[]{:S(2)}) collective-permute-start(bf16[256,512]{1,0:T(8,128)(2,1)S(1)} %get-tuple-element.81), channel_id=1, source_target_pairs={{0,4},{4,0},{8,12},{12,8},{16,20},{20,16},{24,28},{28,24},{32,36},... | collective-permute-start | bytes 786440 | tf_op jit(solution)/shard_map/ppermute | solution.py:489
  63.1 1.9 %collective-permute-start.16 = (bf16[256,512]{1,0:T(8,128)(2,1)S(1)}, bf16[256,512]{1,0:T(8,128)(2,1)S(1)}, u32[]{:S(2)}, u32[]{:S(2)}) collective-permute-start(bf16[256,512]{1,0:T(8,128)(2,1)S(1)} %get-tuple-element.82), channel_id=1, source_target_pairs={{4,8},{8,4},{12,16},{16,12},{20,24},{24,20},{28,32},{32,28},{36,40... | collective-permute-start | bytes 786440 | tf_op jit(solution)/shard_map/ppermute | solution.py:494
  65.0 0.1 collective-permute-start.14
  65.2 1.9 %collective-permute-start.21 = (bf16[128,512]{1,0:T(8,128)(2,1)S(1)}, bf16[128,512]{1,0:T(8,128)(2,1)S(1)}, u32[]{:S(2)}, u32[]{:S(2)}) collective-permute-start(bf16[128,512]{1,0:T(8,128)(2,1)S(1)} %get-tuple-element.89), channel_id=1, source_target_pairs={{0,8},{4,12},{8,0},{12,4},{16,24},{20,28},{24,16},{28,20},{32,40},... | collective-permute-start | bytes 393224 | tf_op jit(solution)/shard_map/ppermute | solution.py:489
  67.1 5.1 %collective-permute-done.16.hn = bf16[256,512]{1,0:T(8,128)(2,1)S(1)} collective-permute-done((bf16[256,512]{1,0:T(8,128)(2,1)S(1)}, bf16[256,512]{1,0:T(8,128)(2,1)S(1)}, u32[]{:S(2)}, u32[]{:S(2)}) %collective-permute-start.16) | collective-permute-done | bytes 262176 | tf_op jit(solution)/shard_map/ppermute | solution.py:494
  72.2 1.2 %collective-permute-start.23 = (bf16[64,512]{1,0:T(8,128)(2,1)S(1)}, bf16[64,512]{1,0:T(8,128)(2,1)S(1)}, u32[]{:S(2)}, u32[]{:S(2)}) collective-permute-start(bf16[64,512]{1,0:T(8,128)(2,1)S(1)} %get-tuple-element.91), channel_id=1, source_target_pairs={{0,24},{4,28},{8,16},{12,20},{16,8},{20,12},{24,0},{28,4},{32,56},... | collective-permute-start | bytes 196616 | tf_op jit(solution)/shard_map/ppermute | solution.py:489
  73.4 0.2 shard_map.117.acc
  73.6 3.3 %collective-permute-done.22.x2a = bf16[64,512]{1,0:T(8,128)(2,1)S(1)} collective-permute-done((bf16[64,512]{1,0:T(8,128)(2,1)S(1)}, bf16[64,512]{1,0:T(8,128)(2,1)S(1)}, u32[]{:S(2)}, u32[]{:S(2)}) %collective-permute-start.22) | collective-permute-done | bytes 65568 | tf_op jit(solution)/shard_map/ppermute | solution.py:489
  76.9 1.2 %collective-permute-done.23.x2b = bf16[64,512]{1,0:T(8,128)(2,1)S(1)} collective-permute-done((bf16[64,512]{1,0:T(8,128)(2,1)S(1)}, bf16[64,512]{1,0:T(8,128)(2,1)S(1)}, u32[]{:S(2)}, u32[]{:S(2)}) %collective-permute-start.23) | collective-permute-done | bytes 65568 | tf_op jit(solution)/shard_map/ppermute | solution.py:489
  78.1 1.8 %shard_map.119 = (bf16[512,256]{1,0:T(8,128)(2,1)}, bf16[512,256]{1,0:T(8,128)(2,1)}) custom-call(s32[4]{0:T(128)S(1)} %copy-done.1, s32[1]{0:T(128)} %bitcast.tm.refs_2_.refs_1_, f32[512,512]{1,0:T(8,128)S(1)} %shard_map.117.acc, bf16[128,512]{1,0:T(8,128)(2,1)S(1)} %collective-permute-done.21.x1, bf16[64,512]{1,0:T(8,128)(2,1)S(1)} %collective-permute-done.22.x2a, ...), custom_call_target="tpu_custom_call" | custom-call | flops 300000000 | bytes 3000000 | tf_op jit(solution)/shard_map/pallas_call | solution.py:33
  79.9 2.2 %shard_map.111 = bf16[512,1024]{1,0:T(8,128)(2,1)} custom-call(s32[1]{0:T(128)} %bitcast.tm.refs_2_.refs_1_, bf16[512,512]{1,0:T(8,128)(2,1)S(1)} %shard_map.109.a01, bf16[512,512]{1,0:T(8,128)(2,1)S(1)} %collective-permute-done.11.a23, bf16[512,1024]{1,0:T(8,128)(2,1)S(1)} %shard_map.110.w02, bf16[512,1024]{1,0:T(8,128)(2,1)S(1)} %collective-permute-done.13.w13), custom_call_target="tpu_custom_call" | custom-call | flops 1000000000 | bytes 4000000 | tf_op jit(solution)/shard_map/pallas_call | solution.py:33
  (24 shorter events, 0.2 us)
Async XLA Ops:
  0.6 0.7 copy-start
  1.3 21.5 %copy-start.1 = (s32[4]{0:T(128)S(1)}, s32[4]{0:T(128)}, u32[]{:S(2)}) copy-start(s32[4]{0:T(128)} %off.7) | copy-start | bytes 52
  3.6 24.1 %collective-permute-start = (bf16[384,512]{1,0:T(8,128)(2,1)S(1)}, bf16[384,512]{1,0:T(8,128)(2,1)S(1)}, u32[]{:S(2)}, u32[]{:S(2)}) collective-permute-start(bf16[384,512]{1,0:T(8,128)(2,1)S(1)} %get-tuple-element.55), channel_id=1, source_target_pairs={{0,4},{4,0},{8,12},{12,8},{16,20},{20,16},{24,28},{28,24},{32,36},... | collective-permute-start | bytes 1179656 | tf_op jit(solution)/shard_map/ppermute | solution.py:489
  5.1 9.9 %collective-permute-start.2 = (bf16[128,512]{1,0:T(8,128)(2,1)S(1)}, bf16[128,512]{1,0:T(8,128)(2,1)S(1)}, u32[]{:S(2)}, u32[]{:S(2)}) collective-permute-start(bf16[128,512]{1,0:T(8,128)(2,1)S(1)} %get-tuple-element.61), channel_id=1, source_target_pairs={{0,8},{4,12},{8,0},{12,4},{16,24},{20,28},{24,16},{28,20},{32,40},... | collective-permute-start | bytes 393224 | tf_op jit(solution)/shard_map/ppermute | solution.py:489
  6.4 7.4 %collective-permute-start.3 = (bf16[64,512]{1,0:T(8,128)(2,1)S(1)}, bf16[64,512]{1,0:T(8,128)(2,1)S(1)}, u32[]{:S(2)}, u32[]{:S(2)}) collective-permute-start(bf16[64,512]{1,0:T(8,128)(2,1)S(1)} %get-tuple-element.62), channel_id=1, source_target_pairs={{0,16},{4,20},{8,24},{12,28},{16,0},{20,4},{24,8},{28,12},{32,48},... | collective-permute-start | bytes 196616 | tf_op jit(solution)/shard_map/ppermute | solution.py:489
  8.9 6.1 %collective-permute-start.4 = (bf16[64,512]{1,0:T(8,128)(2,1)S(1)}, bf16[64,512]{1,0:T(8,128)(2,1)S(1)}, u32[]{:S(2)}, u32[]{:S(2)}) collective-permute-start(bf16[64,512]{1,0:T(8,128)(2,1)S(1)} %get-tuple-element.62), channel_id=1, source_target_pairs={{0,24},{4,28},{8,16},{12,20},{16,8},{20,12},{24,0},{28,4},{32,56},... | collective-permute-start | bytes 196616 | tf_op jit(solution)/shard_map/ppermute | solution.py:489
  15.0 12.8 %copy-start.2 = (s32[4]{0:T(128)S(1)}, s32[4]{0:T(128)}, u32[]{:S(2)}) copy-start(s32[4]{0:T(128)} %refs_1_.3) | copy-start | bytes 52
  15.0 12.0 %collective-permute-start.6 = (bf16[128,512]{1,0:T(8,128)(2,1)S(1)}, bf16[128,512]{1,0:T(8,128)(2,1)S(1)}, u32[]{:S(2)}, u32[]{:S(2)}) collective-permute-start(bf16[128,512]{1,0:T(8,128)(2,1)S(1)} %get-tuple-element.64), channel_id=1, source_target_pairs={{0,32},{4,36},{8,40},{12,44},{16,48},{20,52},{24,56},{28,60},{32,0... | collective-permute-start | bytes 393224 | tf_op jit(solution)/shard_map/ppermute | solution.py:489
  16.4 7.6 %collective-permute-start.7 = (bf16[64,512]{1,0:T(8,128)(2,1)S(1)}, bf16[64,512]{1,0:T(8,128)(2,1)S(1)}, u32[]{:S(2)}, u32[]{:S(2)}) collective-permute-start(bf16[64,512]{1,0:T(8,128)(2,1)S(1)} %get-tuple-element.65), channel_id=1, source_target_pairs={{0,64},{4,68},{8,72},{12,76},{16,80},{20,84},{24,88},{28,92},{32,9... | collective-permute-start | bytes 196616 | tf_op jit(solution)/shard_map/ppermute | solution.py:489
  19.0 7.9 %collective-permute-start.8 = (bf16[64,512]{1,0:T(8,128)(2,1)S(1)}, bf16[64,512]{1,0:T(8,128)(2,1)S(1)}, u32[]{:S(2)}, u32[]{:S(2)}) collective-permute-start(bf16[64,512]{1,0:T(8,128)(2,1)S(1)} %get-tuple-element.65), channel_id=1, source_target_pairs={{0,96},{4,100},{8,104},{12,108},{16,112},{20,116},{24,120},{28,124... | collective-permute-start | bytes 196616 | tf_op jit(solution)/shard_map/ppermute | solution.py:489
  19.0 21.7 %collective-permute-start.12 = (bf16[256,1024]{1,0:T(8,128)(2,1)S(1)}, bf16[256,1024]{1,0:T(8,128)(2,1)S(1)}, u32[]{:S(2)}, u32[]{:S(2)}) collective-permute-start(bf16[256,1024]{1,0:T(8,128)(2,1)S(1)} %get-tuple-element.51.w.refs_0_), channel_id=1, source_target_pairs={{0,3},{1,2},{2,1},{3,0},{4,7},{5,6},{6,5},{7,4},{8,11},{9,10},{10,... | collective-permute-start | bytes 1572872 | tf_op jit(solution)/shard_map/ppermute | solution.py:489
  24.0 8.0 %collective-permute-start.1 = (bf16[256,512]{1,0:T(8,128)(2,1)S(1)}, bf16[256,512]{1,0:T(8,128)(2,1)S(1)}, u32[]{:S(2)}, u32[]{:S(2)}) collective-permute-start(bf16[256,512]{1,0:T(8,128)(2,1)S(1)} %get-tuple-element.57), channel_id=1, source_target_pairs={{4,8},{8,4},{12,16},{16,12},{20,24},{24,20},{28,32},{32,28},{36,40... | collective-permute-start | bytes 786440 | tf_op jit(solution)/shard_map/ppermute | solution.py:494
  26.9 8.1 %collective-permute-start.5 = (bf16[256,512]{1,0:T(8,128)(2,1)S(1)}, bf16[256,512]{1,0:T(8,128)(2,1)S(1)}, u32[]{:S(2)}, u32[]{:S(2)}) collective-permute-start(bf16[256,512]{1,0:T(8,128)(2,1)S(1)} %get-tuple-element.63.rest_0_), channel_id=1, source_target_pairs={{0,4},{4,0},{8,12},{12,8},{16,20},{20,16},{24,28},{28,24},{32,36},... | collective-permute-start | bytes 786440 | tf_op jit(solution)/shard_map/ppermute | solution.py:489
  27.0 8.0 %collective-permute-start.9 = (bf16[256,512]{1,0:T(8,128)(2,1)S(1)}, bf16[256,512]{1,0:T(8,128)(2,1)S(1)}, u32[]{:S(2)}, u32[]{:S(2)}) collective-permute-start(bf16[256,512]{1,0:T(8,128)(2,1)S(1)} %shard_map.107.rest_2_), channel_id=1, source_target_pairs={{0,4},{4,0},{8,12},{12,8},{16,20},{20,16},{24,28},{28,24},{32,36},... | collective-permute-start | bytes 786440 | tf_op jit(solution)/shard_map/ppermute | solution.py:489
  40.0 10.4 %collective-permute-start.17 = (bf16[512,512]{1,0:T(8,128)(2,1)S(1)}, bf16[512,512]{1,0:T(8,128)(2,1)S(1)}, u32[]{:S(2)}, u32[]{:S(2)}) collective-permute-start(bf16[512,512]{1,0:T(8,128)(2,1)S(1)} %get-tuple-element.84), channel_id=1, source_target_pairs={{0,4},{4,0},{8,12},{12,8},{16,20},{20,16},{24,28},{28,24},{32,36},... | collective-permute-start | bytes 1572872 | tf_op jit(solution)/shard_map/ppermute | solution.py:489
  40.1 7.5 %collective-permute-start.10 = (bf16[512,256]{1,0:T(8,128)(2,1)S(1)}, bf16[512,256]{1,0:T(8,128)(2,1)S(1)}, u32[]{:S(2)}, u32[]{:S(2)}) collective-permute-start(bf16[512,256]{1,0:T(8,128)(2,1)S(1)} %get-tuple-element.66.left), channel_id=1, source_target_pairs={{0,1},{1,0},{2,3},{3,2},{4,5},{5,4},{6,7},{7,6},{8,9},{9,8},{10,11... | collective-permute-start | bytes 786440 | tf_op jit(solution)/shard_map/ppermute | solution.py:489
  40.7 39.2 %collective-permute-start.13 = (bf16[512,1024]{1,0:T(8,128)(2,1)S(1)}, bf16[512,1024]{1,0:T(8,128)(2,1)S(1)}, u32[]{:S(2)}, u32[]{:S(2)}) collective-permute-start(bf16[512,1024]{1,0:T(8,128)(2,1)S(1)} %shard_map.110.w02), channel_id=1, source_target_pairs={{0,1},{1,0},{2,3},{3,2},{4,5},{5,4},{6,7},{7,6},{8,9},{9,8},{10,11... | collective-permute-start | bytes 3145736 | tf_op jit(solution)/shard_map/ppermute | solution.py:489
  47.6 32.3 %collective-permute-start.11 = (bf16[512,512]{1,0:T(8,128)(2,1)S(1)}, bf16[512,512]{1,0:T(8,128)(2,1)S(1)}, u32[]{:S(2)}, u32[]{:S(2)}) collective-permute-start(bf16[512,512]{1,0:T(8,128)(2,1)S(1)} %shard_map.109.a01), channel_id=1, source_target_pairs={{0,3},{1,2},{2,1},{3,0},{4,7},{5,6},{6,5},{7,4},{8,11},{9,10},{10,... | collective-permute-start | bytes 1572872 | tf_op jit(solution)/shard_map/ppermute | solution.py:489
  50.5 14.6 %collective-permute-start.18 = (bf16[128,512]{1,0:T(8,128)(2,1)S(1)}, bf16[128,512]{1,0:T(8,128)(2,1)S(1)}, u32[]{:S(2)}, u32[]{:S(2)}) collective-permute-start(bf16[128,512]{1,0:T(8,128)(2,1)S(1)} %get-tuple-element.85), channel_id=1, source_target_pairs={{0,32},{4,36},{8,40},{12,44},{16,48},{20,52},{24,56},{28,60},{32,0... | collective-permute-start | bytes 393224 | tf_op jit(solution)/shard_map/ppermute | solution.py:489
  54.5 6.2 %collective-permute-start.19 = (bf16[64,512]{1,0:T(8,128)(2,1)S(1)}, bf16[64,512]{1,0:T(8,128)(2,1)S(1)}, u32[]{:S(2)}, u32[]{:S(2)}) collective-permute-start(bf16[64,512]{1,0:T(8,128)(2,1)S(1)} %get-tuple-element.86), channel_id=1, source_target_pairs={{0,64},{4,68},{8,72},{12,76},{16,80},{20,84},{24,88},{28,92},{32,9... | collective-permute-start | bytes 196616 | tf_op jit(solution)/shard_map/ppermute | solution.py:489
  56.0 7.0 %collective-permute-start.20 = (bf16[64,512]{1,0:T(8,128)(2,1)S(1)}, bf16[64,512]{1,0:T(8,128)(2,1)S(1)}, u32[]{:S(2)}, u32[]{:S(2)}) collective-permute-start(bf16[64,512]{1,0:T(8,128)(2,1)S(1)} %get-tuple-element.87), channel_id=1, source_target_pairs={{0,96},{4,100},{8,104},{12,108},{16,112},{20,116},{24,120},{28,124... | collective-permute-start | bytes 196616 | tf_op jit(solution)/shard_map/ppermute | solution.py:489
  60.7 4.4 %collective-permute-start.15 = (bf16[256,512]{1,0:T(8,128)(2,1)S(1)}, bf16[256,512]{1,0:T(8,128)(2,1)S(1)}, u32[]{:S(2)}, u32[]{:S(2)}) collective-permute-start(bf16[256,512]{1,0:T(8,128)(2,1)S(1)} %get-tuple-element.81), channel_id=1, source_target_pairs={{0,4},{4,0},{8,12},{12,8},{16,20},{20,16},{24,28},{28,24},{32,36},... | collective-permute-start | bytes 786440 | tf_op jit(solution)/shard_map/ppermute | solution.py:489
  63.1 9.1 %collective-permute-start.16 = (bf16[256,512]{1,0:T(8,128)(2,1)S(1)}, bf16[256,512]{1,0:T(8,128)(2,1)S(1)}, u32[]{:S(2)}, u32[]{:S(2)}) collective-permute-start(bf16[256,512]{1,0:T(8,128)(2,1)S(1)} %get-tuple-element.82), channel_id=1, source_target_pairs={{4,8},{8,4},{12,16},{16,12},{20,24},{24,20},{28,32},{32,28},{36,40... | collective-permute-start | bytes 786440 | tf_op jit(solution)/shard_map/ppermute | solution.py:494
  65.0 7.2 %collective-permute-start.14 = (bf16[256,512]{1,0:T(8,128)(2,1)S(1)}, bf16[256,512]{1,0:T(8,128)(2,1)S(1)}, u32[]{:S(2)}, u32[]{:S(2)}) collective-permute-start(bf16[256,512]{1,0:T(8,128)(2,1)S(1)} %get-tuple-element.80), channel_id=1, source_target_pairs={{0,4},{4,0},{8,12},{12,8},{16,20},{20,16},{24,28},{28,24},{32,36},... | collective-permute-start | bytes 786440 | tf_op jit(solution)/shard_map/ppermute | solution.py:489
  65.2 12.9 %collective-permute-start.21 = (bf16[128,512]{1,0:T(8,128)(2,1)S(1)}, bf16[128,512]{1,0:T(8,128)(2,1)S(1)}, u32[]{:S(2)}, u32[]{:S(2)}) collective-permute-start(bf16[128,512]{1,0:T(8,128)(2,1)S(1)} %get-tuple-element.89), channel_id=1, source_target_pairs={{0,8},{4,12},{8,0},{12,4},{16,24},{20,28},{24,16},{28,20},{32,40},... | collective-permute-start | bytes 393224 | tf_op jit(solution)/shard_map/ppermute | solution.py:489
  72.2 4.7 %collective-permute-start.22 = (bf16[64,512]{1,0:T(8,128)(2,1)S(1)}, bf16[64,512]{1,0:T(8,128)(2,1)S(1)}, u32[]{:S(2)}, u32[]{:S(2)}) collective-permute-start(bf16[64,512]{1,0:T(8,128)(2,1)S(1)} %get-tuple-element.90), channel_id=1, source_target_pairs={{0,16},{4,20},{8,24},{12,28},{16,0},{20,4},{24,8},{28,12},{32,48},... | collective-permute-start | bytes 196616 | tf_op jit(solution)/shard_map/ppermute | solution.py:489
  72.2 5.9 %collective-permute-start.23 = (bf16[64,512]{1,0:T(8,128)(2,1)S(1)}, bf16[64,512]{1,0:T(8,128)(2,1)S(1)}, u32[]{:S(2)}, u32[]{:S(2)}) collective-permute-start(bf16[64,512]{1,0:T(8,128)(2,1)S(1)} %get-tuple-element.91), channel_id=1, source_target_pairs={{0,24},{4,28},{8,16},{12,20},{16,8},{20,12},{24,0},{28,4},{32,56},... | collective-permute-start | bytes 196616 | tf_op jit(solution)/shard_map/ppermute | solution.py:489

commit v3 on v2

--- a/solution.py
+++ b/solution.py
@@ -102,7 +102,7 @@
     return pl.ds(pl.multiple_of(256 * block, 256), 256)
 
 
-def prep_kv(off, tm, k, v, q, up, w, kvp, c1, n1, x1, x2, qv, upv, wv, kb, vb, sem):
+def prep_kv(tm, off_hbm, k, v, q, up, w, kvp, c1, n1, x1, x2, qv, upv, wv, kb, vb, off, sem):
     copies = []
     for src, dst in ((k, kb), (v, vb), (q, qv), (up, upv)):
         for which in range(2):
@@ -112,8 +112,11 @@
                 )
             )
     copies.append(pltpu.make_async_copy(w, wv, sem.at[8]))
+    table = pltpu.make_async_copy(off_hbm, off, sem.at[9])
+    table.start()
     for c in copies:
         c.start()
+    table.wait()
     perms = [to_depth(off[h]) for h in range(4)]
     for c in copies[:4]:
         c.wait()
@@ -385,7 +388,8 @@
     if which == 1:
         own, halo_out, gq, dqt = rest
     else:
-        own_in, own_near, gq_in, own, halo_out, gq, dqt = rest
+        own_in, own_near, near_s, gq_in, own, halo_out, gq, dqt = rest
+        halo_out[256:384] = near_s[128:256]
         gq[block_rows(tm, 1), :] = gq_in[...]
     bs = slice(256 * which, 256 * which + 256)
     ob = slice(256 - 256 * which, 512 - 256 * which)
@@ -412,7 +416,11 @@
         probs = jnp.concatenate([pw[2 * pair], pw[2 * pair + 1]], axis=1)
         for lanes, left, right in ((lo, jnp.concatenate(grads, axis=1), scaled_q), (hi, probs, scaled_g)):
             d = dot_nt(left, jnp.concatenate(right, axis=1))
-            halo_out[:, lanes] = d[0:256].astype(BF16)
+            if which == 1:
+                halo_out[:, lanes] = d[0:256].astype(BF16)
+            else:
+                halo_out[0:128, lanes] = (d[0:128] + near_s[0:128, lanes].astype(F32)).astype(BF16)
+                halo_out[128:256, lanes] = d[128:256].astype(BF16)
             if which == 1:
                 own[bs, lanes] = d[256:512]
                 own[ob, lanes] = d[512:768]
@@ -450,13 +458,12 @@
     x2b[...] = jnp.concatenate(total[12:18], axis=0).astype(BF16)
 
 
-def gather_own(own, near_r, hc, hn, y1, y2a, y2b, acc):
+def gather_own(own, hc, hn, y1, y2a, y2b, acc):
     acc[...] = own[...]
-    acc[0:256] += hc[...].astype(F32)
+    acc[0:384] += hc[...].astype(F32)
     acc[256:512] += hn[...].astype(F32)
     for b in range(2):
         at = 256 * b
-        acc[at : at + 128] += near_r[128 * b : 128 * b + 128].astype(F32)
         acc[at : at + 16] += y1[16 * b : 16 * b + 16].astype(F32)
         acc[at : at + 8] += (y2a[0:16].astype(F32) + y2b[0:16].astype(F32))[8 * b : 8 * b + 8]
 
@@ -477,16 +484,36 @@
             gv[block_rows(tm, b), lanes] = r[:, 128:256]
 
 
-def project(tm, a01, a23, w02, w13, out):
-    w = jnp.concatenate([w02[0:256], w13[0:256], w02[256:512], w13[256:512]], axis=0)
+def half_rows(tm, w, out):
+    out[...] = w[pl.ds(pl.multiple_of(128 * parity(tm), 128), 128), :]
+
+
+def asm_w(tm, own, first, other, mine, theirs, out):
+    out[0:256] = own[...]
+    out[256:512] = first[...]
+    out[512:768] = other[...]
+    p = parity(tm)
+    out[pl.ds(pl.multiple_of(768 + 128 * p, 128), 128), :] = mine[...]
+    out[pl.ds(pl.multiple_of(896 - 128 * p, 128), 128), :] = theirs[...]
+
+
+def project(tm, a01, a23, w, out):
     for b in range(2):
         bs = slice(256 * b, 256 * b + 256)
         a = jnp.concatenate([a01[bs], a23[bs]], axis=1)
-        out[block_rows(tm, b), :] = dot(a, w).astype(BF16)
+        out[block_rows(tm, b), :] = dot(a, w[...]).astype(BF16)
 
 
 def swap(x, axis, mask):
     return lax.ppermute(x, axis, [(i, i ^ mask) for i in range(lax.axis_size(axis))])
+
+
+def cross(x, masks):
+    heads = lax.axis_size("head")
+    pairs = []
+    for i in range(lax.axis_size("tm")):
+        pairs += [(i * heads + z, i * heads + (z ^ masks[i % 2])) for z in range(heads)]
+    return lax.ppermute(x, ("tm", "head"), pairs)
 
 
 def side(x):
@@ -507,19 +534,23 @@
     hbm = pl.BlockSpec(memory_space=pltpu.HBM)
     rows = lambda n: sds((n, 512), BF16)
     kvp, c1s, n1s, x1s, x2s, qv, upv, wv = call(
-        prep_kv, (off, tm) + tuple(pltpu.with_memory_space_constraint(x, pltpu.HBM) for x in (k, v, q, up, w)),
+        prep_kv, (tm,) + tuple(pltpu.with_memory_space_constraint(x, pltpu.HBM) for x in (off, k, v, q, up, w)),
         [rows(512), rows(384), rows(256), rows(128), rows(64),
          sds((512, 256), BF16), sds((512, 1024), BF16), sds((256, 1024), BF16)],
-        specs=[SMEM, SMEM] + [hbm] * 5,
-        scratch=[VM((512, 256), BF16), VM((512, 256), BF16), pltpu.SemaphoreType.DMA((9,))],
+        specs=[SMEM] + [hbm] * 6,
+        scratch=[VM((512, 256), BF16), VM((512, 256), BF16), pltpu.SMEM((4,), jnp.int32), pltpu.SemaphoreType.DMA((10,))],
         flops=3e8, nbytes=3e6,
     )
     x1, x2a, x2b = swap(x1s, "tm", 2), swap(x2s, "tm", 4), swap(x2s, "tm", 6)
     c1 = swap(c1s, "tm", 1)
     n1 = side(n1s)
-    w1 = swap(wv, "head", 3)
-    (w02,) = call(stack, (wv, w1), [sds((512, 1024), BF16)])
-    w13 = swap(w02, "head", 1)
+    w1 = cross(wv, (1, 3))
+    (w1h,) = call(half_rows, (tm, w1), [sds((128, 1024), BF16)], specs=[SMEM, None])
+    w2 = cross(w1h, (3, 1))
+    (w_all,) = call(
+        asm_w, (tm, wv, w1, swap(w1, "tm", 1), w2, swap(w2, "tm", 1)),
+        [sds((1024, 1024), BF16)], specs=[SMEM] + [None] * 5, nbytes=4e6,
+    )
     qt, gt = call(
         prep_qg, (off, qv, upv, wv), [sds((2, 256, 256), BF16), sds((2, 256, 256), BF16)],
         specs=[SMEM] + [None] * 3, flops=6e8, nbytes=3e6,
@@ -549,12 +580,12 @@
         scratch=[VM((1024, 128), BF16), VM((128, 1024), BF16), VM((1024, 128), F32), VM((128, 512), BF16)],
         flops=3e9, nbytes=4e6,
     )
-    a1 = swap(attn, "head", 1)
+    a1 = cross(attn, (1, 3))
     (a01,) = call(beside, (attn, a1), [rows(512)])
-    a23 = swap(a01, "head", 3)
+    a23 = cross(a01, (3, 1))
     (mixed,) = call(
-        project, (tm, a01, a23, w02, w13), [sds((512, 1024), BF16)],
-        specs=[SMEM] + [None] * 4, flops=1e9, nbytes=4e6,
+        project, (tm, a01, a23, w_all), [sds((512, 1024), BF16)],
+        specs=[SMEM] + [None] * 3, flops=1e9, nbytes=4e6,
     )
     ret_s, own_far, dqf = call(
         bwd_far, (qt, gt, stat2, pf, *bufs),
@@ -567,24 +598,23 @@
         [sds((256, 512), BF16), sds((256, 512), F32), sds((256, 256), F32)],
         flops=4e9, nbytes=5e6,
     )
-    near_r = swap(near_s, "tm", 1)
-
-    def back(which, halo, gq_rows, more):
+
+    def back(which, halo, gq_rows, halo_rows, more):
         return call(
             bind(bwd_near, which), (off, tm, qt, gt, stat2, kvp, halo, near[which][0], dqf, dqn, *more),
-            [sds((512, 512), F32), sds((256, 512), BF16), sds((gq_rows, 256), BF16)],
+            [sds((512, 512), F32), rows(halo_rows), sds((gq_rows, 256), BF16)],
             specs=[SMEM] * 2 + [None] * (8 + len(more)),
             scratch=[VM((128, 256), BF16)], flops=4e9, nbytes=4e6,
         )
 
-    own1, hn_s, gq1 = back(1, n1, 256, ())
-    own, hc_s, gq = back(0, c1, 512, (own1, own_near, gq1))
+    own1, hn_s, gq1 = back(1, n1, 256, 256, ())
+    own, hc_s, gq = back(0, c1, 512, 384, (own1, own_near, near_s, gq1))
     rest, y1s, y2as, y2bs = call(ret_y, (own_far, ret), [sds((256, 512), F32), rows(128), rows(64), rows(64)])
     yr = [swap(x, "tm", m) for x, m in ((y1s, 8), (y2as, 16), (y2bs, 24))]
     x1s, x2as, x2bs = call(ret_x, (rest, *yr), [rows(128), rows(64), rows(64)])
     xr = [swap(x, "tm", m) for x, m in ((x1s, 2), (x2as, 4), (x2bs, 6))]
     hc, hn = swap(hc_s, "tm", 1), side(hn_s)
-    (acc,) = call(gather_own, (own, near_r, hc, hn, *yr), [sds((512, 512), F32)], nbytes=3e6)
+    (acc,) = call(gather_own, (own, hc, hn, *yr), [sds((512, 512), F32)], nbytes=3e6)
     gk, gv = call(
         finish, (off, tm, acc, *xr), [sds((512, 256), BF16), sds((512, 256), BF16)],
         specs=[SMEM] * 2 + [None] * 4, flops=3e8, nbytes=3e6,

time: 82.4 us -> 81.7 us (level)
    ppermute x0 -> x4, starting transfers between devices: none -> 7.34 us  [cross(): return lax.ppermute(x, ('tm', 'head'), pairs)]
    ppermute x22 -> x19, starting transfers between devices: 30.6 us -> 24.1 us  [swap(): lax.ppermute(x, axis, [(i, i ^ mask) for i in range(lax.axis_size(axis))])]
    ppermute x2, waiting for transfers between devices: 6.25 us -> 7.45 us  [side(): return lax.ppermute(x, 'tm', pairs)]
    ppermute x2, starting transfers between devices: 4.79 us -> 3.83 us  [side(): return lax.ppermute(x, 'tm', pairs)]
    ppermute x22 -> x19, waiting for transfers between devices: 10.7 us -> 10.1 us  [swap(): lax.ppermute(x, axis, [(i, i ^ mask) for i in range(lax.axis_size(axis))])]
    pallas_call x18 -> x19, Pallas kernels: 28.2 us -> 27.8 us  [call(): pl.pallas_call(body, out_shape=outs, grid=(1,), in_specs=in_specs, out_sp...]
  transfers between devices with their start and end apart: 24 -> 25, of which waited for: 7 -> 6; matrix products, arithmetic and copies ran while one was open for 0% -> 0% of each run, Pallas kernels for 29% -> 29%
where the time goes in v3:
time: 81.7 us; the launch traced here: 81.5 us
  starting transfers between devices  35.3 us (43%)
  Pallas kernels  27.8 us (34%)
  waiting for transfers between devices  17.5 us (21%)
  between operations  0.89 us (1%)
    pallas_call x19, Pallas kernels, call(): pl.pallas_call(body, out_shape=outs, grid=(1,), in_specs=in_specs, out_sp...  27.8 us
    ppermute x19, starting transfers between devices, swap(): lax.ppermute(x, axis, [(i, i ^ mask) for i in range(lax.axis_size(axis))])  24.1 us
    ppermute x19, waiting for transfers between devices, swap(): lax.ppermute(x, axis, [(i, i ^ mask) for i in range(lax.axis_size(axis))])  10.1 us
    ppermute x2, waiting for transfers between devices, side(): return lax.ppermute(x, 'tm', pairs)  7.45 us
    ppermute x4, starting transfers between devices, cross(): return lax.ppermute(x, ('tm', 'head'), pairs)  7.34 us
    ppermute x2, starting transfers between devices, side(): return lax.ppermute(x, 'tm', pairs)  3.83 us
  transfers between devices with their start and end apart: 25, of which 6 were waited for; matrix products, arithmetic and copies ran while one was open for 0% of the time, Pallas kernels for 29%

profile of v3, /device:TPU:1, one launch (start us, length us, event | category | flops | bytes accessed | tf_op | source)
XLA Modules:
  0.0 81.5 jit_solution(14222678647121558093)
XLA Ops:
  0.6 1.8 %shard_map.102 = (bf16[512,512]{1,0:T(8,128)(2,1)S(1)}, bf16[384,512]{1,0:T(8,128)(2,1)S(1)}, bf16[256,512]{1,0:T(8,128)(2,1)S(1)}, bf16[128,512]{1,0:T(8,128)(2...) custom-call(s32[1]{0:T(128)} %bitcast.tm.refs_2_.refs_1_, ...), custom_call_target="tpu_custom_call" | custom-call | flops 300000000 | bytes 3000000 | tf_op jit(solution)/shard_map/pallas_call | solution.py:33
  2.5 1.5 %collective-permute-start = (bf16[384,512]{1,0:T(8,128)(2,1)S(1)}, bf16[384,512]{1,0:T(8,128)(2,1)S(1)}, u32[]{:S(2)}, u32[]{:S(2)}) collective-permute-start(bf16[384,512]{1,0:T(8,128)(2,1)S(1)} %get-tuple-element.55), channel_id=1, source_target_pairs={{0,4},{4,0},{8,12},{12,8},{16,20},{20,16},{24,28},{28,24},{32,36},... | collective-permute-start | bytes 1179656 | tf_op jit(solution)/shard_map/ppermute | solution.py:508
  3.9 1.3 %collective-permute-start.2 = (bf16[128,512]{1,0:T(8,128)(2,1)S(1)}, bf16[128,512]{1,0:T(8,128)(2,1)S(1)}, u32[]{:S(2)}, u32[]{:S(2)}) collective-permute-start(bf16[128,512]{1,0:T(8,128)(2,1)S(1)} %get-tuple-element.61), channel_id=1, source_target_pairs={{0,8},{4,12},{8,0},{12,4},{16,24},{20,28},{24,16},{28,20},{32,40},... | collective-permute-start | bytes 393224 | tf_op jit(solution)/shard_map/ppermute | solution.py:508
  5.2 2.5 %collective-permute-start.3 = (bf16[64,512]{1,0:T(8,128)(2,1)S(1)}, bf16[64,512]{1,0:T(8,128)(2,1)S(1)}, u32[]{:S(2)}, u32[]{:S(2)}) collective-permute-start(bf16[64,512]{1,0:T(8,128)(2,1)S(1)} %get-tuple-element.62), channel_id=1, source_target_pairs={{0,16},{4,20},{8,24},{12,28},{16,0},{20,4},{24,8},{28,12},{32,48},... | collective-permute-start | bytes 196616 | tf_op jit(solution)/shard_map/ppermute | solution.py:508
  7.7 0.1 collective-permute-start.4
  7.8 4.8 %collective-permute-done.3.x2a = bf16[64,512]{1,0:T(8,128)(2,1)S(1)} collective-permute-done((bf16[64,512]{1,0:T(8,128)(2,1)S(1)}, bf16[64,512]{1,0:T(8,128)(2,1)S(1)}, u32[]{:S(2)}, u32[]{:S(2)}) %collective-permute-start.3) | collective-permute-done | bytes 65568 | tf_op jit(solution)/shard_map/ppermute | solution.py:508
  12.6 1.2 %collective-permute-done.4.x2b = bf16[64,512]{1,0:T(8,128)(2,1)S(1)} collective-permute-done((bf16[64,512]{1,0:T(8,128)(2,1)S(1)}, bf16[64,512]{1,0:T(8,128)(2,1)S(1)}, u32[]{:S(2)}, u32[]{:S(2)}) %collective-permute-start.4) | collective-permute-done | bytes 65568 | tf_op jit(solution)/shard_map/ppermute | solution.py:508
  13.8 0.0 copy-start.1
  13.8 1.4 %collective-permute-start.6 = (bf16[128,512]{1,0:T(8,128)(2,1)S(1)}, bf16[128,512]{1,0:T(8,128)(2,1)S(1)}, u32[]{:S(2)}, u32[]{:S(2)}) collective-permute-start(bf16[128,512]{1,0:T(8,128)(2,1)S(1)} %get-tuple-element.64), channel_id=1, source_target_pairs={{0,32},{4,36},{8,40},{12,44},{16,48},{20,52},{24,56},{28,60},{32,0... | collective-permute-start | bytes 393224 | tf_op jit(solution)/shard_map/ppermute | solution.py:508
  15.2 2.6 %collective-permute-start.7 = (bf16[64,512]{1,0:T(8,128)(2,1)S(1)}, bf16[64,512]{1,0:T(8,128)(2,1)S(1)}, u32[]{:S(2)}, u32[]{:S(2)}) collective-permute-start(bf16[64,512]{1,0:T(8,128)(2,1)S(1)} %get-tuple-element.65), channel_id=1, source_target_pairs={{0,64},{4,68},{8,72},{12,76},{16,80},{20,84},{24,88},{28,92},{32,9... | collective-permute-start | bytes 196616 | tf_op jit(solution)/shard_map/ppermute | solution.py:508
  17.8 0.0 collective-permute-start.8
  17.8 3.8 %collective-permute-start.12 = (bf16[256,1024]{1,0:T(8,128)(2,1)S(1)}, bf16[256,1024]{1,0:T(8,128)(2,1)S(1)}, u32[]{:S(2)}, u32[]{:S(2)}) collective-permute-start(bf16[256,1024]{1,0:T(8,128)(2,1)S(1)} %get-tuple-element.51.w.own), channel_id=1, source_target_pairs={{0,1},{1,0},{2,3},{3,2},{4,7},{5,6},{6,5},{7,4},{8,9},{9,8},{10,11... | collective-permute-start | bytes 1572872 | tf_op jit(solution)/shard_map/ppermute | solution.py:516
  21.6 1.2 %shard_map.103 = (bf16[2,256,256]{2,1,0:T(8,128)(2,1)S(1)}, bf16[2,256,256]{2,1,0:T(8,128)(2,1)S(1)}) custom-call(s32[4]{0:T(128)S(1)} %copy-done, bf16[512,256]{1,0:T(8,128)(2,1)S(1)} %get-tuple-element.49.q, bf16[512,1024]{1,0:T(8,128)(2,1)S(1)} %get-tuple-element.50.up, bf16[256,1024]{1,0:T(8,128)(2,1)S(1)} %get-tuple-element.51.w.own), custom_call_target="tpu_custom_call" | custom-call | flops 600000000 | bytes 3000000 | tf_op jit(solution)/shard_map/pallas_call | solution.py:33
  22.8 1.9 %collective-permute-start.1 = (bf16[256,512]{1,0:T(8,128)(2,1)S(1)}, bf16[256,512]{1,0:T(8,128)(2,1)S(1)}, u32[]{:S(2)}, u32[]{:S(2)}) collective-permute-start(bf16[256,512]{1,0:T(8,128)(2,1)S(1)} %get-tuple-element.57), channel_id=1, source_target_pairs={{4,8},{8,4},{12,16},{16,12},{20,24},{24,20},{28,32},{32,28},{36,40... | collective-permute-start | bytes 786440 | tf_op jit(solution)/shard_map/ppermute | solution.py:521
  24.7 0.0 collective-permute-done.8.refs_2_
  24.7 0.1 collective-permute-start.5
  24.8 0.0 collective-permute-done.6.refs_0_
  24.9 0.7 collective-permute-start.9
  25.6 3.0 %shard_map.104 = (bf16[4,768,256]{2,1,0:T(8,128)(2,1)S(1)}, bf16[4,512,128]{2,1,0:T(8,128)(2,1)S(1)}, f32[256,256]{1,0:T(8,128)S(1)}, f32[8,256]{1,0:T(8,128)S(1)}) custom-call(s32[4]{0:T(128)S(1)} %copy-done, s32[4]{0:T(128)S(1)} %copy-done.1, s32[1]{0:T(128)} %bitcast.tm.refs_2_.refs_1_, bf16[2,256,256]{2,1,0:T(8,128)(2,1)S(1)} %get-tuple-element.52.refs_3_.qt.refs_2_, ...), custom_call_target="tpu_custom_call" | custom-call | flops 3000000000 | bytes 4000000 | tf_op jit(solution)/shard_map/pallas_call | solution.py:33
  28.7 1.8 %collective-permute-done.1.refs_6_ = bf16[256,512]{1,0:T(8,128)(2,1)S(1)} collective-permute-done((bf16[256,512]{1,0:T(8,128)(2,1)S(1)}, bf16[256,512]{1,0:T(8,128)(2,1)S(1)}, u32[]{:S(2)}, u32[]{:S(2)}) %collective-permute-start.1) | collective-permute-done | bytes 262176 | tf_op jit(solution)/shard_map/ppermute | solution.py:521
  30.5 3.0 %shard_map.105 = (bf16[4,768,256]{2,1,0:T(8,128)(2,1)S(1)}, bf16[4,512,128]{2,1,0:T(8,128)(2,1)S(1)}, f32[256,256]{1,0:T(8,128)S(1)}, f32[8,256]{1,0:T(8,128)S(1)}) custom-call(s32[4]{0:T(128)S(1)} %copy-done, s32[4]{0:T(128)S(1)} %copy-done.1, s32[1]{0:T(128)} %bitcast.tm.refs_2_.refs_1_, bf16[2,256,256]{2,1,0:T(8,128)(2,1)S(1)} %get-tuple-element.52.refs_3_.qt.refs_2_, ...), custom_call_target="tpu_custom_call" | custom-call | flops 3000000000 | bytes 4000000 | tf_op jit(solution)/shard_map/pallas_call | solution.py:33
  33.5 0.0 collective-permute-done.5.rest_1_
  33.5 3.1 %shard_map.108 = (bf16[4,1024,128]{2,1,0:T(8,128)(2,1)S(1)}, bf16[512,256]{1,0:T(8,128)(2,1)S(1)}, f32[16,512]{1,0:T(8,128)S(1)}) custom-call(s32[4]{0:T(128)S(1)} %copy-done, bf16[2,256,256]{2,1,0:T(8,128)(2,1)S(1)} %get-tuple-element.52.refs_3_.qt.refs_2_, bf16[2,256,256]{2,1,0:T(8,128)(2,1)S(1)} %get-tuple-element.53.gt.refs_3_, ...), custom_call_target="tpu_custom_call" | custom-call | flops 3000000000 | bytes 4000000 | tf_op jit(solution)/shard_map/pallas_call | solution.py:33
  36.7 1.8 %shard_map.113 = (bf16[512,512]{1,0:T(8,128)(2,1)S(1)}, f32[512,512]{1,0:T(8,128)S(1)}, f32[256,128]{1,0:T(8,128)S(1)}) custom-call(bf16[2,256,256]{2,1,0:T(8,128)(2,1)S(1)} %get-tuple-element.52.refs_3_.qt.refs_2_, bf16[2,256,256]{2,1,0:T(8,128)(2,1)S(1)} %get-tuple-element.53.gt.refs_3_, f32[16,512]{1,0:T(8,128)S(1)} %get-tuple-element.67.stat2.refs_4_, ...), custom_call_target="tpu_custom_call" | custom-call | flops 4000000000 | bytes 5000000 | tf_op jit(solution)/shard_map/pallas_call | solution.py:33
  38.5 0.1 collective-permute-start.18
  38.6 2.7 %collective-permute-start.10 = (bf16[512,256]{1,0:T(8,128)(2,1)S(1)}, bf16[512,256]{1,0:T(8,128)(2,1)S(1)}, u32[]{:S(2)}, u32[]{:S(2)}) collective-permute-start(bf16[512,256]{1,0:T(8,128)(2,1)S(1)} %get-tuple-element.66.left), channel_id=1, source_target_pairs={{0,1},{1,0},{2,3},{3,2},{4,7},{5,6},{6,5},{7,4},{8,9},{9,8},{10,11... | collective-permute-start | bytes 786440 | tf_op jit(solution)/shard_map/ppermute | solution.py:516
  41.3 0.1 collective-permute-start.14
  41.4 1.1 %collective-permute-start.13 = (bf16[256,1024]{1,0:T(8,128)(2,1)S(1)}, bf16[256,1024]{1,0:T(8,128)(2,1)S(1)}, u32[]{:S(2)}, u32[]{:S(2)}) collective-permute-start(bf16[256,1024]{1,0:T(8,128)(2,1)S(1)} %collective-permute-done.12.w.first), channel_id=1, source_target_pairs={{0,4},{4,0},{8,12},{12,8},{16,20},{20,16},{24,28},{28,24},{32,36},... | collective-permute-start | bytes 1572872 | tf_op jit(solution)/shard_map/ppermute | solution.py:508
  42.5 2.3 %shard_map.114 = (bf16[256,512]{1,0:T(8,128)(2,1)S(1)}, f32[256,512]{1,0:T(8,128)S(1)}, f32[256,256]{1,0:T(8,128)S(1)}) custom-call(bf16[2,256,256]{2,1,0:T(8,128)(2,1)S(1)} %get-tuple-element.52.refs_3_.qt.refs_2_, bf16[2,256,256]{2,1,0:T(8,128)(2,1)S(1)} %get-tuple-element.53.gt.refs_3_, f32[16,512]{1,0:T(8,128)S(1)} %get-tuple-element.67.stat2.refs_4_, ...), custom_call_target="tpu_custom_call" | custom-call | flops 4000000000 | bytes 5000000 | tf_op jit(solution)/shard_map/pallas_call | solution.py:33
  44.9 3.0 %shard_map.115 = (f32[512,512]{1,0:T(8,128)S(1)}, bf16[256,512]{1,0:T(8,128)(2,1)S(1)}, bf16[256,256]{1,0:T(8,128)(2,1)S(1)}) custom-call(s32[4]{0:T(128)S(1)} %copy-done, s32[1]{0:T(128)} %bitcast.tm.refs_2_.refs_1_, bf16[2,256,256]{2,1,0:T(8,128)(2,1)S(1)} %get-tuple-element.52.refs_3_.qt.refs_2_, bf16[2,256,256]{2,1,0:T(8,128)(2,1)S(1)} %get-tuple-element.53.gt.refs_3_, ...), custom_call_target="tpu_custom_call" | custom-call | flops 4000000000 | bytes 4000000 | tf_op jit(solution)/shard_map/pallas_call | solution.py:33
  48.0 0.8 collective-permute-start.11
  48.8 0.1 shard_map.117
  48.9 3.7 %collective-permute-start.19 = (bf16[128,512]{1,0:T(8,128)(2,1)S(1)}, bf16[128,512]{1,0:T(8,128)(2,1)S(1)}, u32[]{:S(2)}, u32[]{:S(2)}) collective-permute-start(bf16[128,512]{1,0:T(8,128)(2,1)S(1)} %get-tuple-element.85), channel_id=1, source_target_pairs={{0,32},{4,36},{8,40},{12,44},{16,48},{20,52},{24,56},{28,60},{32,0... | collective-permute-start | bytes 393224 | tf_op jit(solution)/shard_map/ppermute | solution.py:508
  52.6 1.9 %collective-permute-start.20 = (bf16[64,512]{1,0:T(8,128)(2,1)S(1)}, bf16[64,512]{1,0:T(8,128)(2,1)S(1)}, u32[]{:S(2)}, u32[]{:S(2)}) collective-permute-start(bf16[64,512]{1,0:T(8,128)(2,1)S(1)} %get-tuple-element.86), channel_id=1, source_target_pairs={{0,64},{4,68},{8,72},{12,76},{16,80},{20,84},{24,88},{28,92},{32,9... | collective-permute-start | bytes 196616 | tf_op jit(solution)/shard_map/ppermute | solution.py:508
  54.5 0.6 collective-permute-start.21
  55.1 3.8 %shard_map.116 = (f32[512,512]{1,0:T(8,128)S(1)}, bf16[384,512]{1,0:T(8,128)(2,1)S(1)}, bf16[512,256]{1,0:T(8,128)(2,1)}) custom-call(s32[4]{0:T(128)S(1)} %copy-done, s32[1]{0:T(128)} %bitcast.tm.refs_2_.refs_1_, bf16[2,256,256]{2,1,0:T(8,128)(2,1)S(1)} %get-tuple-element.52.refs_3_.qt.refs_2_, bf16[2,256,256]{2,1,0:T(8,128)(2,1)S(1)} %get-tuple-element.53.gt.refs_3_, ...), custom_call_target="tpu_custom_call" | custom-call | flops 4000000000 | bytes 4000000 | tf_op jit(solution)/shard_map/pallas_call | solution.py:33
  58.8 2.6 %collective-permute-start.16 = (bf16[384,512]{1,0:T(8,128)(2,1)S(1)}, bf16[384,512]{1,0:T(8,128)(2,1)S(1)}, u32[]{:S(2)}, u32[]{:S(2)}) collective-permute-start(bf16[384,512]{1,0:T(8,128)(2,1)S(1)} %get-tuple-element.81), channel_id=1, source_target_pairs={{0,4},{4,0},{8,12},{12,8},{16,20},{20,16},{24,28},{28,24},{32,36},... | collective-permute-start | bytes 1179656 | tf_op jit(solution)/shard_map/ppermute | solution.py:508
  61.5 1.9 %collective-permute-start.17 = (bf16[256,512]{1,0:T(8,128)(2,1)S(1)}, bf16[256,512]{1,0:T(8,128)(2,1)S(1)}, u32[]{:S(2)}, u32[]{:S(2)}) collective-permute-start(bf16[256,512]{1,0:T(8,128)(2,1)S(1)} %get-tuple-element.82), channel_id=1, source_target_pairs={{4,8},{8,4},{12,16},{16,12},{20,24},{24,20},{28,32},{32,28},{36,40... | collective-permute-start | bytes 786440 | tf_op jit(solution)/shard_map/ppermute | solution.py:521
  63.4 0.1 collective-permute-start.15
  63.5 5.6 %collective-permute-done.17.hn = bf16[256,512]{1,0:T(8,128)(2,1)S(1)} collective-permute-done((bf16[256,512]{1,0:T(8,128)(2,1)S(1)}, bf16[256,512]{1,0:T(8,128)(2,1)S(1)}, u32[]{:S(2)}, u32[]{:S(2)}) %collective-permute-start.17) | collective-permute-done | bytes 262176 | tf_op jit(solution)/shard_map/ppermute | solution.py:521
  69.2 3.5 %collective-permute-start.23 = (bf16[64,512]{1,0:T(8,128)(2,1)S(1)}, bf16[64,512]{1,0:T(8,128)(2,1)S(1)}, u32[]{:S(2)}, u32[]{:S(2)}) collective-permute-start(bf16[64,512]{1,0:T(8,128)(2,1)S(1)} %get-tuple-element.90), channel_id=1, source_target_pairs={{0,16},{4,20},{8,24},{12,28},{16,0},{20,4},{24,8},{28,12},{32,48},... | collective-permute-start | bytes 196616 | tf_op jit(solution)/shard_map/ppermute | solution.py:508
  72.7 0.4 collective-permute-start.24
  73.0 0.1 shard_map.111.w
  73.2 0.2 shard_map.118.acc
  73.3 3.2 %collective-permute-done.23.x2a = bf16[64,512]{1,0:T(8,128)(2,1)S(1)} collective-permute-done((bf16[64,512]{1,0:T(8,128)(2,1)S(1)}, bf16[64,512]{1,0:T(8,128)(2,1)S(1)}, u32[]{:S(2)}, u32[]{:S(2)}) %collective-permute-start.23) | collective-permute-done | bytes 65568 | tf_op jit(solution)/shard_map/ppermute | solution.py:508
  76.5 0.9 %collective-permute-done.24.x2b = bf16[64,512]{1,0:T(8,128)(2,1)S(1)} collective-permute-done((bf16[64,512]{1,0:T(8,128)(2,1)S(1)}, bf16[64,512]{1,0:T(8,128)(2,1)S(1)}, u32[]{:S(2)}, u32[]{:S(2)}) %collective-permute-start.24) | collective-permute-done | bytes 65568 | tf_op jit(solution)/shard_map/ppermute | solution.py:508
  77.4 1.8 %shard_map.120 = (bf16[512,256]{1,0:T(8,128)(2,1)}, bf16[512,256]{1,0:T(8,128)(2,1)}) custom-call(s32[4]{0:T(128)S(1)} %copy-done, s32[1]{0:T(128)} %bitcast.tm.refs_2_.refs_1_, f32[512,512]{1,0:T(8,128)S(1)} %shard_map.118.acc, bf16[128,512]{1,0:T(8,128)(2,1)S(1)} %collective-permute-done.22.x1, bf16[64,512]{1,0:T(8,128)(2,1)S(1)} %collective-permute-done.23.x2a, ...), custom_call_target="tpu_custom_call" | custom-call | flops 300000000 | bytes 3000000 | tf_op jit(solution)/shard_map/pallas_call | solution.py:33
  79.2 2.3 %shard_map.112 = bf16[512,1024]{1,0:T(8,128)(2,1)} custom-call(s32[1]{0:T(128)} %bitcast.tm.refs_2_.refs_1_, bf16[512,512]{1,0:T(8,128)(2,1)S(1)} %shard_map.109.a01, bf16[512,512]{1,0:T(8,128)(2,1)S(1)} %collective-permute-done.11.a23, bf16[1024,1024]{1,0:T(8,128)(2,1)S(1)} %shard_map.111.w), custom_call_target="tpu_custom_call" | custom-call | flops 1000000000 | bytes 4000000 | tf_op jit(solution)/shard_map/pallas_call | solution.py:33
  (25 shorter events, 0.2 us)
Async XLA Ops:
  0.6 20.9 %copy-start = (s32[4]{0:T(128)S(1)}, s32[4]{0:T(128)}, u32[]{:S(2)}) copy-start(s32[4]{0:T(128)} %off.5) | copy-start | bytes 52
  2.5 23.2 %collective-permute-start = (bf16[384,512]{1,0:T(8,128)(2,1)S(1)}, bf16[384,512]{1,0:T(8,128)(2,1)S(1)}, u32[]{:S(2)}, u32[]{:S(2)}) collective-permute-start(bf16[384,512]{1,0:T(8,128)(2,1)S(1)} %get-tuple-element.55), channel_id=1, source_target_pairs={{0,4},{4,0},{8,12},{12,8},{16,20},{20,16},{24,28},{28,24},{32,36},... | collective-permute-start | bytes 1179656 | tf_op jit(solution)/shard_map/ppermute | solution.py:508
  3.9 9.9 %collective-permute-start.2 = (bf16[128,512]{1,0:T(8,128)(2,1)S(1)}, bf16[128,512]{1,0:T(8,128)(2,1)S(1)}, u32[]{:S(2)}, u32[]{:S(2)}) collective-permute-start(bf16[128,512]{1,0:T(8,128)(2,1)S(1)} %get-tuple-element.61), channel_id=1, source_target_pairs={{0,8},{4,12},{8,0},{12,4},{16,24},{20,28},{24,16},{28,20},{32,40},... | collective-permute-start | bytes 393224 | tf_op jit(solution)/shard_map/ppermute | solution.py:508
  5.2 7.4 %collective-permute-start.3 = (bf16[64,512]{1,0:T(8,128)(2,1)S(1)}, bf16[64,512]{1,0:T(8,128)(2,1)S(1)}, u32[]{:S(2)}, u32[]{:S(2)}) collective-permute-start(bf16[64,512]{1,0:T(8,128)(2,1)S(1)} %get-tuple-element.62), channel_id=1, source_target_pairs={{0,16},{4,20},{8,24},{12,28},{16,0},{20,4},{24,8},{28,12},{32,48},... | collective-permute-start | bytes 196616 | tf_op jit(solution)/shard_map/ppermute | solution.py:508
  7.7 6.1 %collective-permute-start.4 = (bf16[64,512]{1,0:T(8,128)(2,1)S(1)}, bf16[64,512]{1,0:T(8,128)(2,1)S(1)}, u32[]{:S(2)}, u32[]{:S(2)}) collective-permute-start(bf16[64,512]{1,0:T(8,128)(2,1)S(1)} %get-tuple-element.62), channel_id=1, source_target_pairs={{0,24},{4,28},{8,16},{12,20},{16,8},{20,12},{24,0},{28,4},{32,56},... | collective-permute-start | bytes 196616 | tf_op jit(solution)/shard_map/ppermute | solution.py:508
  13.8 11.8 %copy-start.1 = (s32[4]{0:T(128)S(1)}, s32[4]{0:T(128)}, u32[]{:S(2)}) copy-start(s32[4]{0:T(128)} %refs_1_.3) | copy-start | bytes 52
  13.8 11.0 %collective-permute-start.6 = (bf16[128,512]{1,0:T(8,128)(2,1)S(1)}, bf16[128,512]{1,0:T(8,128)(2,1)S(1)}, u32[]{:S(2)}, u32[]{:S(2)}) collective-permute-start(bf16[128,512]{1,0:T(8,128)(2,1)S(1)} %get-tuple-element.64), channel_id=1, source_target_pairs={{0,32},{4,36},{8,40},{12,44},{16,48},{20,52},{24,56},{28,60},{32,0... | collective-permute-start | bytes 393224 | tf_op jit(solution)/shard_map/ppermute | solution.py:508
  15.2 7.6 %collective-permute-start.7 = (bf16[64,512]{1,0:T(8,128)(2,1)S(1)}, bf16[64,512]{1,0:T(8,128)(2,1)S(1)}, u32[]{:S(2)}, u32[]{:S(2)}) collective-permute-start(bf16[64,512]{1,0:T(8,128)(2,1)S(1)} %get-tuple-element.65), channel_id=1, source_target_pairs={{0,64},{4,68},{8,72},{12,76},{16,80},{20,84},{24,88},{28,92},{32,9... | collective-permute-start | bytes 196616 | tf_op jit(solution)/shard_map/ppermute | solution.py:508
  17.8 6.9 %collective-permute-start.8 = (bf16[64,512]{1,0:T(8,128)(2,1)S(1)}, bf16[64,512]{1,0:T(8,128)(2,1)S(1)}, u32[]{:S(2)}, u32[]{:S(2)}) collective-permute-start(bf16[64,512]{1,0:T(8,128)(2,1)S(1)} %get-tuple-element.65), channel_id=1, source_target_pairs={{0,96},{4,100},{8,104},{12,108},{16,112},{20,116},{24,120},{28,124... | collective-permute-start | bytes 196616 | tf_op jit(solution)/shard_map/ppermute | solution.py:508
  17.8 23.5 %collective-permute-start.12 = (bf16[256,1024]{1,0:T(8,128)(2,1)S(1)}, bf16[256,1024]{1,0:T(8,128)(2,1)S(1)}, u32[]{:S(2)}, u32[]{:S(2)}) collective-permute-start(bf16[256,1024]{1,0:T(8,128)(2,1)S(1)} %get-tuple-element.51.w.own), channel_id=1, source_target_pairs={{0,1},{1,0},{2,3},{3,2},{4,7},{5,6},{6,5},{7,4},{8,9},{9,8},{10,11... | collective-permute-start | bytes 1572872 | tf_op jit(solution)/shard_map/ppermute | solution.py:516
  22.8 7.7 %collective-permute-start.1 = (bf16[256,512]{1,0:T(8,128)(2,1)S(1)}, bf16[256,512]{1,0:T(8,128)(2,1)S(1)}, u32[]{:S(2)}, u32[]{:S(2)}) collective-permute-start(bf16[256,512]{1,0:T(8,128)(2,1)S(1)} %get-tuple-element.57), channel_id=1, source_target_pairs={{4,8},{8,4},{12,16},{16,12},{20,24},{24,20},{28,32},{32,28},{36,40... | collective-permute-start | bytes 786440 | tf_op jit(solution)/shard_map/ppermute | solution.py:521
  24.7 8.8 %collective-permute-start.5 = (bf16[256,512]{1,0:T(8,128)(2,1)S(1)}, bf16[256,512]{1,0:T(8,128)(2,1)S(1)}, u32[]{:S(2)}, u32[]{:S(2)}) collective-permute-start(bf16[256,512]{1,0:T(8,128)(2,1)S(1)} %get-tuple-element.63.rest_0_), channel_id=1, source_target_pairs={{0,4},{4,0},{8,12},{12,8},{16,20},{20,16},{24,28},{28,24},{32,36},... | collective-permute-start | bytes 786440 | tf_op jit(solution)/shard_map/ppermute | solution.py:508
  24.9 8.7 %collective-permute-start.9 = (bf16[256,512]{1,0:T(8,128)(2,1)S(1)}, bf16[256,512]{1,0:T(8,128)(2,1)S(1)}, u32[]{:S(2)}, u32[]{:S(2)}) collective-permute-start(bf16[256,512]{1,0:T(8,128)(2,1)S(1)} %shard_map.107.rest_2_), channel_id=1, source_target_pairs={{0,4},{4,0},{8,12},{12,8},{16,20},{20,16},{24,28},{28,24},{32,36},... | collective-permute-start | bytes 786440 | tf_op jit(solution)/shard_map/ppermute | solution.py:508
  38.5 10.3 %collective-permute-start.18 = (bf16[512,512]{1,0:T(8,128)(2,1)S(1)}, bf16[512,512]{1,0:T(8,128)(2,1)S(1)}, u32[]{:S(2)}, u32[]{:S(2)}) collective-permute-start(bf16[512,512]{1,0:T(8,128)(2,1)S(1)} %get-tuple-element.84), channel_id=1, source_target_pairs={{0,4},{4,0},{8,12},{12,8},{16,20},{20,16},{24,28},{28,24},{32,36},... | collective-permute-start | bytes 1572872 | tf_op jit(solution)/shard_map/ppermute | solution.py:508
  38.6 9.3 %collective-permute-start.10 = (bf16[512,256]{1,0:T(8,128)(2,1)S(1)}, bf16[512,256]{1,0:T(8,128)(2,1)S(1)}, u32[]{:S(2)}, u32[]{:S(2)}) collective-permute-start(bf16[512,256]{1,0:T(8,128)(2,1)S(1)} %get-tuple-element.66.left), channel_id=1, source_target_pairs={{0,1},{1,0},{2,3},{3,2},{4,7},{5,6},{6,5},{7,4},{8,9},{9,8},{10,11... | collective-permute-start | bytes 786440 | tf_op jit(solution)/shard_map/ppermute | solution.py:516
  41.3 13.1 %collective-permute-start.14 = (bf16[128,1024]{1,0:T(8,128)(2,1)S(1)}, bf16[128,1024]{1,0:T(8,128)(2,1)S(1)}, u32[]{:S(2)}, u32[]{:S(2)}) collective-permute-start(bf16[128,1024]{1,0:T(8,128)(2,1)S(1)} %shard_map.110), channel_id=1, source_target_pairs={{0,3},{1,2},{2,1},{3,0},{4,5},{5,4},{6,7},{7,6},{8,11},{9,10},{10,... | collective-permute-start | bytes 786440 | tf_op jit(solution)/shard_map/ppermute | solution.py:516
  41.4 31.2 %collective-permute-start.13 = (bf16[256,1024]{1,0:T(8,128)(2,1)S(1)}, bf16[256,1024]{1,0:T(8,128)(2,1)S(1)}, u32[]{:S(2)}, u32[]{:S(2)}) collective-permute-start(bf16[256,1024]{1,0:T(8,128)(2,1)S(1)} %collective-permute-done.12.w.first), channel_id=1, source_target_pairs={{0,4},{4,0},{8,12},{12,8},{16,20},{20,16},{24,28},{28,24},{32,36},... | collective-permute-start | bytes 1572872 | tf_op jit(solution)/shard_map/ppermute | solution.py:508
  48.0 31.3 %collective-permute-start.11 = (bf16[512,512]{1,0:T(8,128)(2,1)S(1)}, bf16[512,512]{1,0:T(8,128)(2,1)S(1)}, u32[]{:S(2)}, u32[]{:S(2)}) collective-permute-start(bf16[512,512]{1,0:T(8,128)(2,1)S(1)} %shard_map.109.a01), channel_id=1, source_target_pairs={{0,3},{1,2},{2,1},{3,0},{4,5},{5,4},{6,7},{7,6},{8,11},{9,10},{10,... | collective-permute-start | bytes 1572872 | tf_op jit(solution)/shard_map/ppermute | solution.py:516
  48.9 14.5 %collective-permute-start.19 = (bf16[128,512]{1,0:T(8,128)(2,1)S(1)}, bf16[128,512]{1,0:T(8,128)(2,1)S(1)}, u32[]{:S(2)}, u32[]{:S(2)}) collective-permute-start(bf16[128,512]{1,0:T(8,128)(2,1)S(1)} %get-tuple-element.85), channel_id=1, source_target_pairs={{0,32},{4,36},{8,40},{12,44},{16,48},{20,52},{24,56},{28,60},{32,0... | collective-permute-start | bytes 393224 | tf_op jit(solution)/shard_map/ppermute | solution.py:508
  52.6 6.2 %collective-permute-start.20 = (bf16[64,512]{1,0:T(8,128)(2,1)S(1)}, bf16[64,512]{1,0:T(8,128)(2,1)S(1)}, u32[]{:S(2)}, u32[]{:S(2)}) collective-permute-start(bf16[64,512]{1,0:T(8,128)(2,1)S(1)} %get-tuple-element.86), channel_id=1, source_target_pairs={{0,64},{4,68},{8,72},{12,76},{16,80},{20,84},{24,88},{28,92},{32,9... | collective-permute-start | bytes 196616 | tf_op jit(solution)/shard_map/ppermute | solution.py:508
  54.5 7.0 %collective-permute-start.21 = (bf16[64,512]{1,0:T(8,128)(2,1)S(1)}, bf16[64,512]{1,0:T(8,128)(2,1)S(1)}, u32[]{:S(2)}, u32[]{:S(2)}) collective-permute-start(bf16[64,512]{1,0:T(8,128)(2,1)S(1)} %get-tuple-element.87), channel_id=1, source_target_pairs={{0,96},{4,100},{8,104},{12,108},{16,112},{20,116},{24,120},{28,124... | collective-permute-start | bytes 196616 | tf_op jit(solution)/shard_map/ppermute | solution.py:508
  58.8 14.3 %collective-permute-start.16 = (bf16[384,512]{1,0:T(8,128)(2,1)S(1)}, bf16[384,512]{1,0:T(8,128)(2,1)S(1)}, u32[]{:S(2)}, u32[]{:S(2)}) collective-permute-start(bf16[384,512]{1,0:T(8,128)(2,1)S(1)} %get-tuple-element.81), channel_id=1, source_target_pairs={{0,4},{4,0},{8,12},{12,8},{16,20},{20,16},{24,28},{28,24},{32,36},... | collective-permute-start | bytes 1179656 | tf_op jit(solution)/shard_map/ppermute | solution.py:508
  61.5 7.7 %collective-permute-start.17 = (bf16[256,512]{1,0:T(8,128)(2,1)S(1)}, bf16[256,512]{1,0:T(8,128)(2,1)S(1)}, u32[]{:S(2)}, u32[]{:S(2)}) collective-permute-start(bf16[256,512]{1,0:T(8,128)(2,1)S(1)} %get-tuple-element.82), channel_id=1, source_target_pairs={{4,8},{8,4},{12,16},{16,12},{20,24},{24,20},{28,32},{32,28},{36,40... | collective-permute-start | bytes 786440 | tf_op jit(solution)/shard_map/ppermute | solution.py:521
  63.4 5.8 %collective-permute-start.15 = (bf16[128,1024]{1,0:T(8,128)(2,1)S(1)}, bf16[128,1024]{1,0:T(8,128)(2,1)S(1)}, u32[]{:S(2)}, u32[]{:S(2)}) collective-permute-start(bf16[128,1024]{1,0:T(8,128)(2,1)S(1)} %collective-permute-done.14.mine), channel_id=1, source_target_pairs={{0,4},{4,0},{8,12},{12,8},{16,20},{20,16},{24,28},{28,24},{32,36},... | collective-permute-start | bytes 786440 | tf_op jit(solution)/shard_map/ppermute | solution.py:508
  69.1 8.2 %collective-permute-start.22 = (bf16[128,512]{1,0:T(8,128)(2,1)S(1)}, bf16[128,512]{1,0:T(8,128)(2,1)S(1)}, u32[]{:S(2)}, u32[]{:S(2)}) collective-permute-start(bf16[128,512]{1,0:T(8,128)(2,1)S(1)} %get-tuple-element.89), channel_id=1, source_target_pairs={{0,8},{4,12},{8,0},{12,4},{16,24},{20,28},{24,16},{28,20},{32,40},... | collective-permute-start | bytes 393224 | tf_op jit(solution)/shard_map/ppermute | solution.py:508
  69.2 7.3 %collective-permute-start.23 = (bf16[64,512]{1,0:T(8,128)(2,1)S(1)}, bf16[64,512]{1,0:T(8,128)(2,1)S(1)}, u32[]{:S(2)}, u32[]{:S(2)}) collective-permute-start(bf16[64,512]{1,0:T(8,128)(2,1)S(1)} %get-tuple-element.90), channel_id=1, source_target_pairs={{0,16},{4,20},{8,24},{12,28},{16,0},{20,4},{24,8},{28,12},{32,48},... | collective-permute-start | bytes 196616 | tf_op jit(solution)/shard_map/ppermute | solution.py:508
  72.7 4.7 %collective-permute-start.24 = (bf16[64,512]{1,0:T(8,128)(2,1)S(1)}, bf16[64,512]{1,0:T(8,128)(2,1)S(1)}, u32[]{:S(2)}, u32[]{:S(2)}) collective-permute-start(bf16[64,512]{1,0:T(8,128)(2,1)S(1)} %get-tuple-element.91), channel_id=1, source_target_pairs={{0,24},{4,28},{8,16},{12,20},{16,8},{20,12},{24,0},{28,4},{32,56},... | collective-permute-start | bytes 196616 | tf_op jit(solution)/shard_map/ppermute | solution.py:508
